TPU v7x, 512 devices: a whole 4x8x8 slice. The times are simulated.
512 devices in a mesh: member: 8 (over y_lo, core), slab: 64 (over y_hi, x, z).
Axes of the slice: x: 4, y: 8 (y_hi: 2, y_lo: 4; y = y_hi * 4 + y_lo), z: 8, core: 2. Of those that a mesh axis runs over, the one named last changes fastest.
Arguments:
- base_field: bfloat16 [32, 512, 2, 512], P(None, 'slab'), may hold values from -6 to 6
- forcing: bfloat16 [512, 2, 512], P('slab'), may hold values from -6 to 6
- load: float32 [32], replicated, may hold values from 0.25 to 1.75
- amplitudes: float32 [16], replicated, may hold values from 0.25 to 2
- amp_index: int32 [8], P('member'), may hold values from 0 to 15
- mode_count: int32 [8], P('member'), may hold values from 32 to 64, as said below
- point_weight: bfloat16 [32, 32], replicated, may hold values from -1 to 1
- point_bias: float32 [32], replicated, may hold values from -3 to 3
- spectral_weight: bfloat16 [64, 64, 2, 32, 32], P('slab'), may hold values from -6 to 6
Outputs:
- dependence: bfloat16 [32, 512, 2, 512], P('member', 'slab')
Inputs may be any that keep to these rules, and one draw needn't show every extreme that they name: `mode_count`: each member keeps the second-dimension modes below its count; some member keeps all 64.
All inputs are finite; a program needn't handle non-finite values.
Results may differ from a plain program's by a relative error of at most 0.015.
Values may be sent and summed in bfloat16 or wider, within the bound.
A program may use at most 64 MiB of HBM per device.

v0:
```python
import math

import jax
import jax.numpy as jnp
from jax import lax
from jax.sharding import PartitionSpec as P

TWO_PI = 2.0 * math.pi


def phases(frequency, positions, length):
    product = frequency[:, None] * positions[None, :] % length
    angles = product.astype(jnp.float32) * (TWO_PI / length)
    return (jnp.cos(angles), jnp.sin(angles))


def forward_x(pencil, cos_table, sin_table):
    row_total = pencil.shape[0]
    modes = cos_table.shape[0]
    with_cos = jnp.einsum(
        "kxf,mx->kmf", pencil, cos_table, preferred_element_type=jnp.float32
    ).reshape(row_total, modes, 2, -1)
    with_sin = jnp.einsum(
        "kxf,mx->kmf", pencil, sin_table, preferred_element_type=jnp.float32
    ).reshape(row_total, modes, 2, -1)
    real_part = with_cos[:, :, 0] + with_sin[:, :, 1]
    imag_part = with_cos[:, :, 1] - with_sin[:, :, 0]
    return jnp.stack([real_part, imag_part], axis=2).reshape(row_total, modes, -1)


def inverse_x(spectra, cos_table, sin_table):
    row_total = spectra.shape[0]
    points = cos_table.shape[1]
    with_cos = jnp.einsum(
        "kmf,mx->kxf", spectra, cos_table, preferred_element_type=jnp.float32
    ).reshape(row_total, points, 2, -1)
    with_sin = jnp.einsum(
        "kmf,mx->kxf", spectra, sin_table, preferred_element_type=jnp.float32
    ).reshape(row_total, points, 2, -1)
    real_part = with_cos[:, :, 0] - with_sin[:, :, 1]
    imag_part = with_cos[:, :, 1] + with_sin[:, :, 0]
    return jnp.stack([real_part, imag_part], axis=2).reshape(row_total, points, -1)


def mixing(weights, values):
    return jnp.einsum("kmoi,kmiz->kmoz", weights, values, preferred_element_type=jnp.float32)


def local(
    base_field,
    forcing,
    load,
    amplitudes,
    amp_index,
    mode_count,
    point_weight,
    point_bias,
    spectral_weight,
):
    channels, slab_rows, plane_count, length_y = base_field.shape
    slab_count = lax.axis_size("slab")
    local_modes = spectral_weight.shape[0]
    modes_y = local_modes * slab_count
    modes_x = spectral_weight.shape[1]
    length_x = slab_rows * slab_count
    packed_width = 2 * channels * plane_count
    slab_index = lax.axis_index("slab")
    level_ids = jnp.arange(amplitudes.shape[0], dtype=jnp.int32)
    amplitude = jnp.sum(jnp.where(level_ids == amp_index[0], amplitudes, 0.0))
    driven = base_field.astype(jnp.float32) + amplitude * load[:, None, None, None] * forcing[
        None
    ].astype(jnp.float32)
    field_now = (2.0 * jnp.tanh(0.5 * driven)).astype(jnp.bfloat16)
    y_cos, y_sin = phases(
        jnp.arange(modes_y, dtype=jnp.int32), jnp.arange(length_y, dtype=jnp.int32), length_y
    )
    y_real = jnp.einsum(
        "cxzy,ky->kxcz", field_now, y_cos.astype(jnp.bfloat16), preferred_element_type=jnp.float32
    )
    y_imag = -jnp.einsum(
        "cxzy,ky->kxcz", field_now, y_sin.astype(jnp.bfloat16), preferred_element_type=jnp.float32
    )
    packed = (
        jnp.stack([y_real, y_imag], axis=2)
        .astype(jnp.bfloat16)
        .reshape(modes_y, slab_rows, packed_width)
    )
    frequency_x = jnp.concatenate(
        [
            jnp.arange(modes_x // 2, dtype=jnp.int32),
            jnp.arange(length_x - modes_x // 2, length_x, dtype=jnp.int32),
        ]
    )
    local_points = slab_index * slab_rows + jnp.arange(slab_rows, dtype=jnp.int32)
    part_cos, part_sin = phases(frequency_x, local_points, length_x)
    part_cos = part_cos.astype(jnp.bfloat16)
    part_sin = part_sin.astype(jnp.bfloat16)
    full_cos, full_sin = phases(frequency_x, jnp.arange(length_x, dtype=jnp.int32), length_x)
    full_cos = full_cos.astype(jnp.bfloat16)
    full_sin = full_sin.astype(jnp.bfloat16)
    spectrum = lax.psum_scatter(
        forward_x(packed, part_cos, part_sin), "slab", scatter_dimension=0, tiled=True
    )
    spectrum = spectrum.astype(jnp.bfloat16).reshape(local_modes, modes_x, 2, channels, plane_count)
    weight_real = spectral_weight[:, :, 0]
    weight_imag = spectral_weight[:, :, 1]
    spec_real = spectrum[:, :, 0]
    spec_imag = spectrum[:, :, 1]
    mix_real = mixing(weight_real, spec_real) - mixing(weight_imag, spec_imag)
    mix_imag = mixing(weight_real, spec_imag) + mixing(weight_imag, spec_real)
    global_modes = slab_index * local_modes + jnp.arange(local_modes, dtype=jnp.int32)
    keep = (global_modes < mode_count[0]).astype(jnp.float32)[:, None, None, None, None]
    mixed = (
        (jnp.stack([mix_real, mix_imag], axis=2) * keep)
        .astype(jnp.bfloat16)
        .reshape(local_modes, modes_x, packed_width)
    )
    returned = inverse_x(
        lax.all_gather(mixed, "slab", axis=0, tiled=True), part_cos, part_sin
    ).astype(jnp.bfloat16)
    returned = returned.reshape(modes_y, slab_rows, 2, channels, plane_count)
    weights_y = jnp.where(jnp.arange(modes_y) == 0, 1.0, 2.0).astype(jnp.float32) / (
        length_x * length_y
    )
    back_cos = (weights_y[:, None] * y_cos).astype(jnp.bfloat16)
    back_sin = (weights_y[:, None] * y_sin).astype(jnp.bfloat16)
    spectral = jnp.einsum(
        "kxcz,ky->cxzy", returned[:, :, 0], back_cos, preferred_element_type=jnp.float32
    )
    spectral = spectral - jnp.einsum(
        "kxcz,ky->cxzy", returned[:, :, 1], back_sin, preferred_element_type=jnp.float32
    )
    pointwise = (
        jnp.einsum("oc,cxzy->oxzy", point_weight, field_now, preferred_element_type=jnp.float32)
        + point_bias[:, None, None, None]
    )
    layer = jax.nn.gelu(pointwise + spectral, approximate=True).astype(jnp.bfloat16)
    layer = lax.optimization_barrier(layer).astype(jnp.float32)
    total = lax.psum_scatter(
        layer.astype(jnp.bfloat16), "member", scatter_dimension=0, tiled=True
    ).astype(jnp.float32)
    return (total / lax.axis_size("member")).astype(jnp.bfloat16)


def solution(mesh):
    in_specs = (
        P(None, "slab", None, None),
        P("slab", None, None),
        P(),
        P(),
        P("member"),
        P("member"),
        P(),
        P(),
        P("slab", None, None, None, None),
    )
    out_specs = P("member", "slab", None, None)
    return jax.shard_map(local, mesh=mesh, in_specs=in_specs, out_specs=out_specs, check_vma=False)
```

profile of v0, /device:TPU:1, one launch (start us, length us, event | category | flops | bytes accessed | tf_op | source)
XLA Modules:
  0.0 676.3 jit_solution(10603344090468271848)
XLA Ops:
  7.9 1.3 fusion.62
  9.3 1.3 broadcast_multiply_fusion
  10.5 1.4 multiply_convert_fusion
  12.0 0.8 fusion.4
  12.8 0.8 fusion.5
  14.1 1.9 convolution_bitcast_fusion.1
  16.6 5.8 reshape.104
  22.4 3.7 reshape.105
  26.1 11.8 %slice_add_fusion = (f32[64,64,1,64]{3,2,1,0:T(1,128)S(1)}, f32[64,64,1,64]{3,2,1,0:T(1,128)S(1)}) fusion(f32[64,64,2,64]{3,2,1,0:T(2,128)} %reshape.105, f32[64,64,2,64]{3,2,1,0:T(2,128)} %reshape.104), kind=kLoop, calls=%fused_computation.2 | loop fusion | flops 524288 | bytes 6291456 | tf_op jit(solution)/shard_map/add | solution.py:26
  37.9 6.8 %pad_maximum_fusion = f32[64,64,2,64]{3,2,1,0:T(2,128)} fusion(f32[64,64,1,64]{3,2,1,0:T(1,128)S(1)} %get-tuple-element.6, f32[64,64,1,64]{3,2,1,0:T(1,128)S(1)} %get-tuple-element.5), kind=kLoop, calls=%fused_computation | loop fusion | flops 524288 | bytes 4194304 | tf_op jit(solution)/shard_map/stack | solution.py:28
  44.7 7.2 %copy.55 = f32[64,64,2,64]{1,3,2,0:T(8,128)} copy(f32[64,64,2,64]{3,2,1,0:T(2,128)} %pad_maximum_fusion) | data formatting | bytes 4194304 | tf_op jit(solution)/shard_map/stack | solution.py:28
  52.2 0.7 copy-done.3
  53.0 0.8 copy.84
  53.8 0.8 copy.82
  55.3 403.6 %reduce-scatter.3.cloned.1.call-done = f32[1,64,128]{1,2,0:T(8,128)} async-done(((f32[64,64,128]{1,2,0:T(8,128)}), f32[1,64,128]{1,2,0:T(8,128)}) %reduce-scatter.3.cloned.1.call-update) | async-done | bytes 32784 | tf_op jit(solution)/shard_map/reduce_scatter | solution.py:101
  458.9 0.8 convert_element_type.91
  462.7 1.3 fusion.2
  464.0 162.6 %all-gather.2.cloned.1.call-done = bf16[64,64,128]{2,1,0:T(8,128)(2,1)} async-done(((bf16[1,64,128]{2,1,0:T(8,128)(2,1)}), bf16[64,64,128]{2,1,0:T(8,128)(2,1)}) %all-gather.2.cloned.1.call-update) | async-done | bytes 1048592 | tf_op jit(solution)/shard_map/all_gather | solution.py:119
  626.6 1.7 convolution_bitcast_fusion.3
  629.3 0.8 fusion.27
  630.1 1.0 fusion.13
  631.2 1.1 copy.72
  632.3 35.9 %reduce-scatter.5.cloned.1.call-done = bf16[4,8,2,512]{3,1,2,0:T(8,128)(2,1)} async-done(((bf16[32,8,2,512]{3,1,2,0:T(8,128)(2,1)}), bf16[4,8,2,512]{3,1,2,0:T(8,128)(2,1)}) %reduce-scatter.5.cloned.1.call-update) | async-done | bytes 65552 | tf_op jit(solution)/shard_map/reduce_scatter | solution.py:139
  668.2 0.9 multiply_convert_fusion.1
  (48 shorter events, 6.9 us)
Async XLA Ops:
  6.5 456.1 %copy-start = (bf16[32,32]{1,0:T(8,128)(2,1)S(1)}, bf16[32,32]{1,0:T(8,128)(2,1)}, u32[]{:S(2)}) copy-start(bf16[32,32]{1,0:T(8,128)(2,1)} %param.15) | copy-start | bytes 6148
  6.5 452.3 %reduce-scatter.3.cloned.1.call-start = ((), (), s32[]{:S(2)}) async-start(), calls=%async_computation.2 | async-start | bytes 4259840 | tf_op jit(solution)/shard_map/reduce_scatter | solution.py:101
  52.0 1.0 copy-start.3
  52.0 574.6 %all-gather.2.cloned.1.call-start = ((), (), s32[]{:S(2)}) async-start(), calls=%async_computation.3 | async-start | bytes 1064960 | tf_op jit(solution)/shard_map/all_gather | solution.py:119
  53.8 408.9 %copy-start.4 = (f32[32]{0:T(128)S(1)}, f32[32]{0:T(128)}, u32[]{:S(2)}) copy-start(f32[32]{0:T(128)} %param.16) | copy-start | bytes 388
  462.6 205.6 %reduce-scatter.5.cloned.1.call-start = ((), (), s32[]{:S(2)}) async-start(), calls=%async_computation.4 | async-start | bytes 589824 | tf_op jit(solution)/shard_map/reduce_scatter | solution.py:139
  626.6 1.9 copy-start.1
  628.9 1.2 copy-start.2
Sparse Core Ops, SparseCore 0:
  52.1 406.7 reduce-scatter.2
  464.0 162.5 all-gather.1
  632.4 35.7 reduce-scatter.4
where the time goes:
time: 678 us; the launch traced here: 676 us
  waiting for transfers between devices  602 us (89%)
  other arithmetic  25.4 us (4%)
  local copies, waits for them, and re-layouts  23.1 us (3%)
  between operations  14.6 us (2%)
  matrix products  10.6 us (2%)
    reduce_scatter x1, waiting for transfers between devices, local(): lax.psum_scatter(forward_x(packed, part_cos, part_sin), 'slab', scatter_d...  404 us
    all_gather x1, waiting for transfers between devices, local(): lax.all_gather(mixed, 'slab', axis=0, tiled=True)  163 us
    reduce_scatter x1, waiting for transfers between devices, local(): lax.psum_scatter(layer.astype(jnp.bfloat16), 'member', scatter_dimension=...  35.9 us
  transfers between devices with their start and end apart: 3, of which 3 were waited for; matrix products, arithmetic and copies ran while one was open for 0% of the time, Pallas kernels for 0%

commit v1 on v0

--- a/solution.py
+++ b/solution.py
@@ -91,16 +91,11 @@
             jnp.arange(length_x - modes_x // 2, length_x, dtype=jnp.int32),
         ]
     )
-    local_points = slab_index * slab_rows + jnp.arange(slab_rows, dtype=jnp.int32)
-    part_cos, part_sin = phases(frequency_x, local_points, length_x)
-    part_cos = part_cos.astype(jnp.bfloat16)
-    part_sin = part_sin.astype(jnp.bfloat16)
     full_cos, full_sin = phases(frequency_x, jnp.arange(length_x, dtype=jnp.int32), length_x)
     full_cos = full_cos.astype(jnp.bfloat16)
     full_sin = full_sin.astype(jnp.bfloat16)
-    spectrum = lax.psum_scatter(
-        forward_x(packed, part_cos, part_sin), "slab", scatter_dimension=0, tiled=True
-    )
+    gathered = lax.all_to_all(packed, "slab", 0, 1, tiled=True)
+    spectrum = forward_x(gathered, full_cos, full_sin)
     spectrum = spectrum.astype(jnp.bfloat16).reshape(local_modes, modes_x, 2, channels, plane_count)
     weight_real = spectral_weight[:, :, 0]
     weight_imag = spectral_weight[:, :, 1]
@@ -115,9 +110,8 @@
         .astype(jnp.bfloat16)
         .reshape(local_modes, modes_x, packed_width)
     )
-    returned = inverse_x(
-        lax.all_gather(mixed, "slab", axis=0, tiled=True), part_cos, part_sin
-    ).astype(jnp.bfloat16)
+    returned = inverse_x(mixed, full_cos, full_sin).astype(jnp.bfloat16)
+    returned = lax.all_to_all(returned, "slab", 1, 0, tiled=True)
     returned = returned.reshape(modes_y, slab_rows, 2, channels, plane_count)
     weights_y = jnp.where(jnp.arange(modes_y) == 0, 1.0, 2.0).astype(jnp.float32) / (
         length_x * length_y

time: 678 us -> 123 us (0.18)
  waiting for transfers between devices: 602 us -> 52.4 us
  starting transfers between devices: 0.31 us -> 25.1 us
  other arithmetic: 25.4 us -> 7.42 us
  local copies, waits for them, and re-layouts: 23.1 us -> 12.7 us
    reduce_scatter x1 -> x0, waiting for transfers between devices: 404 us -> none  [local(): lax.psum_scatter(forward_x(packed, part_cos, part_sin), 'slab', scatter_d...]
    all_gather x1 -> x0, waiting for transfers between devices: 163 us -> none  [local(): lax.all_gather(mixed, 'slab', axis=0, tiled=True)]
    all_to_all x0 -> x2, starting transfers between devices: none -> 24.9 us  [the longest x1 19.6 us: local(): gathered = lax.all_to_all(packed, 'slab', 0, 1, tiled=True)]
    all_to_all x0 -> x2, waiting for transfers between devices: none -> 23.3 us  [the longest x1 12 us: local(): returned = lax.all_to_all(returned, 'slab', 1, 0, tiled=True)]
    add x2 -> x0, other arithmetic: 11.8 us -> none  [the longest x1 11.8 us: forward_x(): real_part = with_cos[:, :, 0] + with_sin[:, :, 1]]
    reshape x4 -> x1, local copies, waits for them, and re-layouts: 10.1 us -> 2.48 us  [local(): returned = returned.reshape(modes_y, slab_rows, 2, channels, plane_count)]
    another operation x1, local copies, waits for them, and re-layouts: 7.21 us -> 0.1 us  [forward_x(): jnp.stack([real_part, imag_part], axis=2).reshape(row_total, modes, -1)]
    reduce_scatter x1, waiting for transfers between devices: 35.9 us -> 29.1 us  [local(): lax.psum_scatter(layer.astype(jnp.bfloat16), 'member', scatter_dimension=...]
  transfers between devices with their start and end apart: 3 -> 3, of which waited for: 3 -> 3; matrix products, arithmetic and copies ran while one was open for 0% -> 2% of each run, Pallas kernels for 0% -> 0%
where the time goes in v1:
time: 123 us; the launch traced here: 121 us
  waiting for transfers between devices  52.4 us (43%)
  starting transfers between devices  25.1 us (20%)
  between operations  15 us (12%)
  local copies, waits for them, and re-layouts  12.7 us (10%)
  matrix products  8.77 us (7%)
  other arithmetic  7.42 us (6%)
    reduce_scatter x1, waiting for transfers between devices, local(): lax.psum_scatter(layer.astype(jnp.bfloat16), 'member', scatter_dimension=...  29.1 us
    all_to_all x1, starting transfers between devices, local(): gathered = lax.all_to_all(packed, 'slab', 0, 1, tiled=True)  19.6 us
    all_to_all x1, waiting for transfers between devices, local(): returned = lax.all_to_all(returned, 'slab', 1, 0, tiled=True)  12 us
    all_to_all x1, waiting for transfers between devices, local(): gathered = lax.all_to_all(packed, 'slab', 0, 1, tiled=True)  11.2 us
    all_to_all x1, starting transfers between devices, local(): returned = lax.all_to_all(returned, 'slab', 1, 0, tiled=True)  5.3 us
    unnamed x17, local copies, waits for them, and re-layouts  5.23 us
    reshape x1, local copies, waits for them, and re-layouts, local(): returned = returned.reshape(modes_y, slab_rows, 2, channels, plane_count)  2.48 us
  transfers between devices with their start and end apart: 3, of which 3 were waited for; matrix products, arithmetic and copies ran while one was open for 2% of the time, Pallas kernels for 0%

profile of v1, /device:TPU:1, one launch (start us, length us, event | category | flops | bytes accessed | tf_op | source)
XLA Modules:
  0.0 121.4 jit_solution(495491254852529494)
XLA Ops:
  6.5 0.7 convert_element_type.156
  7.9 1.3 %fusion.81 = f32[]{:T(128)} fusion(f32[16]{0:T(128)} %param.12, s32[]{:T(128)} %bitcast.127), kind=kLoop, calls=%fused_computation.105 | loop fusion | flops 47 | bytes 72 | tf_op jit(solution)/shard_map/reduce_sum | solution.py:69
  9.3 1.3 %broadcast_multiply_fusion = f32[32]{0:T(128)S(1)} fusion(f32[32]{0:T(128)} %param.11, f32[]{:T(128)} %fusion.81), kind=kLoop, calls=%fused_computation.109 | loop fusion | flops 32 | bytes 260 | tf_op jit(solution)/shard_map/mul | solution.py:70
  10.6 1.4 %multiply_convert_fusion = bf16[32,8,2,512]{3,0,2,1:T(8,128)(2,1)S(1)} fusion(bf16[32,8,2,512]{3,2,1,0:T(2,128)(2,1)} %param.9, f32[8,2,512]{2,1,0:T(2,128)S(1)} %convert_element_type.156, f32[32]{0:T(128)S(1)} %broadcast_multiply_fusion), kind=kLoop, calls=%fused_computation.23 | loop fusion | flops 1572864 | bytes 1081472 | tf_op jit(solution)/shard_map/convert_element_type | solution.py:73
  12.1 0.8 fusion.4
  12.8 0.8 fusion.5
  13.8 0.9 copy.47
  14.7 19.6 %all-to-all-start = ((bf16[64,8,128]{2,1,0:T(8,128)(2,1)}), bf16[64,8,128]{2,1,0:T(8,128)(2,1)S(1)}, u32[]{:S(2)}, u32[]{:S(2)}) async-start(bf16[64,8,128]{2,1,0:T(8,128)(2,1)} %copy.47), calls=%async_computation | async-start | bytes 262144 | tf_op jit(solution)/shard_map/all_to_all | solution.py:97
  34.4 0.8 copy.73
  35.2 0.8 copy.71
  36.7 11.2 %all-to-all-done = bf16[64,8,128]{2,1,0:T(8,128)(2,1)S(1)} async-done(((bf16[64,8,128]{2,1,0:T(8,128)(2,1)}), bf16[64,8,128]{2,1,0:T(8,128)(2,1)S(1)}, u32[]{:S(2)}, u32[]{:S(2)}) %all-to-all-start) | async-done | bytes 131104 | tf_op jit(solution)/shard_map/all_to_all | solution.py:97
  53.9 1.4 %reduce = bf16[512,128]{1,0:T(8,128)(2,1)S(1)} reduce(bf16[512,1,128]{2,1,0:T(2,128)(2,1)S(1)} %bitcast.128, bf16[]{:T(256)} %broadcast.304), dimensions={1}, to_apply=%bitcast.118.reduce_sub_computation | reduce | bytes 262146
  55.3 0.7 reshape.302
  56.0 5.3 %all-to-all-start.1 = ((bf16[64,2,512]{2,1,0:T(2,128)(2,1)}), bf16[64,2,512]{2,1,0:T(2,128)(2,1)S(1)}, u32[]{:S(2)}, u32[]{:S(2)}) async-start(bf16[64,2,512]{2,1,0:T(2,128)(2,1)} %reshape.302), calls=%async_computation.1 | async-start | bytes 262144 | tf_op jit(solution)/shard_map/all_to_all | solution.py:114
  61.6 1.2 %fusion.2 = f32[32,8,2,512]{3,0,2,1:T(8,128)} fusion(bf16[32,8,2,512]{3,0,2,1:T(8,128)(2,1)S(1)} %multiply_convert_fusion, f32[32]{0:T(128)S(1)} %copy-done.3, bf16[32,32]{1,0:T(8,128)(2,1)S(1)} %copy-done), kind=kOutput, calls=%fused_computation.5 | convolution fusion | flops 17039360 | bytes 1575040 | tf_op jit(solution)/shard_map/oc,cxzy->oxzy/dot_general | solution.py:128
  62.8 12.0 %all-to-all-done.1 = bf16[64,2,512]{2,1,0:T(2,128)(2,1)S(1)} async-done(((bf16[64,2,512]{2,1,0:T(2,128)(2,1)}), bf16[64,2,512]{2,1,0:T(2,128)(2,1)S(1)}, u32[]{:S(2)}, u32[]{:S(2)}) %all-to-all-start.1) | async-done | bytes 131104 | tf_op jit(solution)/shard_map/all_to_all | solution.py:114
  75.1 2.5 %reshape.291 = bf16[64,8,2,32,2]{1,0,4,3,2:T(8,128)(2,1)S(1)} reshape(bf16[1,512,128]{1,2,0:T(8,128)(2,1)S(1)} %copy.60) | data formatting | bytes 262144 | tf_op jit(solution)/shard_map/reshape | solution.py:115
  77.6 1.3 %fusion.115 = (bf16[64,8,1,32,2]{1,0,4,3,2:T(8,128)(2,1)S(1)}, bf16[64,8,1,32,2]{1,0,4,3,2:T(8,128)(2,1)}) fusion(bf16[64,8,2,32,2]{1,0,4,3,2:T(8,128)(2,1)S(1)} %reshape.291), kind=kLoop, calls=%fused_computation.142 | loop fusion | bytes 262144 | tf_op jit(solution)/shard_map/slice | solution.py:125
  78.9 1.7 %copy.74 = bf16[64,8,1,32,2]{0,3,4,1,2:T(8,128)(2,1)S(1)} copy(bf16[64,8,1,32,2]{1,0,4,3,2:T(8,128)(2,1)} %get-tuple-element.6) | data formatting | bytes 131072
  81.0 0.8 fusion.34
  81.8 1.0 fusion.13
  82.8 1.1 copy.63
  83.9 29.1 %reduce-scatter.2.cloned.1.call-done = bf16[4,8,2,512]{3,1,2,0:T(8,128)(2,1)} async-done(((bf16[32,8,2,512]{3,1,2,0:T(8,128)(2,1)}), bf16[4,8,2,512]{3,1,2,0:T(8,128)(2,1)}) %reduce-scatter.2.cloned.1.call-update) | async-done | bytes 65552 | tf_op jit(solution)/shard_map/reduce_scatter | solution.py:133
  113.0 0.9 multiply_convert_fusion.1
  (47 shorter events, 7.8 us)
Async XLA Ops:
  6.5 55.1 %copy-start = (bf16[32,32]{1,0:T(8,128)(2,1)S(1)}, bf16[32,32]{1,0:T(8,128)(2,1)}, u32[]{:S(2)}) copy-start(bf16[32,32]{1,0:T(8,128)(2,1)} %param.15) | copy-start | bytes 6148
  12.1 22.2 %copy-start.2 = (bf16[1,64,2,32,32]{1,4,3,2,0:T(8,128)(2,1)S(1)}, bf16[1,64,2,32,32]{1,4,3,2,0:T(8,128)(2,1)}, u32[]{:S(2)}) copy-start(bf16[1,64,2,32,32]{1,4,3,2,0:T(8,128)(2,1)} %param.17) | copy-start | bytes 786436
  14.7 33.2 %all-to-all-start = ((bf16[64,8,128]{2,1,0:T(8,128)(2,1)}), bf16[64,8,128]{2,1,0:T(8,128)(2,1)S(1)}, u32[]{:S(2)}, u32[]{:S(2)}) async-start(bf16[64,8,128]{2,1,0:T(8,128)(2,1)} %copy.47), calls=%async_computation | async-start | bytes 262144 | tf_op jit(solution)/shard_map/all_to_all | solution.py:97
  51.3 10.3 %copy-start.3 = (f32[32]{0:T(128)S(1)}, f32[32]{0:T(128)}, u32[]{:S(2)}) copy-start(f32[32]{0:T(128)} %param.16) | copy-start | bytes 388
  56.0 18.8 %all-to-all-start.1 = ((bf16[64,2,512]{2,1,0:T(2,128)(2,1)}), bf16[64,2,512]{2,1,0:T(2,128)(2,1)S(1)}, u32[]{:S(2)}, u32[]{:S(2)}) async-start(bf16[64,2,512]{2,1,0:T(2,128)(2,1)} %reshape.302), calls=%async_computation.1 | async-start | bytes 262144 | tf_op jit(solution)/shard_map/all_to_all | solution.py:114
  61.4 51.7 %reduce-scatter.2.cloned.1.call-start = ((), (), s32[]{:S(2)}) async-start(), calls=%async_computation.3 | async-start | bytes 589824 | tf_op jit(solution)/shard_map/reduce_scatter | solution.py:133
  78.9 2.9 %copy-start.1 = (f32[32,8,2,512]{3,0,2,1:T(8,128)S(1)}, f32[32,8,2,512]{3,0,2,1:T(8,128)}, u32[]{:S(2)}) copy-start(f32[32,8,2,512]{3,0,2,1:T(8,128)} %fusion.2) | copy-start | bytes 3145732
Sparse Core Ops, SparseCore 0:
  84.1 28.9 reduce-scatter.1

commit v2 on v1

--- a/solution.py
+++ b/solution.py
@@ -1,8 +1,11 @@
+import functools
 import math
 
 import jax
 import jax.numpy as jnp
 from jax import lax
+from jax.experimental import pallas as pl
+from jax.experimental.pallas import tpu as pltpu
 from jax.sharding import PartitionSpec as P
 
 TWO_PI = 2.0 * math.pi
@@ -44,6 +47,61 @@
 
 def mixing(weights, values):
     return jnp.einsum("kmoi,kmiz->kmoz", weights, values, preferred_element_type=jnp.float32)
+
+
+def member_sum_kernel(members, layer_ref, out_ref, landed, send_sems, recv_sems):
+    me = lax.axis_index("member")
+    slab = lax.axis_index("slab")
+    barrier = pltpu.get_barrier_semaphore()
+    for step in range(1, members):
+        peer = lax.rem(me + step, members)
+        pl.semaphore_signal(barrier, inc=1, device_id=(peer, slab), device_id_type=pl.DeviceIdType.MESH)
+    pl.semaphore_wait(barrier, members - 1)
+    copies = []
+    for step in range(1, members):
+        peer = lax.rem(me + step, members)
+        copy = pltpu.make_async_remote_copy(
+            src_ref=layer_ref.at[peer],
+            dst_ref=landed.at[me],
+            send_sem=send_sems.at[peer],
+            recv_sem=recv_sems.at[me],
+            device_id=(peer, slab),
+            device_id_type=pl.DeviceIdType.MESH,
+        )
+        copy.start()
+        copies.append(copy)
+    total = layer_ref[me].astype(jnp.float32)
+    for step in range(1, members):
+        source = lax.rem(me + members - step, members)
+        arrival = pltpu.make_async_remote_copy(
+            src_ref=layer_ref.at[source],
+            dst_ref=landed.at[source],
+            send_sem=send_sems.at[source],
+            recv_sem=recv_sems.at[source],
+            device_id=(source, slab),
+            device_id_type=pl.DeviceIdType.MESH,
+        )
+        arrival.wait_recv()
+        total = total + landed[source].astype(jnp.float32)
+    for copy in copies:
+        copy.wait_send()
+    out_ref[...] = (total / members).astype(out_ref.dtype)
+
+
+def member_sum(layer, members):
+    block_rows, width = layer.shape[1], layer.shape[2]
+    return pl.pallas_call(
+        functools.partial(member_sum_kernel, members),
+        out_shape=jax.ShapeDtypeStruct((block_rows, width), jnp.bfloat16),
+        in_specs=[pl.BlockSpec(memory_space=pltpu.VMEM)],
+        out_specs=pl.BlockSpec(memory_space=pltpu.VMEM),
+        scratch_shapes=[
+            pltpu.VMEM((members, block_rows, width), jnp.bfloat16),
+            pltpu.SemaphoreType.DMA((members,)),
+            pltpu.SemaphoreType.DMA((members,)),
+        ],
+        compiler_params=pltpu.CompilerParams(collective_id=0, has_side_effects=True),
+    )(layer)
 
 
 def local(
@@ -129,11 +187,10 @@
         + point_bias[:, None, None, None]
     )
     layer = jax.nn.gelu(pointwise + spectral, approximate=True).astype(jnp.bfloat16)
-    layer = lax.optimization_barrier(layer).astype(jnp.float32)
-    total = lax.psum_scatter(
-        layer.astype(jnp.bfloat16), "member", scatter_dimension=0, tiled=True
-    ).astype(jnp.float32)
-    return (total / lax.axis_size("member")).astype(jnp.bfloat16)
+    members = lax.axis_size("member")
+    blocks = layer.reshape(members, -1, length_y)
+    total = member_sum(blocks, members)
+    return total.reshape(channels // members, slab_rows, plane_count, length_y)
 
 
 def solution(mesh):

time: 123 us -> 97.6 us (0.79)
  waiting for transfers between devices: 52.4 us -> 23.3 us
  Pallas kernels: 0 us -> 17.3 us
  between operations: 15 us -> 1.61 us
  local copies, waits for them, and re-layouts: 12.7 us -> 14 us
    reduce_scatter x1 -> x0, waiting for transfers between devices: 29.1 us -> none  [local(): lax.psum_scatter(layer.astype(jnp.bfloat16), 'member', scatter_dimension=...]
    pallas_call x0 -> x1, Pallas kernels: none -> 17.3 us  [member_sum(): pl.pallas_call(functools.partial(member_sum_kernel, members), out_shape=j...]
    reshape x0 -> x2, local copies, waits for them, and re-layouts: none -> 2.5 us  [the longest x1 1.5 us: local(): return total.reshape(channels // members, slab_rows, plane_count, length_y)]
  transfers between devices with their start and end apart: 3 -> 2, of which waited for: 3 -> 2; matrix products, arithmetic and copies ran while one was open for 2% -> 3% of each run, Pallas kernels for 0% -> 0%
where the time goes in v2:
time: 97.6 us; the launch traced here: 96.6 us
  starting transfers between devices  25.1 us (26%)
  waiting for transfers between devices  23.3 us (24%)
  Pallas kernels  17.3 us (18%)
  local copies, waits for them, and re-layouts  14 us (14%)
  matrix products  8.77 us (9%)
  other arithmetic  6.57 us (7%)
  between operations  1.61 us (2%)
    all_to_all x1, starting transfers between devices, local(): gathered = lax.all_to_all(packed, 'slab', 0, 1, tiled=True)  19.6 us
    pallas_call x1, Pallas kernels, member_sum(): pl.pallas_call(functools.partial(member_sum_kernel, members), out_shape=j...  17.3 us
    all_to_all x1, waiting for transfers between devices, local(): returned = lax.all_to_all(returned, 'slab', 1, 0, tiled=True)  12.1 us
    all_to_all x1, waiting for transfers between devices, local(): gathered = lax.all_to_all(packed, 'slab', 0, 1, tiled=True)  11.2 us
    all_to_all x1, starting transfers between devices, local(): returned = lax.all_to_all(returned, 'slab', 1, 0, tiled=True)  5.49 us
    unnamed x17, local copies, waits for them, and re-layouts  5.23 us
    reshape x1, local copies, waits for them, and re-layouts, local(): returned = returned.reshape(modes_y, slab_rows, 2, channels, plane_count)  2.48 us
  transfers between devices with their start and end apart: 2, of which 2 were waited for; matrix products, arithmetic and copies ran while one was open for 3% of the time, Pallas kernels for 0%

profile of v2, /device:TPU:1, one launch (start us, length us, event | category | flops | bytes accessed | tf_op | source)
XLA Modules:
  0.0 96.6 jit_solution(4174258837847146055)
XLA Ops:
  0.0 0.7 convert_element_type.148
  1.4 1.3 %fusion.81 = f32[]{:T(128)} fusion(f32[16]{0:T(128)} %param.12, s32[]{:T(128)} %bitcast.127), kind=kLoop, calls=%fused_computation.104 | loop fusion | flops 47 | bytes 72 | tf_op jit(solution)/shard_map/reduce_sum | solution.py:127
  2.7 1.3 %broadcast_multiply_fusion = f32[32]{0:T(128)S(1)} fusion(f32[32]{0:T(128)} %param.11, f32[]{:T(128)} %fusion.81), kind=kLoop, calls=%fused_computation.108 | loop fusion | flops 32 | bytes 260 | tf_op jit(solution)/shard_map/mul | solution.py:128
  4.1 1.4 %multiply_convert_fusion = bf16[32,8,2,512]{3,0,2,1:T(8,128)(2,1)S(1)} fusion(bf16[32,8,2,512]{3,2,1,0:T(2,128)(2,1)} %param.9, f32[8,2,512]{2,1,0:T(2,128)S(1)} %convert_element_type.148, f32[32]{0:T(128)S(1)} %broadcast_multiply_fusion), kind=kLoop, calls=%fused_computation.23 | loop fusion | flops 1572864 | bytes 1081472 | tf_op jit(solution)/shard_map/convert_element_type | solution.py:131
  5.5 0.8 fusion.4
  6.3 0.8 fusion.5
  7.3 0.9 copy.46
  8.2 19.6 %all-to-all-start = ((bf16[64,8,128]{2,1,0:T(8,128)(2,1)}), bf16[64,8,128]{2,1,0:T(8,128)(2,1)S(1)}, u32[]{:S(2)}, u32[]{:S(2)}) async-start(bf16[64,8,128]{2,1,0:T(8,128)(2,1)} %copy.46), calls=%async_computation | async-start | bytes 262144 | tf_op jit(solution)/shard_map/all_to_all | solution.py:155
  27.8 0.8 copy.71
  28.6 0.8 copy.69
  30.2 11.2 %all-to-all-done = bf16[64,8,128]{2,1,0:T(8,128)(2,1)S(1)} async-done(((bf16[64,8,128]{2,1,0:T(8,128)(2,1)}), bf16[64,8,128]{2,1,0:T(8,128)(2,1)S(1)}, u32[]{:S(2)}, u32[]{:S(2)}) %all-to-all-start) | async-done | bytes 131104 | tf_op jit(solution)/shard_map/all_to_all | solution.py:155
  47.4 1.4 %reduce = bf16[512,128]{1,0:T(8,128)(2,1)S(1)} reduce(bf16[512,1,128]{2,1,0:T(2,128)(2,1)S(1)} %bitcast.128, bf16[]{:T(256)} %broadcast.303), dimensions={1}, to_apply=%bitcast.118.reduce_sub_computation | reduce | bytes 262146
  48.8 0.7 reshape.310
  49.5 5.5 %all-to-all-start.1 = ((bf16[64,2,512]{2,1,0:T(2,128)(2,1)}), bf16[64,2,512]{2,1,0:T(2,128)(2,1)S(1)}, u32[]{:S(2)}, u32[]{:S(2)}) async-start(bf16[64,2,512]{2,1,0:T(2,128)(2,1)} %reshape.310), calls=%async_computation.1 | async-start | bytes 262144 | tf_op jit(solution)/shard_map/all_to_all | solution.py:172
  55.0 1.2 %fusion.2 = f32[32,8,2,512]{3,0,2,1:T(8,128)} fusion(bf16[32,8,2,512]{3,0,2,1:T(8,128)(2,1)S(1)} %multiply_convert_fusion, f32[32]{0:T(128)S(1)} %copy-done.3, bf16[32,32]{1,0:T(8,128)(2,1)S(1)} %copy-done), kind=kOutput, calls=%fused_computation.5 | convolution fusion | flops 17039360 | bytes 1575040 | tf_op jit(solution)/shard_map/oc,cxzy->oxzy/dot_general | solution.py:186
  56.3 12.1 %all-to-all-done.1 = bf16[64,2,512]{2,1,0:T(2,128)(2,1)S(1)} async-done(((bf16[64,2,512]{2,1,0:T(2,128)(2,1)}), bf16[64,2,512]{2,1,0:T(2,128)(2,1)S(1)}, u32[]{:S(2)}, u32[]{:S(2)}) %all-to-all-start.1) | async-done | bytes 131104 | tf_op jit(solution)/shard_map/all_to_all | solution.py:172
  68.6 2.5 %reshape.297 = bf16[64,8,2,32,2]{1,0,4,3,2:T(8,128)(2,1)S(1)} reshape(bf16[1,512,128]{1,2,0:T(8,128)(2,1)S(1)} %copy.59) | data formatting | bytes 262144 | tf_op jit(solution)/shard_map/reshape | solution.py:173
  71.1 1.3 %fusion.115 = (bf16[64,8,1,32,2]{1,0,4,3,2:T(8,128)(2,1)S(1)}, bf16[64,8,1,32,2]{1,0,4,3,2:T(8,128)(2,1)}) fusion(bf16[64,8,2,32,2]{1,0,4,3,2:T(8,128)(2,1)S(1)} %reshape.297), kind=kLoop, calls=%fused_computation.141 | loop fusion | bytes 262144 | tf_op jit(solution)/shard_map/slice | solution.py:183
  72.4 1.7 %copy.72 = bf16[64,8,1,32,2]{0,3,4,1,2:T(8,128)(2,1)S(1)} copy(bf16[64,8,1,32,2]{1,0,4,3,2:T(8,128)(2,1)} %get-tuple-element.6) | data formatting | bytes 131072
  74.5 0.8 fusion.34
  75.3 1.0 %fusion.13 = bf16[32,8,2,512]{3,0,2,1:T(8,128)(2,1)S(1)} fusion(f32[32,8,2,512]{3,0,2,1:T(8,128)S(1)} %copy-done.1, f32[512,8,32,2]{0,2,3,1:T(8,128)S(1)} %fusion.34, bf16[64,8,1,32,2]{0,3,4,1,2:T(8,128)(2,1)S(1)} %copy.73, f32[64]{0:T(128)S(1)} %fusion.82), kind=kOutput, calls=%fused_computation.22 | convolution fusion | flops 36962304 | bytes 2687232 | tf_op jit(solution)/shard_map/kxcz,ky->cxzy/dot_general | solution.py:182
  76.8 1.0 %reshape.298.layer_ref = bf16[8,64,512]{2,1,0:T(8,128)(2,1)} reshape(bf16[32,8,2,512]{3,2,1,0:T(2,128)(2,1)S(1)} %copy.62) | data formatting | bytes 1048576 | tf_op jit(solution)/shard_map/reshape | solution.py:191
  77.8 17.3 %shard_map.91 = bf16[64,512]{1,0:T(8,128)(2,1)} custom-call(bf16[8,64,512]{2,1,0:T(8,128)(2,1)} %reshape.298.layer_ref), custom_call_target="tpu_custom_call" | custom-call | tf_op jit(solution)/shard_map/pallas_call | solution.py:93
  95.1 1.5 %reshape.299 = bf16[4,8,2,512]{3,2,1,0:T(2,128)(2,1)} reshape(bf16[64,512]{1,0:T(8,128)(2,1)} %shard_map.91) | data formatting | bytes 131072 | tf_op jit(solution)/shard_map/reshape | solution.py:193
  (45 shorter events, 7.5 us)
Async XLA Ops:
  0.0 55.0 %copy-start = (bf16[32,32]{1,0:T(8,128)(2,1)S(1)}, bf16[32,32]{1,0:T(8,128)(2,1)}, u32[]{:S(2)}) copy-start(bf16[32,32]{1,0:T(8,128)(2,1)} %param.15) | copy-start | bytes 6148
  5.5 22.2 %copy-start.2 = (bf16[1,64,2,32,32]{1,4,3,2,0:T(8,128)(2,1)S(1)}, bf16[1,64,2,32,32]{1,4,3,2,0:T(8,128)(2,1)}, u32[]{:S(2)}) copy-start(bf16[1,64,2,32,32]{1,4,3,2,0:T(8,128)(2,1)} %param.17) | copy-start | bytes 786436
  8.2 33.2 %all-to-all-start = ((bf16[64,8,128]{2,1,0:T(8,128)(2,1)}), bf16[64,8,128]{2,1,0:T(8,128)(2,1)S(1)}, u32[]{:S(2)}, u32[]{:S(2)}) async-start(bf16[64,8,128]{2,1,0:T(8,128)(2,1)} %copy.46), calls=%async_computation | async-start | bytes 262144 | tf_op jit(solution)/shard_map/all_to_all | solution.py:155
  44.8 10.3 %copy-start.3 = (f32[32]{0:T(128)S(1)}, f32[32]{0:T(128)}, u32[]{:S(2)}) copy-start(f32[32]{0:T(128)} %param.16) | copy-start | bytes 388
  49.5 18.8 %all-to-all-start.1 = ((bf16[64,2,512]{2,1,0:T(2,128)(2,1)}), bf16[64,2,512]{2,1,0:T(2,128)(2,1)S(1)}, u32[]{:S(2)}, u32[]{:S(2)}) async-start(bf16[64,2,512]{2,1,0:T(2,128)(2,1)} %reshape.310), calls=%async_computation.1 | async-start | bytes 262144 | tf_op jit(solution)/shard_map/all_to_all | solution.py:172
  72.4 2.9 %copy-start.1 = (f32[32,8,2,512]{3,0,2,1:T(8,128)S(1)}, f32[32,8,2,512]{3,0,2,1:T(8,128)}, u32[]{:S(2)}) copy-start(f32[32,8,2,512]{3,0,2,1:T(8,128)} %fusion.2) | copy-start | bytes 3145732

commit v3 on v2

--- a/solution.py
+++ b/solution.py
@@ -102,6 +102,79 @@
         ],
         compiler_params=pltpu.CompilerParams(collective_id=0, has_side_effects=True),
     )(layer)
+
+
+def slab_exchange_kernel(parts, blocks_ref, out_ref, landed, send_sems, recv_sems):
+    me = lax.axis_index("slab")
+    member = lax.axis_index("member")
+    barrier = pltpu.get_barrier_semaphore()
+
+    def greet(step, carry):
+        peer = lax.rem(me + step, parts)
+        pl.semaphore_signal(barrier, inc=1, device_id=(member, peer), device_id_type=pl.DeviceIdType.MESH)
+        return carry
+
+    lax.fori_loop(1, parts, greet, 0)
+    pl.semaphore_wait(barrier, parts - 1)
+
+    def send(step, carry):
+        peer = lax.rem(me + step, parts)
+        pltpu.make_async_remote_copy(
+            src_ref=blocks_ref.at[peer],
+            dst_ref=landed.at[me],
+            send_sem=send_sems.at[peer],
+            recv_sem=recv_sems.at[me],
+            device_id=(member, peer),
+            device_id_type=pl.DeviceIdType.MESH,
+        ).start()
+        return carry
+
+    lax.fori_loop(1, parts, send, 0)
+    landed[me] = blocks_ref[me]
+
+    def receive(step, carry):
+        source = lax.rem(me + parts - step, parts)
+        pltpu.make_async_remote_copy(
+            src_ref=blocks_ref.at[source],
+            dst_ref=landed.at[source],
+            send_sem=send_sems.at[source],
+            recv_sem=recv_sems.at[source],
+            device_id=(member, source),
+            device_id_type=pl.DeviceIdType.MESH,
+        ).wait_recv()
+        return carry
+
+    lax.fori_loop(1, parts, receive, 0)
+
+    def sent(step, carry):
+        peer = lax.rem(me + step, parts)
+        pltpu.make_async_remote_copy(
+            src_ref=blocks_ref.at[peer],
+            dst_ref=landed.at[me],
+            send_sem=send_sems.at[peer],
+            recv_sem=recv_sems.at[me],
+            device_id=(member, peer),
+            device_id_type=pl.DeviceIdType.MESH,
+        ).wait_send()
+        return carry
+
+    lax.fori_loop(1, parts, sent, 0)
+    out_ref[...] = landed[...]
+
+
+def slab_exchange(blocks, parts, exchange_id):
+    return pl.pallas_call(
+        functools.partial(slab_exchange_kernel, parts),
+        out_shape=jax.ShapeDtypeStruct(blocks.shape, blocks.dtype),
+        in_specs=[pl.BlockSpec(memory_space=pltpu.VMEM)],
+        out_specs=pl.BlockSpec(memory_space=pltpu.VMEM),
+        scratch_shapes=[
+            pltpu.VMEM(blocks.shape, blocks.dtype),
+            pltpu.SemaphoreType.DMA((parts,)),
+            pltpu.SemaphoreType.DMA((parts,)),
+        ],
+        compiler_params=pltpu.CompilerParams(collective_id=exchange_id, has_side_effects=True),
+    )(blocks)
 
 
 def local(
@@ -152,7 +225,7 @@
     full_cos, full_sin = phases(frequency_x, jnp.arange(length_x, dtype=jnp.int32), length_x)
     full_cos = full_cos.astype(jnp.bfloat16)
     full_sin = full_sin.astype(jnp.bfloat16)
-    gathered = lax.all_to_all(packed, "slab", 0, 1, tiled=True)
+    gathered = slab_exchange(packed, slab_count, 1).reshape(length_x, packed_width)[None]
     spectrum = forward_x(gathered, full_cos, full_sin)
     spectrum = spectrum.astype(jnp.bfloat16).reshape(local_modes, modes_x, 2, channels, plane_count)
     weight_real = spectral_weight[:, :, 0]
@@ -169,7 +242,7 @@
         .reshape(local_modes, modes_x, packed_width)
     )
     returned = inverse_x(mixed, full_cos, full_sin).astype(jnp.bfloat16)
-    returned = lax.all_to_all(returned, "slab", 1, 0, tiled=True)
+    returned = slab_exchange(returned.reshape(slab_count, slab_rows, packed_width), slab_count, 2)
     returned = returned.reshape(modes_y, slab_rows, 2, channels, plane_count)
     weights_y = jnp.where(jnp.arange(modes_y) == 0, 1.0, 2.0).astype(jnp.float32) / (
         length_x * length_y

time: 97.6 us -> 89.8 us (0.920)
  the two profiles are of different devices: /device:TPU:1 before, /device:TPU:57 now
where the time goes in v3:
time: 89.8 us; the launch traced here: 89.2 us
  Pallas kernels  65.3 us (73%)
  local copies, waits for them, and re-layouts  11.5 us (13%)
  matrix products  7.81 us (9%)
  other arithmetic  3.02 us (3%)
  between operations  1.6 us (2%)
    pallas_call x2, Pallas kernels, slab_exchange(): pl.pallas_call(functools.partial(slab_exchange_kernel, parts), out_shape=...  45.7 us
    pallas_call x1, Pallas kernels, member_sum(): pl.pallas_call(functools.partial(member_sum_kernel, members), out_shape=j...  19.7 us
    unnamed x16, local copies, waits for them, and re-layouts  3.71 us

profile of v3, /device:TPU:57, one launch (start us, length us, event | category | flops | bytes accessed | tf_op | source)
XLA Modules:
  0.0 89.2 jit_solution(16377145114771999537)
XLA Ops:
  1.3 0.6 copy-done.4
  2.0 0.6 fusion.79
  2.6 0.6 broadcast_multiply_fusion
  3.4 1.5 %multiply_convert_fusion = bf16[32,8,2,512]{3,0,2,1:T(8,128)(2,1)S(1)} fusion(bf16[32,8,2,512]{3,2,1,0:T(2,128)(2,1)} %param.9, f32[8,2,512]{2,1,0:T(2,128)S(1)} %convert_element_type.143, f32[32]{0:T(128)S(1)} %broadcast_multiply_fusion), kind=kLoop, calls=%fused_computation.23 | loop fusion | flops 1572864 | bytes 1081472 | tf_op jit(solution)/shard_map/convert_element_type | solution.py:204
  4.9 0.8 fusion.5
  5.6 0.8 fusion.4
  6.6 0.9 copy.38.blocks_ref
  7.5 25.8 %shard_map.91 = bf16[64,8,128]{2,1,0:T(8,128)(2,1)} custom-call(bf16[64,8,128]{2,1,0:T(8,128)(2,1)} %copy.38.blocks_ref), custom_call_target="tpu_custom_call" | custom-call | tf_op jit(solution)/shard_map/pallas_call | solution.py:166
  33.3 1.0 %copy.39 = bf16[128,512]{1,0:T(8,128)(2,1)S(1)} copy(bf16[128,512]{0,1:T(8,128)(2,1)} %bitcast.126) | data formatting | bytes 262144 | tf_op jit(solution)/shard_map/kxf,mx->kmf/dot_general | solution.py:23
  34.3 0.6 convolution_bitcast_fusion.2
  35.0 0.7 convolution_bitcast_fusion.3
  36.9 0.7 copy-done.1
  37.7 0.8 copy.63
  39.4 0.8 copy.61
  41.2 0.7 convolution_bitcast_fusion
  41.9 0.7 convolution_bitcast_fusion.1
  42.9 0.8 convert_element_type.161.blocks_ref
  43.7 19.9 %shard_map.92 = bf16[64,8,128]{2,1,0:T(8,128)(2,1)} custom-call(bf16[64,8,128]{2,1,0:T(8,128)(2,1)} %convert_element_type.161.blocks_ref), custom_call_target="tpu_custom_call" | custom-call | tf_op jit(solution)/shard_map/pallas_call | solution.py:166
  63.5 1.2 %copy.51 = bf16[64,8,128]{0,1,2:T(8,128)(2,1)S(1)} copy(bf16[64,8,128]{2,1,0:T(8,128)(2,1)} %shard_map.92) | data formatting | bytes 262144 | tf_op jit(solution)/shard_map/pallas_call | solution.py:166
  64.7 0.8 fusion.33
  65.5 1.0 %fusion.13 = bf16[32,8,2,512]{3,0,2,1:T(8,128)(2,1)S(1)} fusion(f32[32,8,2,512]{3,0,2,1:T(8,128)S(1)} %fusion.2, f32[512,8,32,2]{0,2,3,1:T(8,128)S(1)} %fusion.33, bf16[64,8,1,32,2]{0,1,4,3,2:T(8,128)(2,1)S(1)} %get-tuple-element.9, f32[64]{0:T(128)S(1)} %fusion.80), kind=kOutput, calls=%fused_computation.22 | convolution fusion | flops 36962304 | bytes 2687232 | tf_op jit(solution)/shard_map/kxcz,ky->cxzy/dot_general | solution.py:255
  67.1 1.0 %reshape.284.layer_ref = bf16[8,64,512]{2,1,0:T(8,128)(2,1)} reshape(bf16[32,8,2,512]{3,2,1,0:T(2,128)(2,1)S(1)} %copy.54) | data formatting | bytes 1048576 | tf_op jit(solution)/shard_map/reshape | solution.py:264
  68.1 19.7 %shard_map.93 = bf16[64,512]{1,0:T(8,128)(2,1)} custom-call(bf16[8,64,512]{2,1,0:T(8,128)(2,1)} %reshape.284.layer_ref), custom_call_target="tpu_custom_call" | custom-call | tf_op jit(solution)/shard_map/pallas_call | solution.py:93
  87.7 1.5 %reshape.285 = bf16[4,8,2,512]{3,2,1,0:T(2,128)(2,1)} reshape(bf16[64,512]{1,0:T(8,128)(2,1)} %shard_map.93) | data formatting | bytes 131072 | tf_op jit(solution)/shard_map/reshape | solution.py:266
  (41 shorter events, 4.3 us)
Async XLA Ops:
  0.0 36.1 %copy-start = (bf16[32,32]{1,0:T(8,128)(2,1)S(1)}, bf16[32,32]{1,0:T(8,128)(2,1)}, u32[]{:S(2)}) copy-start(bf16[32,32]{1,0:T(8,128)(2,1)} %param.15) | copy-start | bytes 6148
  0.0 3.4 %copy-start.2 = (bf16[8,2,512]{2,1,0:T(2,128)(2,1)S(1)}, bf16[8,2,512]{2,1,0:T(2,128)(2,1)}, u32[]{:S(2)}) copy-start(bf16[8,2,512]{2,1,0:T(2,128)(2,1)} %param.10) | copy-start | bytes 49156
  1.3 0.7 copy-start.4
  2.0 0.7 copy-start.5
  35.9 0.7 copy-start.3
  36.6 1.0 %copy-start.1 = (bf16[1,64,2,32,32]{1,4,3,2,0:T(8,128)(2,1)S(1)}, bf16[1,64,2,32,32]{1,4,3,2,0:T(8,128)(2,1)}, u32[]{:S(2)}) copy-start(bf16[1,64,2,32,32]{1,4,3,2,0:T(8,128)(2,1)} %param.17) | copy-start | bytes 786436

commit v4 on v2

--- a/solution.py
+++ b/solution.py
@@ -102,6 +102,107 @@
         ],
         compiler_params=pltpu.CompilerParams(collective_id=0, has_side_effects=True),
     )(layer)
+
+
+def slab_exchange_kernel(outer, inner, blocks_ref, out_ref, middle, landed, first_send, first_recv,
+                         second_send, second_recv, own_sems):
+    me = lax.axis_index("slab")
+    member = lax.axis_index("member")
+    row, col = me // inner, me % inner
+    mesh_kind = pl.DeviceIdType.MESH
+    barrier = pltpu.get_barrier_semaphore()
+    for step in range(1, inner):
+        peer = row * inner + lax.rem(col + step, inner)
+        pl.semaphore_signal(barrier, inc=1, device_id=(member, peer), device_id_type=mesh_kind)
+    for step in range(1, outer):
+        peer = lax.rem(row + step, outer) * inner + col
+        pl.semaphore_signal(barrier, inc=1, device_id=(member, peer), device_id_type=mesh_kind)
+    pl.semaphore_wait(barrier, inner + outer - 2)
+
+    def first_copy(other):
+        return pltpu.make_async_remote_copy(
+            src_ref=blocks_ref.at[:, other],
+            dst_ref=middle.at[col],
+            send_sem=first_send.at[other],
+            recv_sem=first_recv.at[col],
+            device_id=(member, row * inner + other),
+            device_id_type=mesh_kind,
+        )
+
+    def first_arrival(other):
+        return pltpu.make_async_remote_copy(
+            src_ref=blocks_ref.at[:, col],
+            dst_ref=middle.at[other],
+            send_sem=first_send.at[other],
+            recv_sem=first_recv.at[other],
+            device_id=(member, row * inner + other),
+            device_id_type=mesh_kind,
+        )
+
+    for step in range(1, inner):
+        first_copy(lax.rem(col + step, inner)).start()
+    own_first = pltpu.make_async_copy(blocks_ref.at[:, col], middle.at[col], own_sems.at[0])
+    own_first.start()
+    own_first.wait()
+    for step in range(1, inner):
+        first_arrival(lax.rem(col + inner - step, inner)).wait_recv()
+    for step in range(1, inner):
+        first_copy(lax.rem(col + step, inner)).wait_send()
+
+    def second_copy(other):
+        return pltpu.make_async_remote_copy(
+            src_ref=middle.at[:, other],
+            dst_ref=landed.at[row],
+            send_sem=second_send.at[other],
+            recv_sem=second_recv.at[row],
+            device_id=(member, other * inner + col),
+            device_id_type=mesh_kind,
+        )
+
+    def second_arrival(other):
+        return pltpu.make_async_remote_copy(
+            src_ref=middle.at[:, row],
+            dst_ref=landed.at[other],
+            send_sem=second_send.at[other],
+            recv_sem=second_recv.at[other],
+            device_id=(member, other * inner + col),
+            device_id_type=mesh_kind,
+        )
+
+    for step in range(1, outer):
+        second_copy(lax.rem(row + step, outer)).start()
+    own_second = pltpu.make_async_copy(middle.at[:, row], landed.at[row], own_sems.at[1])
+    own_second.start()
+    own_second.wait()
+    for step in range(1, outer):
+        second_arrival(lax.rem(row + outer - step, outer)).wait_recv()
+    for step in range(1, outer):
+        second_copy(lax.rem(row + step, outer)).wait_send()
+    out_ref[...] = landed[...]
+
+
+def slab_exchange(blocks, parts, exchange_id):
+    inner = 8 if parts % 8 == 0 else 1
+    outer = parts // inner
+    rows, width = blocks.shape[1], blocks.shape[2]
+    grid_blocks = blocks.reshape(outer, inner, rows, width)
+    result = pl.pallas_call(
+        functools.partial(slab_exchange_kernel, outer, inner),
+        out_shape=jax.ShapeDtypeStruct((outer, inner, rows, width), blocks.dtype),
+        in_specs=[pl.BlockSpec(memory_space=pltpu.VMEM)],
+        out_specs=pl.BlockSpec(memory_space=pltpu.VMEM),
+        scratch_shapes=[
+            pltpu.VMEM((inner, outer, rows, width), blocks.dtype),
+            pltpu.VMEM((outer, inner, rows, width), blocks.dtype),
+            pltpu.SemaphoreType.DMA((inner,)),
+            pltpu.SemaphoreType.DMA((inner,)),
+            pltpu.SemaphoreType.DMA((outer,)),
+            pltpu.SemaphoreType.DMA((outer,)),
+            pltpu.SemaphoreType.DMA((2,)),
+        ],
+        compiler_params=pltpu.CompilerParams(collective_id=exchange_id, has_side_effects=True),
+    )(grid_blocks)
+    return result.reshape(parts, rows, width)
 
 
 def local(
@@ -152,7 +253,7 @@
     full_cos, full_sin = phases(frequency_x, jnp.arange(length_x, dtype=jnp.int32), length_x)
     full_cos = full_cos.astype(jnp.bfloat16)
     full_sin = full_sin.astype(jnp.bfloat16)
-    gathered = lax.all_to_all(packed, "slab", 0, 1, tiled=True)
+    gathered = slab_exchange(packed, slab_count, 1).reshape(length_x, packed_width)[None]
     spectrum = forward_x(gathered, full_cos, full_sin)
     spectrum = spectrum.astype(jnp.bfloat16).reshape(local_modes, modes_x, 2, channels, plane_count)
     weight_real = spectral_weight[:, :, 0]
@@ -169,7 +270,7 @@
         .reshape(local_modes, modes_x, packed_width)
     )
     returned = inverse_x(mixed, full_cos, full_sin).astype(jnp.bfloat16)
-    returned = lax.all_to_all(returned, "slab", 1, 0, tiled=True)
+    returned = slab_exchange(returned.reshape(slab_count, slab_rows, packed_width), slab_count, 2)
     returned = returned.reshape(modes_y, slab_rows, 2, channels, plane_count)
     weights_y = jnp.where(jnp.arange(modes_y) == 0, 1.0, 2.0).astype(jnp.float32) / (
         length_x * length_y

time: 97.6 us -> 97.2 us (level)
  Pallas kernels: 17.3 us -> 64 us
  starting transfers between devices: 25.1 us -> 0 us
  waiting for transfers between devices: 23.3 us -> 0 us
  local copies, waits for them, and re-layouts: 14 us -> 17.8 us
  other arithmetic: 6.57 us -> 5.16 us
  matrix products: 8.77 us -> 7.77 us
    pallas_call x0 -> x2, Pallas kernels: none -> 44.5 us  [slab_exchange(): pl.pallas_call(functools.partial(slab_exchange_kernel, outer, inner), out...]
    all_to_all x2 -> x0, starting transfers between devices: 25.1 us -> none  [the longest x1 19.6 us: local(): gathered = lax.all_to_all(packed, 'slab', 0, 1, tiled=True)]
    all_to_all x2 -> x0, waiting for transfers between devices: 23.3 us -> none  [the longest x1 12.1 us: local(): returned = lax.all_to_all(returned, 'slab', 1, 0, tiled=True)]
    pallas_call x0 -> x1, local copies, waits for them, and re-layouts: none -> 4.42 us  [slab_exchange(): pl.pallas_call(functools.partial(slab_exchange_kernel, outer, inner), out...]
    unnamed x17 -> x10, local copies, waits for them, and re-layouts: 5.23 us -> 1.78 us
    convert_element_type x1 -> x2, local copies, waits for them, and re-layouts: 0.86 us -> 4.2 us  [local(): packed = jnp.stack([y_real, y_imag], axis=2).astype(jnp.bfloat16).reshape...]
    reshape x1 -> x0, local copies, waits for them, and re-layouts: 2.48 us -> none  [local(): returned = returned.reshape(modes_y, slab_rows, 2, channels, plane_count)]
    pallas_call x1, Pallas kernels: 17.3 us -> 19.5 us  [member_sum(): pl.pallas_call(functools.partial(member_sum_kernel, members), out_shape=j...]
  transfers between devices with their start and end apart: 2 -> 0, of which waited for: 2 -> 0; matrix products, arithmetic and copies ran while one was open for 3% -> 0% of each run, Pallas kernels for 0% -> 0%
where the time goes in v4:
time: 97.2 us; the launch traced here: 96.3 us
  Pallas kernels  64 us (66%)
  local copies, waits for them, and re-layouts  17.8 us (18%)
  matrix products  7.77 us (8%)
  other arithmetic  5.16 us (5%)
  between operations  1.6 us (2%)
    pallas_call x2, Pallas kernels, slab_exchange(): pl.pallas_call(functools.partial(slab_exchange_kernel, outer, inner), out...  44.5 us
    pallas_call x1, Pallas kernels, member_sum(): pl.pallas_call(functools.partial(member_sum_kernel, members), out_shape=j...  19.5 us
    pallas_call x1, local copies, waits for them, and re-layouts, slab_exchange(): pl.pallas_call(functools.partial(slab_exchange_kernel, outer, inner), out...  4.42 us
    convert_element_type x2, local copies, waits for them, and re-layouts, local(): packed = jnp.stack([y_real, y_imag], axis=2).astype(jnp.bfloat16).reshape...  4.2 us

profile of v4, /device:TPU:1, one launch (start us, length us, event | category | flops | bytes accessed | tf_op | source)
XLA Modules:
  0.0 96.3 jit_solution(11126997357830062506)
XLA Ops:
  0.0 0.7 convert_element_type.143
  1.4 1.3 %fusion.79 = f32[]{:T(128)} fusion(f32[16]{0:T(128)} %param.12, s32[]{:T(128)} %bitcast.129), kind=kLoop, calls=%fused_computation.104 | loop fusion | flops 47 | bytes 72 | tf_op jit(solution)/shard_map/reduce_sum | solution.py:228
  2.7 1.3 %broadcast_multiply_fusion = f32[32]{0:T(128)S(1)} fusion(f32[32]{0:T(128)} %param.11, f32[]{:T(128)} %fusion.79), kind=kLoop, calls=%fused_computation.108 | loop fusion | flops 32 | bytes 260 | tf_op jit(solution)/shard_map/mul | solution.py:229
  4.1 1.4 %multiply_convert_fusion = bf16[32,8,2,512]{3,0,2,1:T(8,128)(2,1)S(1)} fusion(bf16[32,8,2,512]{3,2,1,0:T(2,128)(2,1)} %param.9, f32[8,2,512]{2,1,0:T(2,128)S(1)} %convert_element_type.143, f32[32]{0:T(128)S(1)} %broadcast_multiply_fusion), kind=kLoop, calls=%fused_computation.23 | loop fusion | flops 1572864 | bytes 1081472 | tf_op jit(solution)/shard_map/convert_element_type | solution.py:232
  5.5 0.8 fusion.4
  6.3 0.8 fusion.5
  7.3 1.4 %convert_element_type.154 = bf16[8,8,8,128]{1,0,2,3:T(8,128)(2,1)S(1)} reshape(bf16[64,8,2,32,2]{0,1,4,3,2:T(8,128)(2,1)S(1)} %copy.37) | data formatting | bytes 262144 | tf_op jit(solution)/shard_map/convert_element_type | solution.py:244
  8.7 2.8 %copy.38.blocks_ref = bf16[8,8,8,128]{3,2,1,0:T(8,128)(2,1)} copy(bf16[8,8,8,128]{1,0,2,3:T(8,128)(2,1)S(1)} %convert_element_type.154) | data formatting | bytes 262144 | tf_op jit(solution)/shard_map/convert_element_type | solution.py:244
  11.5 26.4 %shard_map.91 = bf16[8,8,8,128]{3,2,1,0:T(8,128)(2,1)} custom-call(bf16[8,8,8,128]{3,2,1,0:T(8,128)(2,1)} %copy.38.blocks_ref), custom_call_target="tpu_custom_call" | custom-call | tf_op jit(solution)/shard_map/pallas_call | solution.py:189
  37.9 1.0 %copy.39 = bf16[128,512]{1,0:T(8,128)(2,1)S(1)} copy(bf16[128,512]{0,1:T(8,128)(2,1)} %bitcast.130) | data formatting | bytes 262144 | tf_op jit(solution)/shard_map/kxf,mx->kmf/dot_general | solution.py:23
  39.7 0.7 convolution_bitcast_fusion.3
  40.7 0.8 copy.63
  42.0 0.8 copy.61
  45.0 0.7 convolution_bitcast_fusion.1
  45.7 0.7 convolution_bitcast_fusion
  46.6 0.8 convert_element_type.161.blocks_ref
  47.4 18.1 %shard_map.92 = bf16[8,8,8,128]{3,2,1,0:T(8,128)(2,1)} custom-call(bf16[8,8,8,128]{3,2,1,0:T(8,128)(2,1)} %convert_element_type.161.blocks_ref), custom_call_target="tpu_custom_call" | custom-call | tf_op jit(solution)/shard_map/pallas_call | solution.py:189
  65.6 4.4 %copy.51 = bf16[8,8,8,128]{1,0,2,3:T(8,128)(2,1)S(1)} copy(bf16[8,8,8,128]{3,2,1,0:T(8,128)(2,1)} %shard_map.92) | data formatting | bytes 262144 | tf_op jit(solution)/shard_map/pallas_call | solution.py:189
  70.0 1.6 %reshape_reshape.2 = bf16[64,8,2,32,2]{0,1,4,3,2:T(8,128)(2,1)S(1)} reshape(bf16[8,8,8,128]{1,0,2,3:T(8,128)(2,1)S(1)} %copy.51) | data formatting | bytes 262144 | tf_op jit(solution)/shard_map/reshape;reshape | solution.py:274
  71.6 0.8 fusion.33
  72.7 1.0 %fusion.13 = bf16[32,8,2,512]{3,0,2,1:T(8,128)(2,1)S(1)} fusion(f32[32,8,2,512]{3,0,2,1:T(8,128)S(1)} %fusion.2, f32[512,8,32,2]{0,2,3,1:T(8,128)S(1)} %fusion.33, bf16[64,8,1,32,2]{0,1,4,3,2:T(8,128)(2,1)S(1)} %get-tuple-element.9, f32[64]{0:T(128)S(1)} %fusion.80), kind=kOutput, calls=%fused_computation.22 | convolution fusion | flops 36962304 | bytes 2687232 | tf_op jit(solution)/shard_map/kxcz,ky->cxzy/dot_general | solution.py:283
  74.3 1.0 %reshape.278.layer_ref = bf16[8,64,512]{2,1,0:T(8,128)(2,1)} reshape(bf16[32,8,2,512]{3,2,1,0:T(2,128)(2,1)S(1)} %copy.54) | data formatting | bytes 1048576 | tf_op jit(solution)/shard_map/reshape | solution.py:292
  75.3 19.5 %shard_map.93 = bf16[64,512]{1,0:T(8,128)(2,1)} custom-call(bf16[8,64,512]{2,1,0:T(8,128)(2,1)} %reshape.278.layer_ref), custom_call_target="tpu_custom_call" | custom-call | tf_op jit(solution)/shard_map/pallas_call | solution.py:93
  94.8 1.5 %reshape.279 = bf16[4,8,2,512]{3,2,1,0:T(2,128)(2,1)} reshape(bf16[64,512]{1,0:T(8,128)(2,1)} %shard_map.93) | data formatting | bytes 131072 | tf_op jit(solution)/shard_map/reshape | solution.py:294
  (37 shorter events, 4.4 us)
Async XLA Ops:
  0.0 72.4 %copy-start = (bf16[32,32]{1,0:T(8,128)(2,1)S(1)}, bf16[32,32]{1,0:T(8,128)(2,1)}, u32[]{:S(2)}) copy-start(bf16[32,32]{1,0:T(8,128)(2,1)} %param.15) | copy-start | bytes 6148
  8.7 32.0 %copy-start.1 = (bf16[1,64,2,32,32]{1,4,3,2,0:T(8,128)(2,1)S(1)}, bf16[1,64,2,32,32]{1,4,3,2,0:T(8,128)(2,1)}, u32[]{:S(2)}) copy-start(bf16[1,64,2,32,32]{1,4,3,2,0:T(8,128)(2,1)} %param.17) | copy-start | bytes 786436
  70.0 2.4 %copy-start.2 = (f32[32]{0:T(128)S(1)}, f32[32]{0:T(128)}, u32[]{:S(2)}) copy-start(f32[32]{0:T(128)} %param.16) | copy-start | bytes 388

commit v5 on v3

--- a/solution.py
+++ b/solution.py
@@ -49,59 +49,61 @@
     return jnp.einsum("kmoi,kmiz->kmoz", weights, values, preferred_element_type=jnp.float32)
 
 
-def member_sum_kernel(members, layer_ref, out_ref, landed, send_sems, recv_sems):
+def layer_sum_kernel(members, back_ref, table_ref, kron_ref, field_ref, bias_ref, out_ref, layer, landed,
+                     send_sems, recv_sems):
     me = lax.axis_index("member")
     slab = lax.axis_index("slab")
+    mesh_kind = pl.DeviceIdType.MESH
     barrier = pltpu.get_barrier_semaphore()
     for step in range(1, members):
         peer = lax.rem(me + step, members)
-        pl.semaphore_signal(barrier, inc=1, device_id=(peer, slab), device_id_type=pl.DeviceIdType.MESH)
+        pl.semaphore_signal(barrier, inc=1, device_id=(peer, slab), device_id_type=mesh_kind)
+    spectral = jnp.dot(back_ref[...], table_ref[...], preferred_element_type=jnp.float32)
+    pointwise = jnp.dot(kron_ref[...], field_ref[...], preferred_element_type=jnp.float32)
+    value = jax.nn.gelu(pointwise + bias_ref[...] + spectral, approximate=True)
+    layer[...] = value.astype(layer.dtype).reshape(layer.shape)
     pl.semaphore_wait(barrier, members - 1)
-    copies = []
+
+    def copy_of(source, target, peer):
+        return pltpu.make_async_remote_copy(
+            src_ref=layer.at[source],
+            dst_ref=landed.at[target],
+            send_sem=send_sems.at[source],
+            recv_sem=recv_sems.at[target],
+            device_id=(peer, slab),
+            device_id_type=mesh_kind,
+        )
+
     for step in range(1, members):
         peer = lax.rem(me + step, members)
-        copy = pltpu.make_async_remote_copy(
-            src_ref=layer_ref.at[peer],
-            dst_ref=landed.at[me],
-            send_sem=send_sems.at[peer],
-            recv_sem=recv_sems.at[me],
-            device_id=(peer, slab),
-            device_id_type=pl.DeviceIdType.MESH,
-        )
-        copy.start()
-        copies.append(copy)
-    total = layer_ref[me].astype(jnp.float32)
+        copy_of(peer, me, peer).start()
+    total = layer[me].astype(jnp.float32)
     for step in range(1, members):
         source = lax.rem(me + members - step, members)
-        arrival = pltpu.make_async_remote_copy(
-            src_ref=layer_ref.at[source],
-            dst_ref=landed.at[source],
-            send_sem=send_sems.at[source],
-            recv_sem=recv_sems.at[source],
-            device_id=(source, slab),
-            device_id_type=pl.DeviceIdType.MESH,
-        )
-        arrival.wait_recv()
+        copy_of(source, source, source).wait_recv()
         total = total + landed[source].astype(jnp.float32)
-    for copy in copies:
-        copy.wait_send()
+    for step in range(1, members):
+        peer = lax.rem(me + step, members)
+        copy_of(peer, me, peer).wait_send()
     out_ref[...] = (total / members).astype(out_ref.dtype)
 
 
-def member_sum(layer, members):
-    block_rows, width = layer.shape[1], layer.shape[2]
+def layer_sum(back, table, kron, field, bias, members):
+    rows, width = field.shape
+    block_rows = rows // members
     return pl.pallas_call(
-        functools.partial(member_sum_kernel, members),
+        functools.partial(layer_sum_kernel, members),
         out_shape=jax.ShapeDtypeStruct((block_rows, width), jnp.bfloat16),
-        in_specs=[pl.BlockSpec(memory_space=pltpu.VMEM)],
+        in_specs=[pl.BlockSpec(memory_space=pltpu.VMEM)] * 5,
         out_specs=pl.BlockSpec(memory_space=pltpu.VMEM),
         scratch_shapes=[
+            pltpu.VMEM((members, block_rows, width), jnp.bfloat16),
             pltpu.VMEM((members, block_rows, width), jnp.bfloat16),
             pltpu.SemaphoreType.DMA((members,)),
             pltpu.SemaphoreType.DMA((members,)),
         ],
         compiler_params=pltpu.CompilerParams(collective_id=0, has_side_effects=True),
-    )(layer)
+    )(back, table, kron, field, bias)
 
 
 def slab_exchange_kernel(parts, blocks_ref, out_ref, landed, send_sems, recv_sems):
@@ -249,20 +251,17 @@
     )
     back_cos = (weights_y[:, None] * y_cos).astype(jnp.bfloat16)
     back_sin = (weights_y[:, None] * y_sin).astype(jnp.bfloat16)
-    spectral = jnp.einsum(
-        "kxcz,ky->cxzy", returned[:, :, 0], back_cos, preferred_element_type=jnp.float32
-    )
-    spectral = spectral - jnp.einsum(
-        "kxcz,ky->cxzy", returned[:, :, 1], back_sin, preferred_element_type=jnp.float32
-    )
-    pointwise = (
-        jnp.einsum("oc,cxzy->oxzy", point_weight, field_now, preferred_element_type=jnp.float32)
-        + point_bias[:, None, None, None]
-    )
-    layer = jax.nn.gelu(pointwise + spectral, approximate=True).astype(jnp.bfloat16)
+    table = jnp.concatenate([back_cos, -back_sin], axis=0)
+    rows = channels * slab_rows * plane_count
+    back = returned.transpose(3, 1, 4, 2, 0).reshape(rows, 2 * modes_y)
+    cells = slab_rows * plane_count
+    kron = (
+        point_weight[:, None, :, None] * jnp.eye(cells, dtype=point_weight.dtype)[None, :, None, :]
+    ).reshape(rows, rows)
+    bias = jnp.repeat(point_bias, cells).reshape(rows, 1)
+    field_rows = field_now.reshape(rows, length_y)
     members = lax.axis_size("member")
-    blocks = layer.reshape(members, -1, length_y)
-    total = member_sum(blocks, members)
+    total = layer_sum(back, table, kron, field_rows, bias, members)
     return total.reshape(channels // members, slab_rows, plane_count, length_y)
 
 

time: 89.8 us -> 103 us (1.15)
  the two profiles are of different devices: /device:TPU:57 before, /device:TPU:1 now
where the time goes in v5:
time: 103 us; the launch traced here: 101 us
  Pallas kernels  64.7 us (63%)
  local copies, waits for them, and re-layouts  19.4 us (19%)
  other arithmetic  9.55 us (9%)
  matrix products  6.03 us (6%)
  between operations  1.56 us (2%)
    pallas_call x2, Pallas kernels, slab_exchange(): pl.pallas_call(functools.partial(slab_exchange_kernel, parts), out_shape=...  46.3 us
    pallas_call x1, Pallas kernels, layer_sum(): pl.pallas_call(functools.partial(layer_sum_kernel, members), out_shape=ja...  18.4 us
    mul x1, local copies, waits for them, and re-layouts, local(): point_weight[:, None, :, None]  8.4 us
    mul x1, other arithmetic, local(): point_weight[:, None, :, None]  2.28 us

profile of v5, /device:TPU:1, one launch (start us, length us, event | category | flops | bytes accessed | tf_op | source)
XLA Modules:
  0.0 101.2 jit_solution(12059648724571258954)
XLA Ops:
  0.0 0.8 convert_element_type.154
  1.4 1.3 %fusion.62 = f32[]{:T(128)} fusion(f32[16]{0:T(128)} %param.12, s32[]{:T(128)} %bitcast.93), kind=kLoop, calls=%fused_computation.89 | loop fusion | flops 47 | bytes 72 | tf_op jit(solution)/shard_map/reduce_sum | solution.py:202
  2.7 1.2 %broadcast_multiply_fusion.1 = f32[32]{0:T(128)S(1)} fusion(f32[32]{0:T(128)} %param.11, f32[]{:T(128)} %fusion.62), kind=kLoop, calls=%fused_computation.93 | loop fusion | flops 32 | bytes 260 | tf_op jit(solution)/shard_map/mul | solution.py:203
  3.9 2.0 %multiply_convert_fusion = bf16[32,8,2,512]{3,2,1,0:T(2,128)(2,1)S(1)} fusion(bf16[32,8,2,512]{3,2,1,0:T(2,128)(2,1)} %param.9, f32[8,2,512]{2,1,0:T(2,128)S(1)} %convert_element_type.154, f32[32]{0:T(128)S(1)} %broadcast_multiply_fusion.1), kind=kLoop, calls=%fused_computation.10 | loop fusion | flops 1572864 | bytes 1081472 | tf_op jit(solution)/shard_map/convert_element_type | solution.py:206
  6.0 0.9 fusion.1
  6.9 0.9 fusion.2
  8.1 0.9 copy.38.blocks_ref
  8.9 27.2 %shard_map.91 = bf16[64,8,128]{2,1,0:T(8,128)(2,1)} custom-call(bf16[64,8,128]{2,1,0:T(8,128)(2,1)} %copy.38.blocks_ref), custom_call_target="tpu_custom_call" | custom-call | tf_op jit(solution)/shard_map/pallas_call | solution.py:168
  36.1 1.0 copy.39
  37.9 0.7 convolution_bitcast_fusion.3
  38.9 0.8 copy.59
  40.3 0.8 copy.57
  43.2 0.7 convolution_bitcast_fusion.1
  43.9 0.7 convolution_bitcast_fusion
  44.8 0.8 convert_element_type.164.blocks_ref
  45.6 19.1 %shard_map.92 = bf16[64,8,128]{2,1,0:T(8,128)(2,1)} custom-call(bf16[64,8,128]{2,1,0:T(8,128)(2,1)} %convert_element_type.164.blocks_ref), custom_call_target="tpu_custom_call" | custom-call | tf_op jit(solution)/shard_map/pallas_call | solution.py:168
  64.8 1.2 %copy.51 = bf16[64,8,128]{0,1,2:T(8,128)(2,1)S(1)} copy(bf16[64,8,128]{2,1,0:T(8,128)(2,1)} %shard_map.92) | data formatting | bytes 262144 | tf_op jit(solution)/shard_map/pallas_call | solution.py:168
  66.2 0.8 reshape.299.back_ref
  67.0 1.0 reshape.300.field_ref
  69.7 2.3 %broadcast_multiply_fusion = bf16[32,16,32,16]{3,2,1,0:T(8,128)(2,1)} fusion(bf16[16,16]{1,0:T(8,128)(2,1)S(1)} %fusion.61, bf16[32,32]{1,0:T(8,128)(2,1)S(1)} %copy-done.1), kind=kLoop, calls=%fused_computation | loop fusion | flops 262144 | bytes 526848 | tf_op jit(solution)/shard_map/mul | solution.py:259
  72.0 8.4 %mul.227.kron_ref = bf16[512,512]{1,0:T(8,128)(2,1)} reshape(bf16[32,16,32,16]{3,2,1,0:T(8,128)(2,1)} %broadcast_multiply_fusion) | data formatting | bytes 1048576 | tf_op jit(solution)/shard_map/mul | solution.py:259
  80.5 0.9 reshape_reshape.4.bias_ref
  81.3 18.4 %shard_map.93 = bf16[64,512]{1,0:T(8,128)(2,1)} custom-call(bf16[512,128]{1,0:T(8,128)(2,1)} %reshape.299.back_ref, bf16[128,512]{1,0:T(8,128)(2,1)} %pad_maximum_fusion.2.table_ref, bf16[512,512]{1,0:T(8,128)(2,1)} %mul.227.kron_ref, bf16[512,512]{1,0:T(8,128)(2,1)} %reshape.300.field_ref, f32[512,1]{1,0:T(8,128)} %reshape_reshape.4.bias_ref), custom_call_target="tpu_custom_call" | custom-call | tf_op jit(solution)/shard_map/pallas_call | solution.py:94
  99.7 1.5 %reshape.301 = bf16[4,8,2,512]{3,2,1,0:T(2,128)(2,1)} reshape(bf16[64,512]{1,0:T(8,128)(2,1)} %shard_map.93) | data formatting | bytes 131072 | tf_op jit(solution)/shard_map/reshape | solution.py:265
  (40 shorter events, 5.5 us)
Async XLA Ops:
  0.0 38.9 %copy-start = (bf16[1,64,2,32,32]{1,4,3,2,0:T(8,128)(2,1)S(1)}, bf16[1,64,2,32,32]{1,4,3,2,0:T(8,128)(2,1)}, u32[]{:S(2)}) copy-start(bf16[1,64,2,32,32]{1,4,3,2,0:T(8,128)(2,1)} %param.17) | copy-start | bytes 786436
  41.0 28.7 %copy-start.1 = (bf16[32,32]{1,0:T(8,128)(2,1)S(1)}, bf16[32,32]{1,0:T(8,128)(2,1)}, u32[]{:S(2)}) copy-start(bf16[32,32]{1,0:T(8,128)(2,1)} %param.15) | copy-start | bytes 6148
  69.7 10.7 %copy-start.2 = (f32[32]{0:T(128)S(1)}, f32[32]{0:T(128)}, u32[]{:S(2)}) copy-start(f32[32]{0:T(128)} %param.16) | copy-start | bytes 388

commit v6 on v5

--- a/solution.py
+++ b/solution.py
@@ -49,8 +49,8 @@
     return jnp.einsum("kmoi,kmiz->kmoz", weights, values, preferred_element_type=jnp.float32)
 
 
-def layer_sum_kernel(members, back_ref, table_ref, kron_ref, field_ref, bias_ref, out_ref, layer, landed,
-                     send_sems, recv_sems):
+def layer_sum_kernel(members, back_ref, table_ref, weight_ref, field_ref, bias_ref, out_ref, value, layer,
+                     landed, send_sems, recv_sems):
     me = lax.axis_index("member")
     slab = lax.axis_index("slab")
     mesh_kind = pl.DeviceIdType.MESH
@@ -58,10 +58,16 @@
     for step in range(1, members):
         peer = lax.rem(me + step, members)
         pl.semaphore_signal(barrier, inc=1, device_id=(peer, slab), device_id_type=mesh_kind)
-    spectral = jnp.dot(back_ref[...], table_ref[...], preferred_element_type=jnp.float32)
-    pointwise = jnp.dot(kron_ref[...], field_ref[...], preferred_element_type=jnp.float32)
-    value = jax.nn.gelu(pointwise + bias_ref[...] + spectral, approximate=True)
-    layer[...] = value.astype(layer.dtype).reshape(layer.shape)
+    cells = back_ref.shape[0]
+    length = table_ref.shape[1]
+    block_rows = layer.shape[1]
+    for cell in range(cells):
+        lanes = pl.ds(cell * length, length)
+        spectral = jnp.dot(back_ref[cell], table_ref[...], preferred_element_type=jnp.float32)
+        pointwise = jnp.dot(weight_ref[...], field_ref[:, lanes], preferred_element_type=jnp.float32)
+        value[:, lanes] = jax.nn.gelu(pointwise + bias_ref[...] + spectral, approximate=True)
+    for block in range(members):
+        layer[block] = value[pl.ds(block * block_rows, block_rows), :].astype(layer.dtype)
     pl.semaphore_wait(barrier, members - 1)
 
     def copy_of(source, target, peer):
@@ -88,22 +94,23 @@
     out_ref[...] = (total / members).astype(out_ref.dtype)
 
 
-def layer_sum(back, table, kron, field, bias, members):
-    rows, width = field.shape
-    block_rows = rows // members
+def layer_sum(back, table, weight, field, bias, members):
+    channels, width = field.shape
+    block_rows = channels // members
     return pl.pallas_call(
         functools.partial(layer_sum_kernel, members),
         out_shape=jax.ShapeDtypeStruct((block_rows, width), jnp.bfloat16),
         in_specs=[pl.BlockSpec(memory_space=pltpu.VMEM)] * 5,
         out_specs=pl.BlockSpec(memory_space=pltpu.VMEM),
         scratch_shapes=[
+            pltpu.VMEM((channels, width), jnp.float32),
             pltpu.VMEM((members, block_rows, width), jnp.bfloat16),
             pltpu.VMEM((members, block_rows, width), jnp.bfloat16),
             pltpu.SemaphoreType.DMA((members,)),
             pltpu.SemaphoreType.DMA((members,)),
         ],
         compiler_params=pltpu.CompilerParams(collective_id=0, has_side_effects=True),
-    )(back, table, kron, field, bias)
+    )(back, table, weight, field, bias)
 
 
 def slab_exchange_kernel(parts, blocks_ref, out_ref, landed, send_sems, recv_sems):
@@ -252,16 +259,12 @@
     back_cos = (weights_y[:, None] * y_cos).astype(jnp.bfloat16)
     back_sin = (weights_y[:, None] * y_sin).astype(jnp.bfloat16)
     table = jnp.concatenate([back_cos, -back_sin], axis=0)
-    rows = channels * slab_rows * plane_count
-    back = returned.transpose(3, 1, 4, 2, 0).reshape(rows, 2 * modes_y)
     cells = slab_rows * plane_count
-    kron = (
-        point_weight[:, None, :, None] * jnp.eye(cells, dtype=point_weight.dtype)[None, :, None, :]
-    ).reshape(rows, rows)
-    bias = jnp.repeat(point_bias, cells).reshape(rows, 1)
-    field_rows = field_now.reshape(rows, length_y)
+    back = returned.transpose(1, 4, 3, 2, 0).reshape(cells, channels, 2 * modes_y)
+    bias = point_bias.reshape(channels, 1)
+    field_rows = field_now.reshape(channels, cells * length_y)
     members = lax.axis_size("member")
-    total = layer_sum(back, table, kron, field_rows, bias, members)
+    total = layer_sum(back, table, point_weight, field_rows, bias, members)
     return total.reshape(channels // members, slab_rows, plane_count, length_y)
 
 

time: 103 us -> 89.7 us (0.87)
  local copies, waits for them, and re-layouts: 19.4 us -> 11 us
  other arithmetic: 9.55 us -> 5.15 us
    mul x1 -> x0, local copies, waits for them, and re-layouts: 8.4 us -> none  [local(): point_weight[:, None, :, None]]
    mul x1 -> x0, other arithmetic: 2.28 us -> none  [local(): point_weight[:, None, :, None]]
    reshape x2 -> x3, local copies, waits for them, and re-layouts: 1.8 us -> 2.68 us  [the longest x1 1.18 us: local(): field_rows = field_now.reshape(channels, cells * length_y)]
where the time goes in v6:
time: 89.7 us; the launch traced here: 88.3 us
  Pallas kernels  64.5 us (72%)
  local copies, waits for them, and re-layouts  11 us (12%)
  matrix products  6.04 us (7%)
  other arithmetic  5.15 us (6%)
  between operations  1.62 us (2%)
    pallas_call x2, Pallas kernels, slab_exchange(): pl.pallas_call(functools.partial(slab_exchange_kernel, parts), out_shape=...  46.3 us
    pallas_call x1, Pallas kernels, layer_sum(): pl.pallas_call(functools.partial(layer_sum_kernel, members), out_shape=ja...  18.2 us
    convert_element_type x1, other arithmetic, local(): field_now = (2.0 * jnp.tanh(0.5 * driven)).astype(jnp.bfloat16)  2.05 us

profile of v6, /device:TPU:1, one launch (start us, length us, event | category | flops | bytes accessed | tf_op | source)
XLA Modules:
  0.0 88.3 jit_solution(5018115744784956168)
XLA Ops:
  1.4 0.6 fusion.61
  2.0 0.6 broadcast_multiply_fusion
  2.7 0.7 copy.54.bias_ref
  3.4 0.5 fusion.41
  4.4 0.6 pad_maximum_fusion.2.table_ref
  5.0 2.0 %multiply_convert_fusion = bf16[32,8,2,512]{3,2,1,0:T(2,128)(2,1)S(1)} fusion(bf16[32,8,2,512]{3,2,1,0:T(2,128)(2,1)} %param.9, f32[8,2,512]{2,1,0:T(2,128)S(1)} %convert_element_type.147, f32[32]{0:T(128)S(1)} %broadcast_multiply_fusion), kind=kLoop, calls=%fused_computation.9 | loop fusion | flops 1572864 | bytes 1081472 | tf_op jit(solution)/shard_map/convert_element_type | solution.py:213
  7.1 0.9 %fusion.2 = bf16[64,8,1,32,2]{0,3,4,1,2:T(8,128)(2,1)S(1)} fusion(bf16[32,8,2,512]{3,2,1,0:T(2,128)(2,1)S(1)} %multiply_convert_fusion), kind=kOutput, calls=%fused_computation.6 | convolution fusion | flops 34111488 | bytes 589824 | tf_op jit(solution)/shard_map/cxzy,ky->kxcz/dot_general | solution.py:220
  8.0 0.9 %fusion.1 = bf16[64,8,1,32,2]{0,3,4,1,2:T(8,128)(2,1)S(1)} fusion(bf16[32,8,2,512]{3,2,1,0:T(2,128)(2,1)S(1)} %multiply_convert_fusion), kind=kOutput, calls=%fused_computation.5 | convolution fusion | flops 34078720 | bytes 589824 | tf_op jit(solution)/shard_map/cxzy,ky->kxcz/dot_general | solution.py:217
  8.9 1.2 %reshape.290.field_ref = bf16[32,8192]{1,0:T(8,128)(2,1)} reshape(bf16[32,8,2,512]{3,2,1,0:T(2,128)(2,1)S(1)} %multiply_convert_fusion) | data formatting | bytes 1048576 | tf_op jit(solution)/shard_map/reshape | solution.py:265
  10.3 0.9 copy.39.blocks_ref
  11.2 27.2 %shard_map.91 = bf16[64,8,128]{2,1,0:T(8,128)(2,1)} custom-call(bf16[64,8,128]{2,1,0:T(8,128)(2,1)} %copy.39.blocks_ref), custom_call_target="tpu_custom_call" | custom-call | tf_op jit(solution)/shard_map/pallas_call | solution.py:175
  38.4 1.0 %copy.40 = bf16[128,512]{1,0:T(8,128)(2,1)S(1)} copy(bf16[128,512]{0,1:T(8,128)(2,1)} %bitcast.95) | data formatting | bytes 262144 | tf_op jit(solution)/shard_map/kxf,mx->kmf/dot_general | solution.py:23
  39.4 0.6 convolution_bitcast_fusion.2
  40.1 0.7 convolution_bitcast_fusion.3
  41.2 0.8 copy.60
  42.9 0.8 copy.58
  44.7 0.7 convolution_bitcast_fusion
  45.4 0.7 convolution_bitcast_fusion.1
  46.4 0.8 convert_element_type.157.blocks_ref
  47.2 19.1 %shard_map.92 = bf16[64,8,128]{2,1,0:T(8,128)(2,1)} custom-call(bf16[64,8,128]{2,1,0:T(8,128)(2,1)} %convert_element_type.157.blocks_ref), custom_call_target="tpu_custom_call" | custom-call | tf_op jit(solution)/shard_map/pallas_call | solution.py:175
  66.3 1.2 %copy.52 = bf16[64,8,128]{0,1,2:T(8,128)(2,1)S(1)} copy(bf16[64,8,128]{2,1,0:T(8,128)(2,1)} %shard_map.92) | data formatting | bytes 262144 | tf_op jit(solution)/shard_map/pallas_call | solution.py:175
  67.8 0.8 reshape.289.back_ref
  68.6 18.2 %shard_map.93 = bf16[4,8192]{1,0:T(4,128)(2,1)} custom-call(bf16[16,32,128]{2,1,0:T(8,128)(2,1)} %reshape.289.back_ref, bf16[128,512]{1,0:T(8,128)(2,1)} %pad_maximum_fusion.2.table_ref, bf16[32,32]{1,0:T(8,128)(2,1)} %weight_ref.1, bf16[32,8192]{1,0:T(8,128)(2,1)} %reshape.290.field_ref, f32[32,1]{1,0:T(8,128)} %copy.54.bias_ref), custom_call_target="tpu_custom_call" | custom-call | tf_op jit(solution)/shard_map/pallas_call | solution.py:100
  86.8 1.6 %reshape.292 = bf16[4,8,2,512]{3,2,1,0:T(2,128)(2,1)} reshape(bf16[4,8192]{1,0:T(4,128)(2,1)} %shard_map.93) | data formatting | bytes 131072 | tf_op jit(solution)/shard_map/reshape | solution.py:268
  (40 shorter events, 3.6 us)
Async XLA Ops:
  0.7 0.7 copy-start.3
  0.7 1.3 %copy-start.4 = (f32[32]{0:T(128)S(1)}, f32[32]{0:T(128)}, u32[]{:S(2)}) copy-start(f32[32]{0:T(128)} %param.11) | copy-start | bytes 388
  0.7 2.0 %copy-start.2 = (f32[32]{0:T(128)S(1)}, f32[32]{0:T(128)}, u32[]{:S(2)}) copy-start(f32[32]{0:T(128)} %param.16) | copy-start | bytes 388
  1.4 2.0 %copy-start.1 = (bf16[8,2,512]{2,1,0:T(2,128)(2,1)S(1)}, bf16[8,2,512]{2,1,0:T(2,128)(2,1)}, u32[]{:S(2)}) copy-start(bf16[8,2,512]{2,1,0:T(2,128)(2,1)} %param.10) | copy-start | bytes 49156
  40.1 1.1 %copy-start = (bf16[1,64,2,32,32]{1,4,3,2,0:T(8,128)(2,1)S(1)}, bf16[1,64,2,32,32]{1,4,3,2,0:T(8,128)(2,1)}, u32[]{:S(2)}) copy-start(bf16[1,64,2,32,32]{1,4,3,2,0:T(8,128)(2,1)} %param.17) | copy-start | bytes 786436

commit v7 on v6

--- a/solution.py
+++ b/solution.py
@@ -50,53 +50,74 @@
 
 
 def layer_sum_kernel(members, back_ref, table_ref, weight_ref, field_ref, bias_ref, out_ref, value, layer,
-                     landed, send_sems, recv_sems):
+                     near, part, far, near_sems, far_send, far_recv):
     me = lax.axis_index("member")
     slab = lax.axis_index("slab")
+    chips = members // 2
+    chip, core = me // 2, me % 2
+    sibling = chip * 2 + 1 - core
     mesh_kind = pl.DeviceIdType.MESH
     barrier = pltpu.get_barrier_semaphore()
-    for step in range(1, members):
-        peer = lax.rem(me + step, members)
+    pl.semaphore_signal(barrier, inc=1, device_id=(sibling, slab), device_id_type=mesh_kind)
+    for step in range(1, chips):
+        peer = lax.rem(chip + step, chips) * 2 + core
         pl.semaphore_signal(barrier, inc=1, device_id=(peer, slab), device_id_type=mesh_kind)
     cells = back_ref.shape[0]
     length = table_ref.shape[1]
-    block_rows = layer.shape[1]
+    block_rows = layer.shape[2]
     for cell in range(cells):
         lanes = pl.ds(cell * length, length)
         spectral = jnp.dot(back_ref[cell], table_ref[...], preferred_element_type=jnp.float32)
         pointwise = jnp.dot(weight_ref[...], field_ref[:, lanes], preferred_element_type=jnp.float32)
         value[:, lanes] = jax.nn.gelu(pointwise + bias_ref[...] + spectral, approximate=True)
     for block in range(members):
-        layer[block] = value[pl.ds(block * block_rows, block_rows), :].astype(layer.dtype)
-    pl.semaphore_wait(barrier, members - 1)
-
-    def copy_of(source, target, peer):
+        rows = pl.ds(block * block_rows, block_rows)
+        layer[block % 2, block // 2] = value[rows, :].astype(layer.dtype)
+    pl.semaphore_wait(barrier, chips)
+
+    on_chip = pltpu.make_async_remote_copy(
+        src_ref=layer.at[1 - core],
+        dst_ref=near,
+        send_sem=near_sems.at[0],
+        recv_sem=near_sems.at[1],
+        device_id=(sibling, slab),
+        device_id_type=mesh_kind,
+    )
+    on_chip.start()
+    on_chip.wait_recv()
+    for index in range(chips):
+        pair = layer[core, index].astype(jnp.float32) + near[index].astype(jnp.float32)
+        part[index] = pair.astype(part.dtype)
+    on_chip.wait_send()
+
+    def copy_of(source, target, peer_chip):
         return pltpu.make_async_remote_copy(
-            src_ref=layer.at[source],
-            dst_ref=landed.at[target],
-            send_sem=send_sems.at[source],
-            recv_sem=recv_sems.at[target],
-            device_id=(peer, slab),
+            src_ref=part.at[source],
+            dst_ref=far.at[target],
+            send_sem=far_send.at[source],
+            recv_sem=far_recv.at[target],
+            device_id=(peer_chip * 2 + core, slab),
             device_id_type=mesh_kind,
         )
 
-    for step in range(1, members):
-        peer = lax.rem(me + step, members)
-        copy_of(peer, me, peer).start()
-    total = layer[me].astype(jnp.float32)
-    for step in range(1, members):
-        source = lax.rem(me + members - step, members)
+    for step in range(1, chips):
+        peer = lax.rem(chip + step, chips)
+        copy_of(peer, chip, peer).start()
+    total = part[chip].astype(jnp.float32)
+    for step in range(1, chips):
+        source = lax.rem(chip + chips - step, chips)
         copy_of(source, source, source).wait_recv()
-        total = total + landed[source].astype(jnp.float32)
-    for step in range(1, members):
-        peer = lax.rem(me + step, members)
-        copy_of(peer, me, peer).wait_send()
+        total = total + far[source].astype(jnp.float32)
+    for step in range(1, chips):
+        peer = lax.rem(chip + step, chips)
+        copy_of(peer, chip, peer).wait_send()
     out_ref[...] = (total / members).astype(out_ref.dtype)
 
 
 def layer_sum(back, table, weight, field, bias, members):
     channels, width = field.shape
     block_rows = channels // members
+    chips = members // 2
     return pl.pallas_call(
         functools.partial(layer_sum_kernel, members),
         out_shape=jax.ShapeDtypeStruct((block_rows, width), jnp.bfloat16),
@@ -104,10 +125,13 @@
         out_specs=pl.BlockSpec(memory_space=pltpu.VMEM),
         scratch_shapes=[
             pltpu.VMEM((channels, width), jnp.float32),
-            pltpu.VMEM((members, block_rows, width), jnp.bfloat16),
-            pltpu.VMEM((members, block_rows, width), jnp.bfloat16),
-            pltpu.SemaphoreType.DMA((members,)),
-            pltpu.SemaphoreType.DMA((members,)),
+            pltpu.VMEM((2, chips, block_rows, width), jnp.bfloat16),
+            pltpu.VMEM((chips, block_rows, width), jnp.bfloat16),
+            pltpu.VMEM((chips, block_rows, width), jnp.bfloat16),
+            pltpu.VMEM((chips, block_rows, width), jnp.bfloat16),
+            pltpu.SemaphoreType.DMA((2,)),
+            pltpu.SemaphoreType.DMA((chips,)),
+            pltpu.SemaphoreType.DMA((chips,)),
         ],
         compiler_params=pltpu.CompilerParams(collective_id=0, has_side_effects=True),
     )(back, table, weight, field, bias)

time: 89.7 us -> 85.6 us (0.954)
  Pallas kernels: 64.5 us -> 61.3 us
    pallas_call x1, Pallas kernels: 18.2 us -> 15 us  [layer_sum(): pl.pallas_call(functools.partial(layer_sum_kernel, members), out_shape=ja...]
where the time goes in v7:
time: 85.6 us; the launch traced here: 85.1 us
  Pallas kernels  61.3 us (72%)
  local copies, waits for them, and re-layouts  11 us (13%)
  matrix products  6.04 us (7%)
  other arithmetic  5.15 us (6%)
  between operations  1.62 us (2%)
    pallas_call x2, Pallas kernels, slab_exchange(): pl.pallas_call(functools.partial(slab_exchange_kernel, parts), out_shape=...  46.3 us
    pallas_call x1, Pallas kernels, layer_sum(): pl.pallas_call(functools.partial(layer_sum_kernel, members), out_shape=ja...  15 us
    convert_element_type x1, other arithmetic, local(): field_now = (2.0 * jnp.tanh(0.5 * driven)).astype(jnp.bfloat16)  2.05 us
    unnamed x14, local copies, waits for them, and re-layouts  1.79 us

profile of v7, /device:TPU:1, one launch (start us, length us, event | category | flops | bytes accessed | tf_op | source)
XLA Modules:
  0.0 85.1 jit_solution(4513662535631774712)
XLA Ops:
  1.4 0.6 fusion.61
  2.0 0.6 broadcast_multiply_fusion
  2.7 0.7 copy.54.bias_ref
  3.4 0.5 fusion.41
  4.4 0.6 pad_maximum_fusion.2.table_ref
  5.0 2.0 %multiply_convert_fusion = bf16[32,8,2,512]{3,2,1,0:T(2,128)(2,1)S(1)} fusion(bf16[32,8,2,512]{3,2,1,0:T(2,128)(2,1)} %param.9, f32[8,2,512]{2,1,0:T(2,128)S(1)} %convert_element_type.147, f32[32]{0:T(128)S(1)} %broadcast_multiply_fusion), kind=kLoop, calls=%fused_computation.9 | loop fusion | flops 1572864 | bytes 1081472 | tf_op jit(solution)/shard_map/convert_element_type | solution.py:237
  7.1 0.9 %fusion.2 = bf16[64,8,1,32,2]{0,3,4,1,2:T(8,128)(2,1)S(1)} fusion(bf16[32,8,2,512]{3,2,1,0:T(2,128)(2,1)S(1)} %multiply_convert_fusion), kind=kOutput, calls=%fused_computation.6 | convolution fusion | flops 34111488 | bytes 589824 | tf_op jit(solution)/shard_map/cxzy,ky->kxcz/dot_general | solution.py:244
  8.0 0.9 %fusion.1 = bf16[64,8,1,32,2]{0,3,4,1,2:T(8,128)(2,1)S(1)} fusion(bf16[32,8,2,512]{3,2,1,0:T(2,128)(2,1)S(1)} %multiply_convert_fusion), kind=kOutput, calls=%fused_computation.5 | convolution fusion | flops 34078720 | bytes 589824 | tf_op jit(solution)/shard_map/cxzy,ky->kxcz/dot_general | solution.py:241
  8.9 1.2 %reshape.290.field_ref = bf16[32,8192]{1,0:T(8,128)(2,1)} reshape(bf16[32,8,2,512]{3,2,1,0:T(2,128)(2,1)S(1)} %multiply_convert_fusion) | data formatting | bytes 1048576 | tf_op jit(solution)/shard_map/reshape | solution.py:289
  10.3 0.9 %copy.39.blocks_ref = bf16[64,8,128]{2,1,0:T(8,128)(2,1)} copy(bf16[64,8,128]{0,1,2:T(8,128)(2,1)S(1)} %bitcast.93) | data formatting | bytes 262144 | tf_op jit(solution)/shard_map/convert_element_type | solution.py:249
  11.2 27.2 %shard_map.91 = bf16[64,8,128]{2,1,0:T(8,128)(2,1)} custom-call(bf16[64,8,128]{2,1,0:T(8,128)(2,1)} %copy.39.blocks_ref), custom_call_target="tpu_custom_call" | custom-call | tf_op jit(solution)/shard_map/pallas_call | solution.py:199
  38.4 1.0 %copy.40 = bf16[128,512]{1,0:T(8,128)(2,1)S(1)} copy(bf16[128,512]{0,1:T(8,128)(2,1)} %bitcast.95) | data formatting | bytes 262144 | tf_op jit(solution)/shard_map/kxf,mx->kmf/dot_general | solution.py:23
  39.4 0.6 convolution_bitcast_fusion.2
  40.1 0.7 convolution_bitcast_fusion.3
  41.2 0.8 copy.60
  42.9 0.8 copy.58
  44.7 0.7 convolution_bitcast_fusion
  45.4 0.7 convolution_bitcast_fusion.1
  46.4 0.8 convert_element_type.157.blocks_ref
  47.2 19.1 %shard_map.92 = bf16[64,8,128]{2,1,0:T(8,128)(2,1)} custom-call(bf16[64,8,128]{2,1,0:T(8,128)(2,1)} %convert_element_type.157.blocks_ref), custom_call_target="tpu_custom_call" | custom-call | tf_op jit(solution)/shard_map/pallas_call | solution.py:199
  66.3 1.2 %copy.52 = bf16[64,8,128]{0,1,2:T(8,128)(2,1)S(1)} copy(bf16[64,8,128]{2,1,0:T(8,128)(2,1)} %shard_map.92) | data formatting | bytes 262144 | tf_op jit(solution)/shard_map/pallas_call | solution.py:199
  67.8 0.8 reshape.289.back_ref
  68.6 15.0 %shard_map.93 = bf16[4,8192]{1,0:T(4,128)(2,1)} custom-call(bf16[16,32,128]{2,1,0:T(8,128)(2,1)} %reshape.289.back_ref, bf16[128,512]{1,0:T(8,128)(2,1)} %pad_maximum_fusion.2.table_ref, bf16[32,32]{1,0:T(8,128)(2,1)} %weight_ref.1, bf16[32,8192]{1,0:T(8,128)(2,1)} %reshape.290.field_ref, f32[32,1]{1,0:T(8,128)} %copy.54.bias_ref), custom_call_target="tpu_custom_call" | custom-call | tf_op jit(solution)/shard_map/pallas_call | solution.py:121
  83.6 1.6 %reshape.292 = bf16[4,8,2,512]{3,2,1,0:T(2,128)(2,1)} reshape(bf16[4,8192]{1,0:T(4,128)(2,1)} %shard_map.93) | data formatting | bytes 131072 | tf_op jit(solution)/shard_map/reshape | solution.py:292
  (40 shorter events, 3.6 us)
Async XLA Ops:
  0.7 0.7 copy-start.3
  0.7 1.3 %copy-start.4 = (f32[32]{0:T(128)S(1)}, f32[32]{0:T(128)}, u32[]{:S(2)}) copy-start(f32[32]{0:T(128)} %param.11) | copy-start | bytes 388
  0.7 2.0 %copy-start.2 = (f32[32]{0:T(128)S(1)}, f32[32]{0:T(128)}, u32[]{:S(2)}) copy-start(f32[32]{0:T(128)} %param.16) | copy-start | bytes 388
  1.4 2.0 %copy-start.1 = (bf16[8,2,512]{2,1,0:T(2,128)(2,1)S(1)}, bf16[8,2,512]{2,1,0:T(2,128)(2,1)}, u32[]{:S(2)}) copy-start(bf16[8,2,512]{2,1,0:T(2,128)(2,1)} %param.10) | copy-start | bytes 49156
  40.1 1.1 %copy-start = (bf16[1,64,2,32,32]{1,4,3,2,0:T(8,128)(2,1)S(1)}, bf16[1,64,2,32,32]{1,4,3,2,0:T(8,128)(2,1)}, u32[]{:S(2)}) copy-start(bf16[1,64,2,32,32]{1,4,3,2,0:T(8,128)(2,1)} %param.17) | copy-start | bytes 786436

commit v8 on v7

--- a/solution.py
+++ b/solution.py
@@ -140,58 +140,33 @@
 def slab_exchange_kernel(parts, blocks_ref, out_ref, landed, send_sems, recv_sems):
     me = lax.axis_index("slab")
     member = lax.axis_index("member")
+    mesh_kind = pl.DeviceIdType.MESH
     barrier = pltpu.get_barrier_semaphore()
-
-    def greet(step, carry):
+    for step in range(1, parts):
         peer = lax.rem(me + step, parts)
-        pl.semaphore_signal(barrier, inc=1, device_id=(member, peer), device_id_type=pl.DeviceIdType.MESH)
-        return carry
-
-    lax.fori_loop(1, parts, greet, 0)
+        pl.semaphore_signal(barrier, inc=1, device_id=(member, peer), device_id_type=mesh_kind)
     pl.semaphore_wait(barrier, parts - 1)
 
-    def send(step, carry):
+    def copy_of(source, target, peer):
+        return pltpu.make_async_remote_copy(
+            src_ref=blocks_ref.at[source],
+            dst_ref=landed.at[target],
+            send_sem=send_sems.at[source],
+            recv_sem=recv_sems.at[target],
+            device_id=(member, peer),
+            device_id_type=mesh_kind,
+        )
+
+    for step in range(1, parts):
         peer = lax.rem(me + step, parts)
-        pltpu.make_async_remote_copy(
-            src_ref=blocks_ref.at[peer],
-            dst_ref=landed.at[me],
-            send_sem=send_sems.at[peer],
-            recv_sem=recv_sems.at[me],
-            device_id=(member, peer),
-            device_id_type=pl.DeviceIdType.MESH,
-        ).start()
-        return carry
-
-    lax.fori_loop(1, parts, send, 0)
+        copy_of(peer, me, peer).start()
     landed[me] = blocks_ref[me]
-
-    def receive(step, carry):
+    for step in range(1, parts):
         source = lax.rem(me + parts - step, parts)
-        pltpu.make_async_remote_copy(
-            src_ref=blocks_ref.at[source],
-            dst_ref=landed.at[source],
-            send_sem=send_sems.at[source],
-            recv_sem=recv_sems.at[source],
-            device_id=(member, source),
-            device_id_type=pl.DeviceIdType.MESH,
-        ).wait_recv()
-        return carry
-
-    lax.fori_loop(1, parts, receive, 0)
-
-    def sent(step, carry):
+        copy_of(source, source, source).wait_recv()
+    for step in range(1, parts):
         peer = lax.rem(me + step, parts)
-        pltpu.make_async_remote_copy(
-            src_ref=blocks_ref.at[peer],
-            dst_ref=landed.at[me],
-            send_sem=send_sems.at[peer],
-            recv_sem=recv_sems.at[me],
-            device_id=(member, peer),
-            device_id_type=pl.DeviceIdType.MESH,
-        ).wait_send()
-        return carry
-
-    lax.fori_loop(1, parts, sent, 0)
+        copy_of(peer, me, peer).wait_send()
     out_ref[...] = landed[...]
 
 

time: 85.6 us -> 83.8 us (0.979)
  Pallas kernels: 61.3 us -> 59.6 us
    pallas_call x2, Pallas kernels: 46.3 us -> 44.7 us  [slab_exchange(): pl.pallas_call(functools.partial(slab_exchange_kernel, parts), out_shape=...]
where the time goes in v8:
time: 83.8 us; the launch traced here: 83.4 us
  Pallas kernels  59.6 us (71%)
  local copies, waits for them, and re-layouts  11 us (13%)
  matrix products  6.05 us (7%)
  other arithmetic  5.15 us (6%)
  between operations  1.62 us (2%)
    pallas_call x2, Pallas kernels, slab_exchange(): pl.pallas_call(functools.partial(slab_exchange_kernel, parts), out_shape=...  44.7 us
    pallas_call x1, Pallas kernels, layer_sum(): pl.pallas_call(functools.partial(layer_sum_kernel, members), out_shape=ja...  14.9 us
    convert_element_type x1, other arithmetic, local(): field_now = (2.0 * jnp.tanh(0.5 * driven)).astype(jnp.bfloat16)  2.05 us
    unnamed x14, local copies, waits for them, and re-layouts  1.79 us

profile of v8, /device:TPU:1, one launch (start us, length us, event | category | flops | bytes accessed | tf_op | source)
XLA Modules:
  0.0 83.4 jit_solution(18221673310845998781)
XLA Ops:
  1.4 0.6 fusion.61
  2.0 0.6 broadcast_multiply_fusion
  2.7 0.7 copy.54.bias_ref
  3.4 0.5 fusion.41
  4.4 0.6 pad_maximum_fusion.2.table_ref
  5.0 2.0 %multiply_convert_fusion = bf16[32,8,2,512]{3,2,1,0:T(2,128)(2,1)S(1)} fusion(bf16[32,8,2,512]{3,2,1,0:T(2,128)(2,1)} %param.9, f32[8,2,512]{2,1,0:T(2,128)S(1)} %convert_element_type.147, f32[32]{0:T(128)S(1)} %broadcast_multiply_fusion), kind=kLoop, calls=%fused_computation.9 | loop fusion | flops 1572864 | bytes 1081472 | tf_op jit(solution)/shard_map/convert_element_type | solution.py:212
  7.1 0.9 %fusion.2 = bf16[64,8,1,32,2]{0,3,4,1,2:T(8,128)(2,1)S(1)} fusion(bf16[32,8,2,512]{3,2,1,0:T(2,128)(2,1)S(1)} %multiply_convert_fusion), kind=kOutput, calls=%fused_computation.6 | convolution fusion | flops 34111488 | bytes 589824 | tf_op jit(solution)/shard_map/cxzy,ky->kxcz/dot_general | solution.py:219
  8.0 0.9 %fusion.1 = bf16[64,8,1,32,2]{0,3,4,1,2:T(8,128)(2,1)S(1)} fusion(bf16[32,8,2,512]{3,2,1,0:T(2,128)(2,1)S(1)} %multiply_convert_fusion), kind=kOutput, calls=%fused_computation.5 | convolution fusion | flops 34078720 | bytes 589824 | tf_op jit(solution)/shard_map/cxzy,ky->kxcz/dot_general | solution.py:216
  8.9 1.2 %reshape.290.field_ref = bf16[32,8192]{1,0:T(8,128)(2,1)} reshape(bf16[32,8,2,512]{3,2,1,0:T(2,128)(2,1)S(1)} %multiply_convert_fusion) | data formatting | bytes 1048576 | tf_op jit(solution)/shard_map/reshape | solution.py:264
  10.3 0.9 %copy.39.blocks_ref = bf16[64,8,128]{2,1,0:T(8,128)(2,1)} copy(bf16[64,8,128]{0,1,2:T(8,128)(2,1)S(1)} %bitcast.93) | data formatting | bytes 262144 | tf_op jit(solution)/shard_map/convert_element_type | solution.py:224
  11.2 26.5 %shard_map.91 = bf16[64,8,128]{2,1,0:T(8,128)(2,1)} custom-call(bf16[64,8,128]{2,1,0:T(8,128)(2,1)} %copy.39.blocks_ref), custom_call_target="tpu_custom_call" | custom-call | tf_op jit(solution)/shard_map/pallas_call | solution.py:174
  37.7 1.0 %copy.40 = bf16[128,512]{1,0:T(8,128)(2,1)S(1)} copy(bf16[128,512]{0,1:T(8,128)(2,1)} %bitcast.95) | data formatting | bytes 262144 | tf_op jit(solution)/shard_map/kxf,mx->kmf/dot_general | solution.py:23
  38.7 0.6 convolution_bitcast_fusion.2
  39.3 0.7 convolution_bitcast_fusion.3
  40.5 0.8 copy.60
  42.2 0.8 copy.58
  44.0 0.7 convolution_bitcast_fusion
  44.7 0.7 convolution_bitcast_fusion.1
  45.6 0.8 convert_element_type.157.blocks_ref
  46.4 18.3 %shard_map.92 = bf16[64,8,128]{2,1,0:T(8,128)(2,1)} custom-call(bf16[64,8,128]{2,1,0:T(8,128)(2,1)} %convert_element_type.157.blocks_ref), custom_call_target="tpu_custom_call" | custom-call | tf_op jit(solution)/shard_map/pallas_call | solution.py:174
  64.7 1.2 %copy.52 = bf16[64,8,128]{0,1,2:T(8,128)(2,1)S(1)} copy(bf16[64,8,128]{2,1,0:T(8,128)(2,1)} %shard_map.92) | data formatting | bytes 262144 | tf_op jit(solution)/shard_map/pallas_call | solution.py:174
  66.2 0.8 reshape.289.back_ref
  67.0 14.9 %shard_map.93 = bf16[4,8192]{1,0:T(4,128)(2,1)} custom-call(bf16[16,32,128]{2,1,0:T(8,128)(2,1)} %reshape.289.back_ref, bf16[128,512]{1,0:T(8,128)(2,1)} %pad_maximum_fusion.2.table_ref, bf16[32,32]{1,0:T(8,128)(2,1)} %weight_ref.1, bf16[32,8192]{1,0:T(8,128)(2,1)} %reshape.290.field_ref, f32[32,1]{1,0:T(8,128)} %copy.54.bias_ref), custom_call_target="tpu_custom_call" | custom-call | tf_op jit(solution)/shard_map/pallas_call | solution.py:121
  81.8 1.6 %reshape.292 = bf16[4,8,2,512]{3,2,1,0:T(2,128)(2,1)} reshape(bf16[4,8192]{1,0:T(4,128)(2,1)} %shard_map.93) | data formatting | bytes 131072 | tf_op jit(solution)/shard_map/reshape | solution.py:267
  (40 shorter events, 3.6 us)
Async XLA Ops:
  0.7 0.7 copy-start.3
  0.7 1.3 %copy-start.4 = (f32[32]{0:T(128)S(1)}, f32[32]{0:T(128)}, u32[]{:S(2)}) copy-start(f32[32]{0:T(128)} %param.11) | copy-start | bytes 388
  0.7 2.0 %copy-start.2 = (f32[32]{0:T(128)S(1)}, f32[32]{0:T(128)}, u32[]{:S(2)}) copy-start(f32[32]{0:T(128)} %param.16) | copy-start | bytes 388
  1.4 2.0 %copy-start.1 = (bf16[8,2,512]{2,1,0:T(2,128)(2,1)S(1)}, bf16[8,2,512]{2,1,0:T(2,128)(2,1)}, u32[]{:S(2)}) copy-start(bf16[8,2,512]{2,1,0:T(2,128)(2,1)} %param.10) | copy-start | bytes 49156
  39.3 1.1 %copy-start = (bf16[1,64,2,32,32]{1,4,3,2,0:T(8,128)(2,1)S(1)}, bf16[1,64,2,32,32]{1,4,3,2,0:T(8,128)(2,1)}, u32[]{:S(2)}) copy-start(bf16[1,64,2,32,32]{1,4,3,2,0:T(8,128)(2,1)} %param.17) | copy-start | bytes 786436

commit v9 on v8

--- a/solution.py
+++ b/solution.py
@@ -137,30 +137,34 @@
     )(back, table, weight, field, bias)
 
 
-def slab_exchange_kernel(parts, blocks_ref, out_ref, landed, send_sems, recv_sems):
+def greet_slab(parts):
     me = lax.axis_index("slab")
     member = lax.axis_index("member")
-    mesh_kind = pl.DeviceIdType.MESH
     barrier = pltpu.get_barrier_semaphore()
     for step in range(1, parts):
         peer = lax.rem(me + step, parts)
-        pl.semaphore_signal(barrier, inc=1, device_id=(member, peer), device_id_type=mesh_kind)
-    pl.semaphore_wait(barrier, parts - 1)
+        pl.semaphore_signal(barrier, inc=1, device_id=(member, peer), device_id_type=pl.DeviceIdType.MESH)
+    return barrier
+
+
+def swap_blocks(parts, source_ref, out_ref, landed, send_sems, recv_sems):
+    me = lax.axis_index("slab")
+    member = lax.axis_index("member")
 
     def copy_of(source, target, peer):
         return pltpu.make_async_remote_copy(
-            src_ref=blocks_ref.at[source],
+            src_ref=source_ref.at[source],
             dst_ref=landed.at[target],
             send_sem=send_sems.at[source],
             recv_sem=recv_sems.at[target],
             device_id=(member, peer),
-            device_id_type=mesh_kind,
+            device_id_type=pl.DeviceIdType.MESH,
         )
 
     for step in range(1, parts):
         peer = lax.rem(me + step, parts)
         copy_of(peer, me, peer).start()
-    landed[me] = blocks_ref[me]
+    landed[me] = source_ref[me]
     for step in range(1, parts):
         source = lax.rem(me + parts - step, parts)
         copy_of(source, source, source).wait_recv()
@@ -168,6 +172,55 @@
         peer = lax.rem(me + step, parts)
         copy_of(peer, me, peer).wait_send()
     out_ref[...] = landed[...]
+
+
+def slab_exchange_kernel(parts, blocks_ref, out_ref, landed, send_sems, recv_sems):
+    barrier = greet_slab(parts)
+    pl.semaphore_wait(barrier, parts - 1)
+    swap_blocks(parts, blocks_ref, out_ref, landed, send_sems, recv_sems)
+
+
+def mode_mix_kernel(parts, pencil_ref, xcos_ref, xsin_ref, xcos_t_ref, xsin_t_ref, swap_ref, weight_ref,
+                    keep_ref, out_ref, expanded, blocks, landed, send_sems, recv_sems):
+    barrier = greet_slab(parts)
+    pencil = pencil_ref[...]
+    swapped = jnp.dot(pencil, swap_ref[...], preferred_element_type=jnp.float32).astype(pencil.dtype)
+    spec = jnp.dot(xcos_ref[...], pencil, preferred_element_type=jnp.float32)
+    spec = spec + jnp.dot(xsin_ref[...], swapped, preferred_element_type=jnp.float32)
+    spec = spec.astype(pencil.dtype).astype(jnp.float32)
+    modes, width = spec.shape
+    rows = lax.broadcasted_iota(jnp.int32, spec.shape, 0)
+    for mode in range(modes):
+        lanes = pl.ds(mode * width, width)
+        expanded[:, lanes] = jnp.where(rows == mode, spec, 0.0).astype(expanded.dtype)
+    mixed = jnp.dot(expanded[...], weight_ref[...], preferred_element_type=jnp.float32)
+    mixed = (mixed * keep_ref[...]).astype(pencil.dtype)
+    mixed_swapped = jnp.dot(mixed, swap_ref[...], preferred_element_type=jnp.float32).astype(pencil.dtype)
+    back = jnp.dot(xcos_t_ref[...], mixed, preferred_element_type=jnp.float32)
+    back = back - jnp.dot(xsin_t_ref[...], mixed_swapped, preferred_element_type=jnp.float32)
+    blocks[...] = back.reshape(blocks.shape).astype(blocks.dtype)
+    pl.semaphore_wait(barrier, parts - 1)
+    swap_blocks(parts, blocks, out_ref, landed, send_sems, recv_sems)
+
+
+def mode_mix_exchange(pencil, xcos, xsin, swap, weight, keep, parts):
+    points, width = pencil.shape
+    modes = xcos.shape[0]
+    shape = (parts, points // parts, width)
+    return pl.pallas_call(
+        functools.partial(mode_mix_kernel, parts),
+        out_shape=jax.ShapeDtypeStruct(shape, pencil.dtype),
+        in_specs=[pl.BlockSpec(memory_space=pltpu.VMEM)] * 8,
+        out_specs=pl.BlockSpec(memory_space=pltpu.VMEM),
+        scratch_shapes=[
+            pltpu.VMEM((modes, modes * width), pencil.dtype),
+            pltpu.VMEM(shape, pencil.dtype),
+            pltpu.VMEM(shape, pencil.dtype),
+            pltpu.SemaphoreType.DMA((parts,)),
+            pltpu.SemaphoreType.DMA((parts,)),
+        ],
+        compiler_params=pltpu.CompilerParams(collective_id=2, has_side_effects=True),
+    )(pencil, xcos, xsin, xcos.T, xsin.T, swap, weight, keep)
 
 
 def slab_exchange(blocks, parts, exchange_id):
@@ -221,6 +274,7 @@
     )
     packed = (
         jnp.stack([y_real, y_imag], axis=2)
+        .transpose(0, 1, 4, 2, 3)
         .astype(jnp.bfloat16)
         .reshape(modes_y, slab_rows, packed_width)
     )
@@ -233,25 +287,30 @@
     full_cos, full_sin = phases(frequency_x, jnp.arange(length_x, dtype=jnp.int32), length_x)
     full_cos = full_cos.astype(jnp.bfloat16)
     full_sin = full_sin.astype(jnp.bfloat16)
-    gathered = slab_exchange(packed, slab_count, 1).reshape(length_x, packed_width)[None]
-    spectrum = forward_x(gathered, full_cos, full_sin)
-    spectrum = spectrum.astype(jnp.bfloat16).reshape(local_modes, modes_x, 2, channels, plane_count)
-    weight_real = spectral_weight[:, :, 0]
-    weight_imag = spectral_weight[:, :, 1]
-    spec_real = spectrum[:, :, 0]
-    spec_imag = spectrum[:, :, 1]
-    mix_real = mixing(weight_real, spec_real) - mixing(weight_imag, spec_imag)
-    mix_imag = mixing(weight_real, spec_imag) + mixing(weight_imag, spec_real)
-    global_modes = slab_index * local_modes + jnp.arange(local_modes, dtype=jnp.int32)
-    keep = (global_modes < mode_count[0]).astype(jnp.float32)[:, None, None, None, None]
-    mixed = (
-        (jnp.stack([mix_real, mix_imag], axis=2) * keep)
-        .astype(jnp.bfloat16)
-        .reshape(local_modes, modes_x, packed_width)
-    )
-    returned = inverse_x(mixed, full_cos, full_sin).astype(jnp.bfloat16)
-    returned = slab_exchange(returned.reshape(slab_count, slab_rows, packed_width), slab_count, 2)
-    returned = returned.reshape(modes_y, slab_rows, 2, channels, plane_count)
+    gathered = slab_exchange(packed, slab_count, 1).reshape(length_x, packed_width)
+    lane = jnp.arange(packed_width, dtype=jnp.int32)
+    real_lane = (lane // channels) % 2 == 0
+    swap = jnp.where(
+        real_lane[None, :],
+        (lane[:, None] == lane[None, :] + channels).astype(jnp.float32),
+        -(lane[:, None] == lane[None, :] - channels).astype(jnp.float32),
+    ).astype(jnp.bfloat16)
+    weight_t = spectral_weight[0].transpose(0, 1, 3, 2)
+    block = jnp.concatenate(
+        [
+            jnp.concatenate([weight_t[:, 0], weight_t[:, 1]], axis=2),
+            jnp.concatenate([-weight_t[:, 1], weight_t[:, 0]], axis=2),
+        ],
+        axis=1,
+    )
+    empty = jnp.zeros_like(block)
+    weight = jnp.concatenate(
+        [jnp.concatenate([block, empty], axis=2), jnp.concatenate([empty, block], axis=2)], axis=1
+    ).reshape(modes_x * packed_width, packed_width)
+    kept = (slab_index * local_modes < mode_count[0]).astype(jnp.float32)
+    keep = jnp.full((1, packed_width), kept, jnp.float32)
+    returned = mode_mix_exchange(gathered, full_cos, full_sin, swap, weight, keep, slab_count)
+    returned = returned.reshape(modes_y, slab_rows, plane_count, 2, channels)
     weights_y = jnp.where(jnp.arange(modes_y) == 0, 1.0, 2.0).astype(jnp.float32) / (
         length_x * length_y
     )
@@ -259,7 +318,7 @@
     back_sin = (weights_y[:, None] * y_sin).astype(jnp.bfloat16)
     table = jnp.concatenate([back_cos, -back_sin], axis=0)
     cells = slab_rows * plane_count
-    back = returned.transpose(1, 4, 3, 2, 0).reshape(cells, channels, 2 * modes_y)
+    back = returned.transpose(1, 2, 4, 3, 0).reshape(cells, channels, 2 * modes_y)
     bias = point_bias.reshape(channels, 1)
     field_rows = field_now.reshape(channels, cells * length_y)
     members = lax.axis_size("member")

time: 83.8 us -> 96.4 us (1.15)
  other arithmetic: 5.15 us -> 15.6 us
  local copies, waits for them, and re-layouts: 11 us -> 16.6 us
  matrix products: 6.05 us -> 1.81 us
  Pallas kernels: 59.6 us -> 60.6 us
    pallas_call x0 -> x1, Pallas kernels: none -> 19.3 us  [mode_mix_exchange(): pl.pallas_call(functools.partial(mode_mix_kernel, parts), out_shape=jax.S...]
    pallas_call x2 -> x1, Pallas kernels: 44.7 us -> 26.4 us  [slab_exchange(): pl.pallas_call(functools.partial(slab_exchange_kernel, parts), out_shape=...]
    concatenate x0 -> x1, local copies, waits for them, and re-layouts: none -> 8.57 us  [local(): jnp.concatenate([jnp.concatenate([block, empty], axis=2), jnp.concatenate...]
    concatenate x0 -> x2, other arithmetic: none -> 6.76 us  [the longest x1 6.47 us: local(): jnp.concatenate([jnp.concatenate([block, empty], axis=2), jnp.concatenate...]
    dot_general x8 -> x0, matrix products: 4.23 us -> none  [the longest x4 1.49 us: mixing(): jnp.einsum('kmoi,kmiz->kmoz', weights, values, preferred_element_type=jnp...]
    convert_element_type x1 -> x4, other arithmetic: 0.01 us -> 3.69 us  [the longest x2 3.01 us: local(): full_sin = full_sin.astype(jnp.bfloat16)]
    unnamed x14 -> x10, local copies, waits for them, and re-layouts: 1.79 us -> 0.02 us
    convert_element_type x3 -> x1, local copies, waits for them, and re-layouts: 1.69 us -> 0.02 us  [local(): packed = jnp.stack([y_real, y_imag], axis=2).transpose(0, 1, 4, 2, 3).ast...]
where the time goes in v9:
time: 96.4 us; the launch traced here: 96 us
  Pallas kernels  60.6 us (63%)
  local copies, waits for them, and re-layouts  16.6 us (17%)
  other arithmetic  15.6 us (16%)
  matrix products  1.81 us (2%)
  between operations  1.46 us (2%)
    pallas_call x1, Pallas kernels, slab_exchange(): pl.pallas_call(functools.partial(slab_exchange_kernel, parts), out_shape=...  26.4 us
    pallas_call x1, Pallas kernels, mode_mix_exchange(): pl.pallas_call(functools.partial(mode_mix_kernel, parts), out_shape=jax.S...  19.3 us
    pallas_call x1, Pallas kernels, layer_sum(): pl.pallas_call(functools.partial(layer_sum_kernel, members), out_shape=ja...  14.9 us
    concatenate x1, local copies, waits for them, and re-layouts, local(): jnp.concatenate([jnp.concatenate([block, empty], axis=2), jnp.concatenate...  8.57 us
    concatenate x1, other arithmetic, local(): jnp.concatenate([jnp.concatenate([block, empty], axis=2), jnp.concatenate...  6.47 us
    convert_element_type x2, other arithmetic, local(): full_sin = full_sin.astype(jnp.bfloat16)  3.01 us

profile of v9, /device:TPU:1, one launch (start us, length us, event | category | flops | bytes accessed | tf_op | source)
XLA Modules:
  0.0 96.0 jit_solution(17408669954745494942)
XLA Ops:
  0.0 1.1 %slice_bitcast_fusion = (bf16[64,32,32]{0,1,2:T(8,128)(2,1)S(1)}, bf16[64,32,32]{0,1,2:T(8,128)(2,1)S(1)}) fusion(bf16[64,2,32,32]{0,2,3,1:T(8,128)(2,1)} %bitcast.41), kind=kLoop, calls=%fused_computation.20 | loop fusion | bytes 524288 | tf_op jit(solution)/shard_map/squeeze | solution.py:301
  1.1 1.0 %fusion.47 = bf16[64,32,32]{0,1,2:T(8,128)(2,1)S(1)} fusion(bf16[64,2,32,32]{0,2,3,1:T(8,128)(2,1)} %bitcast.42), kind=kLoop, calls=%fused_computation.87 | loop fusion | flops 65536 | bytes 262144 | tf_op jit(solution)/shard_map/neg | solution.py:302
  2.4 6.5 %fusion.2 = bf16[64,128,128]{0,1,2:T(8,128)(2,1)} fusion(bf16[64,64,64]{0,1,2:T(8,128)(2,1)S(1)} %maximum_maximum_fusion), kind=kLoop, calls=%fused_computation.4 | loop fusion | flops 8388608 | bytes 2621440 | tf_op jit(solution)/shard_map/concatenate | solution.py:307
  8.8 8.6 %copy.20 = bf16[64,128,128]{2,1,0:T(8,128)(2,1)} copy(bf16[64,128,128]{0,1,2:T(8,128)(2,1)} %fusion.2) | data formatting | bytes 4194304 | tf_op jit(solution)/shard_map/concatenate | solution.py:307
  18.1 0.7 fusion.35
  18.8 0.7 broadcast_multiply_fusion
  19.5 1.0 %multiply_convert_fusion = bf16[32,8,2,512]{3,2,1,0:T(2,128)(2,1)S(1)} fusion(bf16[32,8,2,512]{3,2,1,0:T(2,128)(2,1)S(1)} %copy-done, f32[8,2,512]{2,1,0:T(2,128)S(1)} %convert_element_type.67, f32[32]{0:T(128)S(1)} %broadcast_multiply_fusion), kind=kLoop, calls=%fused_computation.11 | loop fusion | flops 1572864 | bytes 1081472 | tf_op jit(solution)/shard_map/convert_element_type | solution.py:265
  20.5 0.9 fusion.4
  21.4 0.9 fusion.5
  22.4 0.8 copy.19.blocks_ref
  23.2 26.4 %shard_map.91 = bf16[64,8,128]{2,1,0:T(8,128)(2,1)} custom-call(bf16[64,8,128]{2,1,0:T(8,128)(2,1)} %copy.19.blocks_ref), custom_call_target="tpu_custom_call" | custom-call | tf_op jit(solution)/shard_map/pallas_call | solution.py:227
  49.8 1.8 %sine_convert_fusion = (bf16[512,64]{1,0:T(8,128)(2,1)}, bf16[512,64]{1,0:T(8,128)(2,1)}) fusion(s32[64]{0:T(128)S(1)} %pad_add_fusion), kind=kLoop, calls=%fused_computation.23 | loop fusion | flops 524288 | bytes 131328 | tf_op jit(solution)/shard_map/convert_element_type | solution.py:289
  51.5 1.2 %sine_convert_fusion.1 = (bf16[64,512]{1,0:T(8,128)(2,1)}, bf16[64,512]{1,0:T(8,128)(2,1)}) fusion(s32[64]{0:T(128)S(1)} %pad_add_fusion), kind=kLoop, calls=%fused_computation.43 | loop fusion | flops 524288 | bytes 131328 | tf_op jit(solution)/shard_map/convert_element_type | solution.py:289
  52.8 0.6 select_convert_fusion.swap_ref
  54.1 0.5 broadcast_in_dim.22.keep_ref
  54.6 19.3 %shard_map.92 = bf16[64,8,128]{2,1,0:T(8,128)(2,1)} custom-call(bf16[512,128]{1,0:T(8,128)(2,1)} %bitcast.45, bf16[64,512]{1,0:T(8,128)(2,1)} %get-tuple-element.10.xcos_ref, bf16[64,512]{1,0:T(8,128)(2,1)} %get-tuple-element.9.xsin_ref, bf16[512,64]{1,0:T(8,128)(2,1)} %get-tuple-element.8.xcos_t_ref, bf16[512,64]{1,0:T(8,128)(2,1)} %get-tuple-element.7.xsin_t_ref, ...), custom_call_target="tpu_custom_call" | custom-call | tf_op jit(solution)/shard_map/pallas_call | solution.py:210
  73.9 1.1 %copy.21 = bf16[64,8,128]{0,2,1:T(8,128)(2,1)S(1)} copy(bf16[64,8,128]{2,1,0:T(8,128)(2,1)} %shard_map.92) | data formatting | bytes 262144 | tf_op jit(solution)/shard_map/pallas_call | solution.py:210
  75.2 0.8 reshape.74.back_ref
  76.0 1.2 %reshape.75.field_ref = bf16[32,8192]{1,0:T(8,128)(2,1)} reshape(bf16[32,8,2,512]{3,2,1,0:T(2,128)(2,1)S(1)} %multiply_convert_fusion) | data formatting | bytes 1048576 | tf_op jit(solution)/shard_map/reshape | solution.py:323
  77.2 0.5 fusion.26
  78.2 0.7 pad_maximum_fusion.table_ref
  78.9 0.7 copy.23.bias_ref
  79.6 14.9 %shard_map.93 = bf16[4,8192]{1,0:T(4,128)(2,1)} custom-call(bf16[16,32,128]{2,1,0:T(8,128)(2,1)} %reshape.74.back_ref, bf16[128,512]{1,0:T(8,128)(2,1)} %pad_maximum_fusion.table_ref, bf16[32,32]{1,0:T(8,128)(2,1)} %weight_ref.1, bf16[32,8192]{1,0:T(8,128)(2,1)} %reshape.75.field_ref, f32[32,1]{1,0:T(8,128)} %copy.23.bias_ref), custom_call_target="tpu_custom_call" | custom-call | tf_op jit(solution)/shard_map/pallas_call | solution.py:121
  94.5 1.6 %reshape.77 = bf16[4,8,2,512]{3,2,1,0:T(2,128)(2,1)} reshape(bf16[4,8192]{1,0:T(4,128)(2,1)} %shard_map.93) | data formatting | bytes 131072 | tf_op jit(solution)/shard_map/reshape | solution.py:326
  (22 shorter events, 1.2 us)
Async XLA Ops:
  8.8 8.6 %copy-start.1 = (bf16[8,2,512]{2,1,0:T(2,128)(2,1)S(1)}, bf16[8,2,512]{2,1,0:T(2,128)(2,1)}, u32[]{:S(2)}) copy-start(bf16[8,2,512]{2,1,0:T(2,128)(2,1)} %param.10) | copy-start | bytes 49156
  8.8 9.2 %copy-start.3 = (f32[16]{0:T(128)S(1)}, f32[16]{0:T(128)}, u32[]{:S(2)}) copy-start(f32[16]{0:T(128)} %param.12) | copy-start | bytes 196
  8.8 9.9 %copy-start.4 = (f32[32]{0:T(128)S(1)}, f32[32]{0:T(128)}, u32[]{:S(2)}) copy-start(f32[32]{0:T(128)} %param.11) | copy-start | bytes 388
  8.8 10.6 %copy-start = (bf16[32,8,2,512]{3,2,1,0:T(2,128)(2,1)S(1)}, bf16[32,8,2,512]{3,2,1,0:T(2,128)(2,1)}, u32[]{:S(2)}) copy-start(bf16[32,8,2,512]{3,2,1,0:T(2,128)(2,1)} %param.9) | copy-start | bytes 1572868
  21.4 57.5 %copy-start.2 = (f32[32]{0:T(128)S(1)}, f32[32]{0:T(128)}, u32[]{:S(2)}) copy-start(f32[32]{0:T(128)} %param.16) | copy-start | bytes 388

commit v10 on v9

--- a/solution.py
+++ b/solution.py
@@ -295,18 +295,14 @@
         (lane[:, None] == lane[None, :] + channels).astype(jnp.float32),
         -(lane[:, None] == lane[None, :] - channels).astype(jnp.float32),
     ).astype(jnp.bfloat16)
-    weight_t = spectral_weight[0].transpose(0, 1, 3, 2)
-    block = jnp.concatenate(
-        [
-            jnp.concatenate([weight_t[:, 0], weight_t[:, 1]], axis=2),
-            jnp.concatenate([-weight_t[:, 1], weight_t[:, 0]], axis=2),
-        ],
-        axis=1,
-    )
-    empty = jnp.zeros_like(block)
-    weight = jnp.concatenate(
-        [jnp.concatenate([block, empty], axis=2), jnp.concatenate([empty, block], axis=2)], axis=1
-    ).reshape(modes_x * packed_width, packed_width)
+    signs = jnp.array(
+        [[[1.0, 0.0], [0.0, 1.0]], [[0.0, 1.0], [-1.0, 0.0]]], dtype=jnp.bfloat16
+    )
+    planes = jnp.eye(plane_count, dtype=jnp.bfloat16)
+    weight = jnp.einsum(
+        "qwoi,wab,zy->qzaiybo", spectral_weight[0], signs, planes,
+        preferred_element_type=jnp.float32,
+    ).astype(jnp.bfloat16).reshape(modes_x * packed_width, packed_width)
     kept = (slab_index * local_modes < mode_count[0]).astype(jnp.float32)
     keep = jnp.full((1, packed_width), kept, jnp.float32)
     returned = mode_mix_exchange(gathered, full_cos, full_sin, swap, weight, keep, slab_count)

time: 96.4 us -> 112 us (1.16)
  local copies, waits for them, and re-layouts: 16.6 us -> 25.2 us
  other arithmetic: 15.6 us -> 20.1 us
  matrix products: 1.81 us -> 4.13 us
    reshape x0 -> x1, local copies, waits for them, and re-layouts: none -> 15.6 us  [local(): weight = jnp.einsum('qwoi,wab,zy->qzaiybo', spectral_weight[0], signs, pl...]
    convert_element_type x0 -> x1, other arithmetic: none -> 9.2 us  [local(): weight = jnp.einsum('qwoi,wab,zy->qzaiybo', spectral_weight[0], signs, pl...]
    concatenate x1 -> x0, local copies, waits for them, and re-layouts: 8.57 us -> none  [local(): jnp.concatenate([jnp.concatenate([block, empty], axis=2), jnp.concatenate...]
    concatenate x2 -> x0, other arithmetic: 6.76 us -> none  [the longest x1 6.47 us: local(): jnp.concatenate([jnp.concatenate([block, empty], axis=2), jnp.concatenate...]
    dot_general x0 -> x1, matrix products: none -> 2.32 us  [local(): jnp.einsum('qwoi,wab,zy->qzaiybo', spectral_weight[0], signs, planes, pre...]
    squeeze x1, local copies, waits for them, and re-layouts: 1.06 us -> 2.74 us  [local(): spectral_weight[0]]
where the time goes in v10:
time: 112 us; the launch traced here: 111 us
  Pallas kernels  60.6 us (54%)
  local copies, waits for them, and re-layouts  25.2 us (22%)
  other arithmetic  20.1 us (18%)
  matrix products  4.13 us (4%)
  between operations  1.44 us (1%)
    pallas_call x1, Pallas kernels, slab_exchange(): pl.pallas_call(functools.partial(slab_exchange_kernel, parts), out_shape=...  26.4 us
    pallas_call x1, Pallas kernels, mode_mix_exchange(): pl.pallas_call(functools.partial(mode_mix_kernel, parts), out_shape=jax.S...  19.3 us
    reshape x1, local copies, waits for them, and re-layouts, local(): weight = jnp.einsum('qwoi,wab,zy->qzaiybo', spectral_weight[0], signs, pl...  15.6 us
    pallas_call x1, Pallas kernels, layer_sum(): pl.pallas_call(functools.partial(layer_sum_kernel, members), out_shape=ja...  14.9 us
    convert_element_type x1, other arithmetic, local(): weight = jnp.einsum('qwoi,wab,zy->qzaiybo', spectral_weight[0], signs, pl...  9.2 us
    convert_element_type x2, other arithmetic, local(): full_sin = full_sin.astype(jnp.bfloat16)  3.13 us
    squeeze x1, local copies, waits for them, and re-layouts, local(): spectral_weight[0]  2.74 us
    dot_general x1, matrix products, local(): jnp.einsum('qwoi,wab,zy->qzaiybo', spectral_weight[0], signs, planes, pre...  2.32 us

profile of v10, /device:TPU:1, one launch (start us, length us, event | category | flops | bytes accessed | tf_op | source)
XLA Modules:
  0.0 111.5 jit_solution(5177906063409903821)
XLA Ops:
  0.0 0.7 convert_element_type.74
  1.4 1.3 %fusion.33 = f32[]{:T(128)} fusion(f32[16]{0:T(128)} %param.13, s32[]{:T(128)} %bitcast.38), kind=kLoop, calls=%fused_computation.65 | loop fusion | flops 47 | bytes 72 | tf_op jit(solution)/shard_map/reduce_sum | solution.py:261
  2.7 1.3 %broadcast_multiply_fusion = f32[32]{0:T(128)S(1)} fusion(f32[32]{0:T(128)} %param.12, f32[]{:T(128)} %fusion.33), kind=kLoop, calls=%fused_computation.73 | loop fusion | flops 32 | bytes 260 | tf_op jit(solution)/shard_map/mul | solution.py:262
  4.0 2.0 %multiply_convert_fusion.1 = bf16[32,8,2,512]{3,2,1,0:T(2,128)(2,1)S(1)} fusion(bf16[32,8,2,512]{3,2,1,0:T(2,128)(2,1)} %param.10, f32[8,2,512]{2,1,0:T(2,128)S(1)} %convert_element_type.74, f32[32]{0:T(128)S(1)} %broadcast_multiply_fusion), kind=kLoop, calls=%fused_computation.7 | loop fusion | flops 1572864 | bytes 1081472 | tf_op jit(solution)/shard_map/convert_element_type | solution.py:265
  6.0 0.9 fusion.2
  6.9 0.9 fusion.3
  7.9 0.8 copy.21.blocks_ref
  8.7 26.4 %shard_map.100 = bf16[64,8,128]{2,1,0:T(8,128)(2,1)} custom-call(bf16[64,8,128]{2,1,0:T(8,128)(2,1)} %copy.21.blocks_ref), custom_call_target="tpu_custom_call" | custom-call | tf_op jit(solution)/shard_map/pallas_call | solution.py:227
  35.3 1.9 %sine_convert_fusion = (bf16[512,64]{1,0:T(8,128)(2,1)}, bf16[512,64]{1,0:T(8,128)(2,1)}) fusion(s32[64]{0:T(128)S(1)} %pad_add_fusion), kind=kLoop, calls=%fused_computation.17 | loop fusion | flops 524288 | bytes 131328 | tf_op jit(solution)/shard_map/convert_element_type | solution.py:289
  37.2 1.2 %sine_convert_fusion.1 = (bf16[64,512]{1,0:T(8,128)(2,1)}, bf16[64,512]{1,0:T(8,128)(2,1)}) fusion(s32[64]{0:T(128)S(1)} %pad_add_fusion), kind=kLoop, calls=%fused_computation.37 | loop fusion | flops 524288 | bytes 131328 | tf_op jit(solution)/shard_map/convert_element_type | solution.py:289
  38.4 0.6 select_convert_fusion.swap_ref
  39.0 2.7 %copy.30 = bf16[64,2,32,32,1]{2,1,3,4,0:T(2,128)(2,1)S(1)} copy(bf16[64,2,32,32,1]{0,3,2,1,4:T(8,128)(2,1)} %bitcast.42) | data formatting | bytes 524288 | tf_op jit(solution)/shard_map/squeeze | solution.py:303
  41.8 2.3 %fusion.45 = f32[2,2,64,32,32]{3,1,4,0,2:T(2,128)S(1)} fusion(bf16[2,2,2,1,1]{0,2,4,1,3:T(2,128)(2,1)} %constant.86, bf16[64,2,32,32,1]{2,1,3,4,0:T(2,128)(2,1)S(1)} %copy.30), kind=kOutput, calls=%fused_computation.82 | convolution fusion | flops 1048576 | bytes 1310736 | tf_op jit(solution)/shard_map/qwoi,wab,zy->qzaiybo/dot_general | solution.py:302
  44.1 9.2 %fusion = bf16[64,2,2,32,2,2,32]{6,5,4,3,2,1,0:T(2,128)(2,1)} fusion(f32[2,2]{1,0:T(2,128)S(1)} %compare_convert_fusion, f32[2,2,64,32,32]{3,1,4,0,2:T(2,128)S(1)} %fusion.45), kind=kLoop, calls=%fused_computation.1 | loop fusion | flops 2097152 | bytes 3145744 | tf_op jit(solution)/shard_map/convert_element_type | solution.py:305
  53.3 15.6 %reshape.72.weight_ref = bf16[8192,128]{1,0:T(8,128)(2,1)} reshape(bf16[64,2,2,32,2,2,32]{6,5,4,3,2,1,0:T(2,128)(2,1)} %fusion) | data formatting | bytes 4194304 | tf_op jit(solution)/shard_map/reshape | solution.py:305
  69.5 0.6 broadcast_in_dim.24.keep_ref
  70.1 19.3 %shard_map.101 = bf16[64,8,128]{2,1,0:T(8,128)(2,1)} custom-call(bf16[512,128]{1,0:T(8,128)(2,1)} %bitcast.43, bf16[64,512]{1,0:T(8,128)(2,1)} %get-tuple-element.8.xcos_ref, bf16[64,512]{1,0:T(8,128)(2,1)} %get-tuple-element.7.xsin_ref, bf16[512,64]{1,0:T(8,128)(2,1)} %get-tuple-element.6.xcos_t_ref, bf16[512,64]{1,0:T(8,128)(2,1)} %get-tuple-element.5.xsin_t_ref, ...), custom_call_target="tpu_custom_call" | custom-call | tf_op jit(solution)/shard_map/pallas_call | solution.py:210
  89.4 1.1 copy.24
  90.7 0.8 reshape.74.back_ref
  91.5 1.2 %reshape.75.field_ref = bf16[32,8192]{1,0:T(8,128)(2,1)} reshape(bf16[32,8,2,512]{3,2,1,0:T(2,128)(2,1)S(1)} %multiply_convert_fusion.1) | data formatting | bytes 1048576 | tf_op jit(solution)/shard_map/reshape | solution.py:319
  93.7 0.7 pad_maximum_fusion.table_ref
  94.4 0.7 copy.26.bias_ref
  95.1 14.9 %shard_map.102 = bf16[4,8192]{1,0:T(4,128)(2,1)} custom-call(bf16[16,32,128]{2,1,0:T(8,128)(2,1)} %reshape.74.back_ref, bf16[128,512]{1,0:T(8,128)(2,1)} %pad_maximum_fusion.table_ref, bf16[32,32]{1,0:T(8,128)(2,1)} %weight_ref.1, bf16[32,8192]{1,0:T(8,128)(2,1)} %reshape.75.field_ref, f32[32,1]{1,0:T(8,128)} %copy.26.bias_ref), custom_call_target="tpu_custom_call" | custom-call | tf_op jit(solution)/shard_map/pallas_call | solution.py:121
  109.9 1.6 %reshape.77 = bf16[4,8,2,512]{3,2,1,0:T(2,128)(2,1)} reshape(bf16[4,8192]{1,0:T(4,128)(2,1)} %shard_map.102) | data formatting | bytes 131072 | tf_op jit(solution)/shard_map/reshape | solution.py:322
  (14 shorter events, 1.4 us)
Async XLA Ops:
  53.3 41.0 %copy-start = (f32[32]{0:T(128)S(1)}, f32[32]{0:T(128)}, u32[]{:S(2)}) copy-start(f32[32]{0:T(128)} %param.17) | copy-start | bytes 388

commit v11 on v10

--- a/solution.py
+++ b/solution.py
@@ -180,24 +180,37 @@
     swap_blocks(parts, blocks_ref, out_ref, landed, send_sems, recv_sems)
 
 
-def mode_mix_kernel(parts, pencil_ref, xcos_ref, xsin_ref, xcos_t_ref, xsin_t_ref, swap_ref, weight_ref,
-                    keep_ref, out_ref, expanded, blocks, landed, send_sems, recv_sems):
+def mode_mix_kernel(parts, pencil_t_ref, xcos_t_ref, xsin_t_ref, swap_t_ref, weight_ref, keep_ref, out_ref,
+                    mixed_t, blocks, landed, send_sems, recv_sems):
     barrier = greet_slab(parts)
-    pencil = pencil_ref[...]
-    swapped = jnp.dot(pencil, swap_ref[...], preferred_element_type=jnp.float32).astype(pencil.dtype)
-    spec = jnp.dot(xcos_ref[...], pencil, preferred_element_type=jnp.float32)
-    spec = spec + jnp.dot(xsin_ref[...], swapped, preferred_element_type=jnp.float32)
-    spec = spec.astype(pencil.dtype).astype(jnp.float32)
-    modes, width = spec.shape
-    rows = lax.broadcasted_iota(jnp.int32, spec.shape, 0)
-    for mode in range(modes):
-        lanes = pl.ds(mode * width, width)
-        expanded[:, lanes] = jnp.where(rows == mode, spec, 0.0).astype(expanded.dtype)
-    mixed = jnp.dot(expanded[...], weight_ref[...], preferred_element_type=jnp.float32)
-    mixed = (mixed * keep_ref[...]).astype(pencil.dtype)
-    mixed_swapped = jnp.dot(mixed, swap_ref[...], preferred_element_type=jnp.float32).astype(pencil.dtype)
-    back = jnp.dot(xcos_t_ref[...], mixed, preferred_element_type=jnp.float32)
-    back = back - jnp.dot(xsin_t_ref[...], mixed_swapped, preferred_element_type=jnp.float32)
+    pencil_t = pencil_t_ref[...]
+    swap_t = swap_t_ref[...]
+    swapped_t = jnp.dot(swap_t, pencil_t, preferred_element_type=jnp.float32).astype(pencil_t.dtype)
+    spec_t = jnp.dot(pencil_t, xcos_t_ref[...], preferred_element_type=jnp.float32)
+    spec_t = spec_t + jnp.dot(swapped_t, xsin_t_ref[...], preferred_element_type=jnp.float32)
+    spec_t = spec_t.astype(pencil_t.dtype).astype(jnp.float32)
+    outputs = weight_ref.shape[1]
+    planes = spec_t.shape[0] // (2 * outputs)
+    for plane in range(planes):
+        base = plane * 2 * outputs
+        real = spec_t[base:base + outputs, :]
+        imag = spec_t[base + outputs:base + 2 * outputs, :]
+        for out in range(outputs):
+            weight_real = weight_ref[0, out].astype(jnp.float32)
+            weight_imag = weight_ref[1, out].astype(jnp.float32)
+            mixed_t[pl.ds(base + out, 1), :] = jnp.sum(
+                weight_real * real - weight_imag * imag, axis=0, keepdims=True
+            )
+            mixed_t[pl.ds(base + outputs + out, 1), :] = jnp.sum(
+                weight_imag * real + weight_real * imag, axis=0, keepdims=True
+            )
+    mixed = (mixed_t[...] * keep_ref[...]).astype(pencil_t.dtype)
+    mixed_swapped = jnp.dot(swap_t, mixed, preferred_element_type=jnp.float32).astype(pencil_t.dtype)
+    contract = (((1,), (1,)), ((), ()))
+    back = lax.dot_general(xcos_t_ref[...], mixed, contract, preferred_element_type=jnp.float32)
+    back = back - lax.dot_general(
+        xsin_t_ref[...], mixed_swapped, contract, preferred_element_type=jnp.float32
+    )
     blocks[...] = back.reshape(blocks.shape).astype(blocks.dtype)
     pl.semaphore_wait(barrier, parts - 1)
     swap_blocks(parts, blocks, out_ref, landed, send_sems, recv_sems)
@@ -210,17 +223,17 @@
     return pl.pallas_call(
         functools.partial(mode_mix_kernel, parts),
         out_shape=jax.ShapeDtypeStruct(shape, pencil.dtype),
-        in_specs=[pl.BlockSpec(memory_space=pltpu.VMEM)] * 8,
+        in_specs=[pl.BlockSpec(memory_space=pltpu.VMEM)] * 6,
         out_specs=pl.BlockSpec(memory_space=pltpu.VMEM),
         scratch_shapes=[
-            pltpu.VMEM((modes, modes * width), pencil.dtype),
+            pltpu.VMEM((width, modes), jnp.float32),
             pltpu.VMEM(shape, pencil.dtype),
             pltpu.VMEM(shape, pencil.dtype),
             pltpu.SemaphoreType.DMA((parts,)),
             pltpu.SemaphoreType.DMA((parts,)),
         ],
         compiler_params=pltpu.CompilerParams(collective_id=2, has_side_effects=True),
-    )(pencil, xcos, xsin, xcos.T, xsin.T, swap, weight, keep)
+    )(pencil.T, xcos.T, xsin.T, swap.T, weight, keep)
 
 
 def slab_exchange(blocks, parts, exchange_id):
@@ -295,16 +308,9 @@
         (lane[:, None] == lane[None, :] + channels).astype(jnp.float32),
         -(lane[:, None] == lane[None, :] - channels).astype(jnp.float32),
     ).astype(jnp.bfloat16)
-    signs = jnp.array(
-        [[[1.0, 0.0], [0.0, 1.0]], [[0.0, 1.0], [-1.0, 0.0]]], dtype=jnp.bfloat16
-    )
-    planes = jnp.eye(plane_count, dtype=jnp.bfloat16)
-    weight = jnp.einsum(
-        "qwoi,wab,zy->qzaiybo", spectral_weight[0], signs, planes,
-        preferred_element_type=jnp.float32,
-    ).astype(jnp.bfloat16).reshape(modes_x * packed_width, packed_width)
+    weight = spectral_weight[0].transpose(1, 2, 3, 0)
     kept = (slab_index * local_modes < mode_count[0]).astype(jnp.float32)
-    keep = jnp.full((1, packed_width), kept, jnp.float32)
+    keep = jnp.full((1, modes_x), kept, jnp.float32)
     returned = mode_mix_exchange(gathered, full_cos, full_sin, swap, weight, keep, slab_count)
     returned = returned.reshape(modes_y, slab_rows, plane_count, 2, channels)
     weights_y = jnp.where(jnp.arange(modes_y) == 0, 1.0, 2.0).astype(jnp.float32) / (

time: 112 us -> 81.9 us (0.73)
  local copies, waits for them, and re-layouts: 25.2 us -> 9.9 us
  other arithmetic: 20.1 us -> 8.38 us
  matrix products: 4.13 us -> 1.82 us
    reshape x1, local copies, waits for them, and re-layouts: 15.6 us -> 1.66 us  [local(): slab_exchange(packed, slab_count, 1).reshape(length_x, packed_width)]
    convert_element_type x1 -> x0, other arithmetic: 9.2 us -> none  [local(): weight = jnp.einsum('qwoi,wab,zy->qzaiybo', spectral_weight[0], signs, pl...]
    squeeze x1 -> x0, local copies, waits for them, and re-layouts: 2.74 us -> none  [local(): spectral_weight[0]]
    dot_general x1 -> x0, matrix products: 2.32 us -> none  [local(): jnp.einsum('qwoi,wab,zy->qzaiybo', spectral_weight[0], signs, planes, pre...]
    convert_element_type x2 -> x1, other arithmetic: 3.13 us -> 1.75 us  [local(): full_sin = full_sin.astype(jnp.bfloat16)]
    unnamed x2 -> x6, local copies, waits for them, and re-layouts: 0.01 us -> 1.31 us
where the time goes in v11:
time: 81.9 us; the launch traced here: 81.5 us
  Pallas kernels  60 us (73%)
  local copies, waits for them, and re-layouts  9.9 us (12%)
  other arithmetic  8.38 us (10%)
  matrix products  1.82 us (2%)
  between operations  1.42 us (2%)
    pallas_call x1, Pallas kernels, slab_exchange(): pl.pallas_call(functools.partial(slab_exchange_kernel, parts), out_shape=...  26.4 us
    pallas_call x1, Pallas kernels, mode_mix_exchange(): pl.pallas_call(functools.partial(mode_mix_kernel, parts), out_shape=jax.S...  18.6 us
    pallas_call x1, Pallas kernels, layer_sum(): pl.pallas_call(functools.partial(layer_sum_kernel, members), out_shape=ja...  14.9 us
    convert_element_type x1, other arithmetic, local(): field_now = (2.0 * jnp.tanh(0.5 * driven)).astype(jnp.bfloat16)  2.05 us
    convert_element_type x1, other arithmetic, local(): full_sin = full_sin.astype(jnp.bfloat16)  1.75 us
    reshape x1, local copies, waits for them, and re-layouts, local(): slab_exchange(packed, slab_count, 1).reshape(length_x, packed_width)  1.66 us

profile of v11, /device:TPU:1, one launch (start us, length us, event | category | flops | bytes accessed | tf_op | source)
XLA Modules:
  0.0 81.5 jit_solution(4514614808385943421)
XLA Ops:
  0.0 0.7 convert_element_type.66
  1.4 0.6 copy-done.1
  2.0 0.7 fusion.26
  2.7 0.6 broadcast_multiply_fusion
  3.3 2.1 %multiply_convert_fusion = bf16[32,8,2,512]{3,2,1,0:T(2,128)(2,1)S(1)} fusion(bf16[32,8,2,512]{3,2,1,0:T(2,128)(2,1)} %param.9, f32[8,2,512]{2,1,0:T(2,128)S(1)} %convert_element_type.66, f32[32]{0:T(128)S(1)} %broadcast_multiply_fusion), kind=kLoop, calls=%fused_computation.5 | loop fusion | flops 1572864 | bytes 1081472 | tf_op jit(solution)/shard_map/convert_element_type | solution.py:278
  5.4 0.9 %fusion.1 = bf16[64,8,1,32,2]{0,3,4,1,2:T(8,128)(2,1)S(1)} fusion(bf16[32,8,2,512]{3,2,1,0:T(2,128)(2,1)S(1)} %multiply_convert_fusion), kind=kOutput, calls=%fused_computation.3 | convolution fusion | flops 34078720 | bytes 589824 | tf_op jit(solution)/shard_map/cxzy,ky->kxcz/dot_general | solution.py:282
  6.3 0.9 %fusion.2 = bf16[64,8,1,32,2]{0,3,4,1,2:T(8,128)(2,1)S(1)} fusion(bf16[32,8,2,512]{3,2,1,0:T(2,128)(2,1)S(1)} %multiply_convert_fusion), kind=kOutput, calls=%fused_computation.4 | convolution fusion | flops 34111488 | bytes 589824 | tf_op jit(solution)/shard_map/cxzy,ky->kxcz/dot_general | solution.py:285
  7.3 0.8 copy.19.blocks_ref
  8.1 26.4 %shard_map.91 = bf16[64,8,128]{2,1,0:T(8,128)(2,1)} custom-call(bf16[64,8,128]{2,1,0:T(8,128)(2,1)} %copy.19.blocks_ref), custom_call_target="tpu_custom_call" | custom-call | tf_op jit(solution)/shard_map/pallas_call | solution.py:240
  34.6 1.7 %copy.20 = bf16[512,128]{0,1:T(8,128)(2,1)} copy(bf16[512,128]{1,0:T(8,128)(2,1)} %bitcast.36) | data formatting | bytes 262144 | tf_op jit(solution)/shard_map/reshape | solution.py:303
  36.2 0.7 select_convert_fusion.swap_t_ref
  37.1 1.7 %sine_convert_fusion = (bf16[512,64]{1,0:T(8,128)(2,1)}, bf16[512,64]{1,0:T(8,128)(2,1)}) fusion(s32[64]{0:T(128)S(1)} %pad_add_fusion), kind=kLoop, calls=%fused_computation.15 | loop fusion | flops 524288 | bytes 131328 | tf_op jit(solution)/shard_map/convert_element_type | solution.py:302
  39.5 0.5 broadcast_in_dim.24.keep_ref
  40.0 18.6 %shard_map.92 = bf16[64,8,128]{2,1,0:T(8,128)(2,1)} custom-call(bf16[128,512]{1,0:T(8,128)(2,1)} %bitcast.38, bf16[512,64]{1,0:T(8,128)(2,1)} %get-tuple-element.6.xcos_t_ref, bf16[512,64]{1,0:T(8,128)(2,1)} %get-tuple-element.5.xsin_t_ref, bf16[128,128]{1,0:T(8,128)(2,1)} %select_convert_fusion.swap_t_ref, bf16[2,32,32,64]{3,2,1,0:T(8,128)(2,1)} %bitcast.37, ...), custom_call_target="tpu_custom_call" | custom-call | tf_op jit(solution)/shard_map/pallas_call | solution.py:223
  58.7 1.1 %copy.21 = bf16[64,8,128]{0,2,1:T(8,128)(2,1)S(1)} copy(bf16[64,8,128]{2,1,0:T(8,128)(2,1)} %shard_map.92) | data formatting | bytes 262144 | tf_op jit(solution)/shard_map/pallas_call | solution.py:223
  60.0 0.8 reshape.70.back_ref
  60.8 1.2 %reshape.71.field_ref = bf16[32,8192]{1,0:T(8,128)(2,1)} reshape(bf16[32,8,2,512]{3,2,1,0:T(2,128)(2,1)S(1)} %multiply_convert_fusion) | data formatting | bytes 1048576 | tf_op jit(solution)/shard_map/reshape | solution.py:325
  62.0 0.5 fusion.17
  62.5 0.5 multiply_convert_fusion.2
  63.0 0.7 pad_maximum_fusion.table_ref
  63.7 0.7 copy-done
  64.3 0.7 copy.23.bias_ref
  65.0 14.9 %shard_map.93 = bf16[4,8192]{1,0:T(4,128)(2,1)} custom-call(bf16[16,32,128]{2,1,0:T(8,128)(2,1)} %reshape.70.back_ref, bf16[128,512]{1,0:T(8,128)(2,1)} %pad_maximum_fusion.table_ref, bf16[32,32]{1,0:T(8,128)(2,1)} %weight_ref.1, bf16[32,8192]{1,0:T(8,128)(2,1)} %reshape.71.field_ref, f32[32,1]{1,0:T(8,128)} %copy.23.bias_ref), custom_call_target="tpu_custom_call" | custom-call | tf_op jit(solution)/shard_map/pallas_call | solution.py:121
  79.9 1.6 %reshape.73 = bf16[4,8,2,512]{3,2,1,0:T(2,128)(2,1)} reshape(bf16[4,8192]{1,0:T(4,128)(2,1)} %shard_map.93) | data formatting | bytes 131072 | tf_op jit(solution)/shard_map/reshape | solution.py:328
  (13 shorter events, 0.4 us)
Async XLA Ops:
  1.4 0.7 copy-start.1
  2.0 0.7 copy-start.2
  63.7 0.7 copy-start

commit v12 on v11

--- a/solution.py
+++ b/solution.py
@@ -2,6 +2,8 @@
 import math
 
 import jax
+import ml_dtypes
+import numpy as np
 import jax.numpy as jnp
 from jax import lax
 from jax.experimental import pallas as pl
@@ -9,6 +11,16 @@
 from jax.sharding import PartitionSpec as P
 
 TWO_PI = 2.0 * math.pi
+
+
+def phase_tables(frequency, positions, length):
+    product = np.outer(frequency, positions) % length
+    angles = (product.astype(np.float32) * np.float32(TWO_PI / length)).astype(np.float64)
+    return np.cos(angles).astype(np.float32), np.sin(angles).astype(np.float32)
+
+
+def bf16_constant(values):
+    return jnp.asarray(np.asarray(values, np.float32).astype(ml_dtypes.bfloat16))
 
 
 def phases(frequency, positions, length):
@@ -216,9 +228,9 @@
     swap_blocks(parts, blocks, out_ref, landed, send_sems, recv_sems)
 
 
-def mode_mix_exchange(pencil, xcos, xsin, swap, weight, keep, parts):
+def mode_mix_exchange(pencil, xcos_t, xsin_t, swap_t, weight, keep, parts):
     points, width = pencil.shape
-    modes = xcos.shape[0]
+    modes = xcos_t.shape[1]
     shape = (parts, points // parts, width)
     return pl.pallas_call(
         functools.partial(mode_mix_kernel, parts),
@@ -233,7 +245,7 @@
             pltpu.SemaphoreType.DMA((parts,)),
         ],
         compiler_params=pltpu.CompilerParams(collective_id=2, has_side_effects=True),
-    )(pencil.T, xcos.T, xsin.T, swap.T, weight, keep)
+    )(pencil.T, xcos_t, xsin_t, swap_t, weight, keep)
 
 
 def slab_exchange(blocks, parts, exchange_id):
@@ -276,14 +288,12 @@
         None
     ].astype(jnp.float32)
     field_now = (2.0 * jnp.tanh(0.5 * driven)).astype(jnp.bfloat16)
-    y_cos, y_sin = phases(
-        jnp.arange(modes_y, dtype=jnp.int32), jnp.arange(length_y, dtype=jnp.int32), length_y
-    )
+    y_cos, y_sin = phase_tables(np.arange(modes_y), np.arange(length_y), length_y)
     y_real = jnp.einsum(
-        "cxzy,ky->kxcz", field_now, y_cos.astype(jnp.bfloat16), preferred_element_type=jnp.float32
+        "cxzy,ky->kxcz", field_now, bf16_constant(y_cos), preferred_element_type=jnp.float32
     )
     y_imag = -jnp.einsum(
-        "cxzy,ky->kxcz", field_now, y_sin.astype(jnp.bfloat16), preferred_element_type=jnp.float32
+        "cxzy,ky->kxcz", field_now, bf16_constant(y_sin), preferred_element_type=jnp.float32
     )
     packed = (
         jnp.stack([y_real, y_imag], axis=2)
@@ -291,34 +301,32 @@
         .astype(jnp.bfloat16)
         .reshape(modes_y, slab_rows, packed_width)
     )
-    frequency_x = jnp.concatenate(
-        [
-            jnp.arange(modes_x // 2, dtype=jnp.int32),
-            jnp.arange(length_x - modes_x // 2, length_x, dtype=jnp.int32),
-        ]
-    )
-    full_cos, full_sin = phases(frequency_x, jnp.arange(length_x, dtype=jnp.int32), length_x)
-    full_cos = full_cos.astype(jnp.bfloat16)
-    full_sin = full_sin.astype(jnp.bfloat16)
+    frequency_x = np.concatenate(
+        [np.arange(modes_x // 2), np.arange(length_x - modes_x // 2, length_x)]
+    )
+    full_cos, full_sin = phase_tables(frequency_x, np.arange(length_x), length_x)
     gathered = slab_exchange(packed, slab_count, 1).reshape(length_x, packed_width)
-    lane = jnp.arange(packed_width, dtype=jnp.int32)
+    lane = np.arange(packed_width)
     real_lane = (lane // channels) % 2 == 0
-    swap = jnp.where(
+    swap = np.where(
         real_lane[None, :],
-        (lane[:, None] == lane[None, :] + channels).astype(jnp.float32),
-        -(lane[:, None] == lane[None, :] - channels).astype(jnp.float32),
-    ).astype(jnp.bfloat16)
+        (lane[:, None] == lane[None, :] + channels).astype(np.float32),
+        -(lane[:, None] == lane[None, :] - channels).astype(np.float32),
+    )
     weight = spectral_weight[0].transpose(1, 2, 3, 0)
     kept = (slab_index * local_modes < mode_count[0]).astype(jnp.float32)
     keep = jnp.full((1, modes_x), kept, jnp.float32)
-    returned = mode_mix_exchange(gathered, full_cos, full_sin, swap, weight, keep, slab_count)
+    returned = mode_mix_exchange(
+        gathered, bf16_constant(full_cos.T), bf16_constant(full_sin.T), bf16_constant(swap.T), weight,
+        keep, slab_count,
+    )
     returned = returned.reshape(modes_y, slab_rows, plane_count, 2, channels)
-    weights_y = jnp.where(jnp.arange(modes_y) == 0, 1.0, 2.0).astype(jnp.float32) / (
+    weights_y = np.where(np.arange(modes_y) == 0, 1.0, 2.0).astype(np.float32) / np.float32(
         length_x * length_y
     )
-    back_cos = (weights_y[:, None] * y_cos).astype(jnp.bfloat16)
-    back_sin = (weights_y[:, None] * y_sin).astype(jnp.bfloat16)
-    table = jnp.concatenate([back_cos, -back_sin], axis=0)
+    table = bf16_constant(
+        np.concatenate([weights_y[:, None] * y_cos, -(weights_y[:, None] * y_sin)], axis=0)
+    )
     cells = slab_rows * plane_count
     back = returned.transpose(1, 2, 4, 3, 0).reshape(cells, channels, 2 * modes_y)
     bias = point_bias.reshape(channels, 1)

time: 81.9 us -> 77 us (0.940)
  other arithmetic: 8.38 us -> 4.16 us
  matrix products: 1.82 us -> 0.56 us
    convert_element_type x3 -> x0, other arithmetic: 2.98 us -> none  [the longest x1 1.75 us: local(): full_sin = full_sin.astype(jnp.bfloat16)]
    dot_general x2, matrix products: 1.82 us -> 0.56 us  [the longest x1 0.28 us: local(): jnp.einsum('cxzy,ky->kxcz', field_now, bf16_constant(y_cos), preferred_el...]
    unnamed x6 -> x10, local copies, waits for them, and re-layouts: 1.31 us -> 1.87 us
where the time goes in v12:
time: 77 us; the launch traced here: 76.6 us
  Pallas kernels  60 us (78%)
  local copies, waits for them, and re-layouts  10.5 us (14%)
  other arithmetic  4.16 us (5%)
  between operations  1.42 us (2%)
    pallas_call x1, Pallas kernels, slab_exchange(): pl.pallas_call(functools.partial(slab_exchange_kernel, parts), out_shape=...  26.4 us
    pallas_call x1, Pallas kernels, mode_mix_exchange(): pl.pallas_call(functools.partial(mode_mix_kernel, parts), out_shape=jax.S...  18.6 us
    pallas_call x1, Pallas kernels, layer_sum(): pl.pallas_call(functools.partial(layer_sum_kernel, members), out_shape=ja...  14.9 us
    convert_element_type x1, other arithmetic, local(): field_now = (2.0 * jnp.tanh(0.5 * driven)).astype(jnp.bfloat16)  2.08 us
    unnamed x10, local copies, waits for them, and re-layouts  1.87 us
    reshape x1, local copies, waits for them, and re-layouts, local(): slab_exchange(packed, slab_count, 1).reshape(length_x, packed_width)  1.65 us
    reshape x1, local copies, waits for them, and re-layouts, local(): return total.reshape(channels // members, slab_rows, plane_count, length_y)  1.56 us

profile of v12, /device:TPU:1, one launch (start us, length us, event | category | flops | bytes accessed | tf_op | source)
XLA Modules:
  0.0 76.6 jit_solution(1424251717648418533)
XLA Ops:
  0.0 0.7 convert_element_type.18
  1.4 0.6 copy-done.2
  2.0 0.7 fusion.5
  2.7 0.6 broadcast_multiply_fusion
  3.3 0.0 copy-start
  3.4 2.1 %multiply_convert_fusion = bf16[32,8,2,512]{3,2,1,0:T(2,128)(2,1)S(1)} fusion(bf16[32,8,2,512]{3,2,1,0:T(2,128)(2,1)} %param.15, f32[8,2,512]{2,1,0:T(2,128)S(1)} %convert_element_type.18, f32[32]{0:T(128)S(1)} %broadcast_multiply_fusion), kind=kLoop, calls=%fused_computation.5 | loop fusion | flops 1572864 | bytes 1081472 | tf_op jit(solution)/shard_map/convert_element_type | solution.py:290
  5.5 0.3 fusion.1
  5.8 0.5 copy-done.4
  6.3 0.3 fusion.2
  6.6 0.1 maximum_bitcast_fusion
  6.7 0.1 copy.24
  6.7 0.8 %copy.25.blocks_ref = bf16[64,8,128]{2,1,0:T(8,128)(2,1)} copy(bf16[64,8,128]{0,2,1:T(8,128)(2,1)S(1)} %bitcast.32) | data formatting | bytes 262144 | tf_op jit(solution)/shard_map/reshape | solution.py:302
  7.5 26.4 %shard_map.145 = bf16[64,8,128]{2,1,0:T(8,128)(2,1)} custom-call(bf16[64,8,128]{2,1,0:T(8,128)(2,1)} %copy.25.blocks_ref), custom_call_target="tpu_custom_call" | custom-call | tf_op jit(solution)/shard_map/pallas_call | solution.py:252
  34.0 1.7 %copy.26 = bf16[512,128]{0,1:T(8,128)(2,1)} copy(bf16[512,128]{1,0:T(8,128)(2,1)} %bitcast.34) | data formatting | bytes 262144 | tf_op jit(solution)/shard_map/reshape | solution.py:308
  36.3 0.5 broadcast_in_dim.10.keep_ref
  36.8 18.6 %shard_map.146 = bf16[64,8,128]{2,1,0:T(8,128)(2,1)} custom-call(bf16[128,512]{1,0:T(8,128)(2,1)} %bitcast.36, bf16[512,64]{1,0:T(8,128)(2,1)} %constant.24.clone.xcos_t_ref, bf16[512,64]{1,0:T(8,128)(2,1)} %constant.25.clone.xsin_t_ref, bf16[128,128]{1,0:T(8,128)(2,1)} %constant.26.clone.swap_t_ref, bf16[2,32,32,64]{3,2,1,0:T(8,128)(2,1)} %bitcast.35, ...), custom_call_target="tpu_custom_call" | custom-call | tf_op jit(solution)/shard_map/pallas_call | solution.py:235
  55.4 1.1 %copy.27 = bf16[64,8,128]{0,2,1:T(8,128)(2,1)S(1)} copy(bf16[64,8,128]{2,1,0:T(8,128)(2,1)} %shard_map.146) | data formatting | bytes 262144 | tf_op jit(solution)/shard_map/pallas_call | solution.py:235
  56.5 0.2 copy.28
  56.8 0.8 %reshape.28.back_ref = bf16[16,32,128]{2,1,0:T(8,128)(2,1)} reshape(bf16[8,2,32,2,64]{4,3,2,1,0:T(2,128)(2,1)S(1)} %copy.28) | data formatting | bytes 262144 | tf_op jit(solution)/shard_map/reshape | solution.py:331
  57.6 1.2 %reshape.29.field_ref = bf16[32,8192]{1,0:T(8,128)(2,1)} reshape(bf16[32,8,2,512]{3,2,1,0:T(2,128)(2,1)S(1)} %multiply_convert_fusion) | data formatting | bytes 1048576 | tf_op jit(solution)/shard_map/reshape | solution.py:333
  58.8 0.7 copy-done.1
  59.4 0.7 copy.29.bias_ref
  60.1 14.9 %shard_map.147 = bf16[4,8192]{1,0:T(4,128)(2,1)} custom-call(bf16[16,32,128]{2,1,0:T(8,128)(2,1)} %reshape.28.back_ref, bf16[128,512]{1,0:T(8,128)(2,1)} %constant.27.clone.table_ref, bf16[32,32]{1,0:T(8,128)(2,1)} %weight_ref.1, bf16[32,8192]{1,0:T(8,128)(2,1)} %reshape.29.field_ref, f32[32,1]{1,0:T(8,128)} %copy.29.bias_ref), custom_call_target="tpu_custom_call" | custom-call | tf_op jit(solution)/shard_map/pallas_call | solution.py:133
  75.0 1.6 %reshape.31 = bf16[4,8,2,512]{3,2,1,0:T(2,128)(2,1)} reshape(bf16[4,8192]{1,0:T(4,128)(2,1)} %shard_map.147) | data formatting | bytes 131072 | tf_op jit(solution)/shard_map/reshape | solution.py:336
  (6 shorter events, 0.0 us)
Async XLA Ops:
  1.4 0.7 copy-start.2
  2.0 0.7 copy-start.3
  3.3 2.1 %copy-start = (bf16[64,512,1,1]{1,0,3,2:T(8,128)(2,1)S(1)}, bf16[64,512,1,1]{1,0,3,2:T(8,128)(2,1)}, u32[]{:S(2)}) copy-start(bf16[64,512,1,1]{1,0,3,2:T(8,128)(2,1)} %constant.33) | copy-start | bytes 196612
  5.5 0.8 %copy-start.4 = (bf16[64,512,1,1]{1,0,3,2:T(8,128)(2,1)S(1)}, bf16[64,512,1,1]{1,0,3,2:T(8,128)(2,1)}, u32[]{:S(2)}) copy-start(bf16[64,512,1,1]{1,0,3,2:T(8,128)(2,1)} %constant.34) | copy-start | bytes 196612
  58.8 0.7 copy-start.1

commit v13 on v12

--- a/solution.py
+++ b/solution.py
@@ -192,10 +192,10 @@
     swap_blocks(parts, blocks_ref, out_ref, landed, send_sems, recv_sems)
 
 
-def mode_mix_kernel(parts, pencil_t_ref, xcos_t_ref, xsin_t_ref, swap_t_ref, weight_ref, keep_ref, out_ref,
+def mode_mix_kernel(parts, pencil_ref, xcos_t_ref, xsin_t_ref, swap_t_ref, weight_ref, count_ref, out_ref,
                     mixed_t, blocks, landed, send_sems, recv_sems):
     barrier = greet_slab(parts)
-    pencil_t = pencil_t_ref[...]
+    pencil_t = pencil_ref[...].astype(jnp.float32).T.astype(pencil_ref.dtype)
     swap_t = swap_t_ref[...]
     swapped_t = jnp.dot(swap_t, pencil_t, preferred_element_type=jnp.float32).astype(pencil_t.dtype)
     spec_t = jnp.dot(pencil_t, xcos_t_ref[...], preferred_element_type=jnp.float32)
@@ -216,7 +216,8 @@
             mixed_t[pl.ds(base + outputs + out, 1), :] = jnp.sum(
                 weight_imag * real + weight_real * imag, axis=0, keepdims=True
             )
-    mixed = (mixed_t[...] * keep_ref[...]).astype(pencil_t.dtype)
+    kept = (lax.axis_index("slab") < count_ref[0]).astype(jnp.float32)
+    mixed = (mixed_t[...] * kept).astype(pencil_t.dtype)
     mixed_swapped = jnp.dot(swap_t, mixed, preferred_element_type=jnp.float32).astype(pencil_t.dtype)
     contract = (((1,), (1,)), ((), ()))
     back = lax.dot_general(xcos_t_ref[...], mixed, contract, preferred_element_type=jnp.float32)
@@ -228,14 +229,15 @@
     swap_blocks(parts, blocks, out_ref, landed, send_sems, recv_sems)
 
 
-def mode_mix_exchange(pencil, xcos_t, xsin_t, swap_t, weight, keep, parts):
+def mode_mix_exchange(pencil, xcos_t, xsin_t, swap_t, weight, count, parts):
     points, width = pencil.shape
     modes = xcos_t.shape[1]
     shape = (parts, points // parts, width)
     return pl.pallas_call(
         functools.partial(mode_mix_kernel, parts),
         out_shape=jax.ShapeDtypeStruct(shape, pencil.dtype),
-        in_specs=[pl.BlockSpec(memory_space=pltpu.VMEM)] * 6,
+        in_specs=[pl.BlockSpec(memory_space=pltpu.VMEM)] * 5
+        + [pl.BlockSpec(memory_space=pltpu.SMEM)],
         out_specs=pl.BlockSpec(memory_space=pltpu.VMEM),
         scratch_shapes=[
             pltpu.VMEM((width, modes), jnp.float32),
@@ -245,7 +247,7 @@
             pltpu.SemaphoreType.DMA((parts,)),
         ],
         compiler_params=pltpu.CompilerParams(collective_id=2, has_side_effects=True),
-    )(pencil.T, xcos_t, xsin_t, swap_t, weight, keep)
+    )(pencil, xcos_t, xsin_t, swap_t, weight, count)
 
 
 def slab_exchange(blocks, parts, exchange_id):
@@ -314,11 +316,9 @@
         -(lane[:, None] == lane[None, :] - channels).astype(np.float32),
     )
     weight = spectral_weight[0].transpose(1, 2, 3, 0)
-    kept = (slab_index * local_modes < mode_count[0]).astype(jnp.float32)
-    keep = jnp.full((1, modes_x), kept, jnp.float32)
     returned = mode_mix_exchange(
         gathered, bf16_constant(full_cos.T), bf16_constant(full_sin.T), bf16_constant(swap.T), weight,
-        keep, slab_count,
+        mode_count, slab_count,
     )
     returned = returned.reshape(modes_y, slab_rows, plane_count, 2, channels)
     weights_y = np.where(np.arange(modes_y) == 0, 1.0, 2.0).astype(np.float32) / np.float32(

time: 77 us -> 74.8 us (0.971)
  local copies, waits for them, and re-layouts: 10.5 us -> 8.3 us
    reshape x1 -> x0, local copies, waits for them, and re-layouts: 1.65 us -> none  [local(): slab_exchange(packed, slab_count, 1).reshape(length_x, packed_width)]
where the time goes in v13:
time: 74.8 us; the launch traced here: 74.4 us
  Pallas kernels  59.9 us (80%)
  local copies, waits for them, and re-layouts  8.3 us (11%)
  other arithmetic  4.16 us (6%)
  between operations  1.41 us (2%)
    pallas_call x1, Pallas kernels, slab_exchange(): pl.pallas_call(functools.partial(slab_exchange_kernel, parts), out_shape=...  26.4 us
    pallas_call x1, Pallas kernels, mode_mix_exchange(): pl.pallas_call(functools.partial(mode_mix_kernel, parts), out_shape=jax.S...  18.6 us
    pallas_call x1, Pallas kernels, layer_sum(): pl.pallas_call(functools.partial(layer_sum_kernel, members), out_shape=ja...  14.9 us
    convert_element_type x1, other arithmetic, local(): field_now = (2.0 * jnp.tanh(0.5 * driven)).astype(jnp.bfloat16)  2.08 us
    unnamed x10, local copies, waits for them, and re-layouts  1.87 us
    reshape x1, local copies, waits for them, and re-layouts, local(): return total.reshape(channels // members, slab_rows, plane_count, length_y)  1.56 us

profile of v13, /device:TPU:1, one launch (start us, length us, event | category | flops | bytes accessed | tf_op | source)
XLA Modules:
  0.0 74.4 jit_solution(1338382300944771731)
XLA Ops:
  0.0 0.7 convert_element_type.15
  1.4 0.0 copy-start.2
  1.4 0.6 copy-done.2
  2.0 0.7 fusion.5
  2.7 0.6 broadcast_multiply_fusion
  3.3 0.0 copy-start
  3.4 2.1 %multiply_convert_fusion = bf16[32,8,2,512]{3,2,1,0:T(2,128)(2,1)S(1)} fusion(bf16[32,8,2,512]{3,2,1,0:T(2,128)(2,1)} %param.15, f32[8,2,512]{2,1,0:T(2,128)S(1)} %convert_element_type.15, f32[32]{0:T(128)S(1)} %broadcast_multiply_fusion), kind=kLoop, calls=%fused_computation.5 | loop fusion | flops 1572864 | bytes 1081472 | tf_op jit(solution)/shard_map/convert_element_type | solution.py:292
  5.5 0.0 copy-start.4
  5.5 0.3 fusion.1
  5.8 0.5 copy-done.4
  6.3 0.3 fusion.2
  6.6 0.1 maximum_bitcast_fusion
  6.7 0.1 copy.23
  6.7 0.8 %copy.24.blocks_ref = bf16[64,8,128]{2,1,0:T(8,128)(2,1)} copy(bf16[64,8,128]{0,2,1:T(8,128)(2,1)S(1)} %bitcast.29) | data formatting | bytes 262144 | tf_op jit(solution)/shard_map/reshape | solution.py:304
  7.5 26.4 %shard_map.145 = bf16[64,8,128]{2,1,0:T(8,128)(2,1)} custom-call(bf16[64,8,128]{2,1,0:T(8,128)(2,1)} %copy.24.blocks_ref), custom_call_target="tpu_custom_call" | custom-call | tf_op jit(solution)/shard_map/pallas_call | solution.py:254
  34.6 18.6 %shard_map.146 = bf16[64,8,128]{2,1,0:T(8,128)(2,1)} custom-call(bf16[512,128]{1,0:T(8,128)(2,1)} %bitcast.32, bf16[512,64]{1,0:T(8,128)(2,1)} %constant.20.clone.xcos_t_ref, bf16[512,64]{1,0:T(8,128)(2,1)} %constant.21.clone.xsin_t_ref, bf16[128,128]{1,0:T(8,128)(2,1)} %constant.22.clone.swap_t_ref, bf16[2,32,32,64]{3,2,1,0:T(8,128)(2,1)} %bitcast.31, ...), custom_call_target="tpu_custom_call" | custom-call | tf_op jit(solution)/shard_map/pallas_call | solution.py:236
  53.2 1.1 %copy.25 = bf16[64,8,128]{0,2,1:T(8,128)(2,1)S(1)} copy(bf16[64,8,128]{2,1,0:T(8,128)(2,1)} %shard_map.146) | data formatting | bytes 262144 | tf_op jit(solution)/shard_map/pallas_call | solution.py:236
  54.3 0.2 copy.26
  54.6 0.8 %reshape.28.back_ref = bf16[16,32,128]{2,1,0:T(8,128)(2,1)} reshape(bf16[8,2,32,2,64]{4,3,2,1,0:T(2,128)(2,1)S(1)} %copy.26) | data formatting | bytes 262144 | tf_op jit(solution)/shard_map/reshape | solution.py:331
  55.4 1.2 %reshape.29.field_ref = bf16[32,8192]{1,0:T(8,128)(2,1)} reshape(bf16[32,8,2,512]{3,2,1,0:T(2,128)(2,1)S(1)} %multiply_convert_fusion) | data formatting | bytes 1048576 | tf_op jit(solution)/shard_map/reshape | solution.py:333
  56.6 0.7 copy-done.1
  57.2 0.7 copy.27.bias_ref
  57.9 14.9 %shard_map.147 = bf16[4,8192]{1,0:T(4,128)(2,1)} custom-call(bf16[16,32,128]{2,1,0:T(8,128)(2,1)} %reshape.28.back_ref, bf16[128,512]{1,0:T(8,128)(2,1)} %constant.23.clone.table_ref, bf16[32,32]{1,0:T(8,128)(2,1)} %weight_ref.1, bf16[32,8192]{1,0:T(8,128)(2,1)} %reshape.29.field_ref, f32[32,1]{1,0:T(8,128)} %copy.27.bias_ref), custom_call_target="tpu_custom_call" | custom-call | tf_op jit(solution)/shard_map/pallas_call | solution.py:133
  72.8 1.6 %reshape.31 = bf16[4,8,2,512]{3,2,1,0:T(2,128)(2,1)} reshape(bf16[4,8192]{1,0:T(4,128)(2,1)} %shard_map.147) | data formatting | bytes 131072 | tf_op jit(solution)/shard_map/reshape | solution.py:336
  (4 shorter events, 0.0 us)
Async XLA Ops:
  1.4 0.7 copy-start.2
  2.0 0.7 copy-start.3
  3.3 2.1 %copy-start = (bf16[64,512,1,1]{1,0,3,2:T(8,128)(2,1)S(1)}, bf16[64,512,1,1]{1,0,3,2:T(8,128)(2,1)}, u32[]{:S(2)}) copy-start(bf16[64,512,1,1]{1,0,3,2:T(8,128)(2,1)} %constant.29) | copy-start | bytes 196612
  5.5 0.8 %copy-start.4 = (bf16[64,512,1,1]{1,0,3,2:T(8,128)(2,1)S(1)}, bf16[64,512,1,1]{1,0,3,2:T(8,128)(2,1)}, u32[]{:S(2)}) copy-start(bf16[64,512,1,1]{1,0,3,2:T(8,128)(2,1)} %constant.30) | copy-start | bytes 196612
  56.6 0.7 copy-start.1

commit v14 on v13

--- a/solution.py
+++ b/solution.py
@@ -74,14 +74,30 @@
     for step in range(1, chips):
         peer = lax.rem(chip + step, chips) * 2 + core
         pl.semaphore_signal(barrier, inc=1, device_id=(peer, slab), device_id_type=mesh_kind)
-    cells = back_ref.shape[0]
+    modes, slab_rows, width = back_ref.shape
+    channels = weight_ref.shape[0]
+    planes = width // (2 * channels)
     length = table_ref.shape[1]
     block_rows = layer.shape[2]
-    for cell in range(cells):
-        lanes = pl.ds(cell * length, length)
-        spectral = jnp.dot(back_ref[cell], table_ref[...], preferred_element_type=jnp.float32)
-        pointwise = jnp.dot(weight_ref[...], field_ref[:, lanes], preferred_element_type=jnp.float32)
-        value[:, lanes] = jax.nn.gelu(pointwise + bias_ref[...] + spectral, approximate=True)
+    table_real = table_ref[:modes, :]
+    table_imag = table_ref[modes:, :]
+    padding = jnp.zeros((width - modes, width), jnp.float32)
+    for row in range(slab_rows):
+        pencil = back_ref[:, row, :].astype(jnp.float32)
+        pencil_t = jnp.concatenate([pencil, padding], axis=0).T[:, :modes].astype(back_ref.dtype)
+        for plane in range(planes):
+            cell = row * planes + plane
+            base = plane * 2 * channels
+            lanes = pl.ds(cell * length, length)
+            spectral = jnp.dot(
+                pencil_t[base:base + channels], table_real, preferred_element_type=jnp.float32
+            )
+            spectral = spectral + jnp.dot(
+                pencil_t[base + channels:base + 2 * channels], table_imag,
+                preferred_element_type=jnp.float32,
+            )
+            pointwise = jnp.dot(weight_ref[...], field_ref[:, lanes], preferred_element_type=jnp.float32)
+            value[:, lanes] = jax.nn.gelu(pointwise + bias_ref[...] + spectral, approximate=True)
     for block in range(members):
         rows = pl.ds(block * block_rows, block_rows)
         layer[block % 2, block // 2] = value[rows, :].astype(layer.dtype)
@@ -320,7 +336,6 @@
         gathered, bf16_constant(full_cos.T), bf16_constant(full_sin.T), bf16_constant(swap.T), weight,
         mode_count, slab_count,
     )
-    returned = returned.reshape(modes_y, slab_rows, plane_count, 2, channels)
     weights_y = np.where(np.arange(modes_y) == 0, 1.0, 2.0).astype(np.float32) / np.float32(
         length_x * length_y
     )
@@ -328,11 +343,10 @@
         np.concatenate([weights_y[:, None] * y_cos, -(weights_y[:, None] * y_sin)], axis=0)
     )
     cells = slab_rows * plane_count
-    back = returned.transpose(1, 2, 4, 3, 0).reshape(cells, channels, 2 * modes_y)
     bias = point_bias.reshape(channels, 1)
     field_rows = field_now.reshape(channels, cells * length_y)
     members = lax.axis_size("member")
-    total = layer_sum(back, table, point_weight, field_rows, bias, members)
+    total = layer_sum(returned, table, point_weight, field_rows, bias, members)
     return total.reshape(channels // members, slab_rows, plane_count, length_y)
 
 

time: 74.8 us -> 72.8 us (0.973)
  local copies, waits for them, and re-layouts: 8.3 us -> 6.16 us
    pallas_call x1 -> x0, local copies, waits for them, and re-layouts: 1.09 us -> none  [mode_mix_exchange(): pl.pallas_call(functools.partial(mode_mix_kernel, parts), out_shape=jax.S...]
    reshape x1 -> x0, local copies, waits for them, and re-layouts: 0.8 us -> none  [local(): returned.transpose(1, 2, 4, 3, 0).reshape(cells, channels, 2 * modes_y)]
where the time goes in v14:
time: 72.8 us; the launch traced here: 72.3 us
  Pallas kernels  60.1 us (83%)
  local copies, waits for them, and re-layouts  6.16 us (8%)
  other arithmetic  4.16 us (6%)
  between operations  1.4 us (2%)
    pallas_call x1, Pallas kernels, slab_exchange(): pl.pallas_call(functools.partial(slab_exchange_kernel, parts), out_shape=...  26.4 us
    pallas_call x1, Pallas kernels, mode_mix_exchange(): pl.pallas_call(functools.partial(mode_mix_kernel, parts), out_shape=jax.S...  18.6 us
    pallas_call x1, Pallas kernels, layer_sum(): pl.pallas_call(functools.partial(layer_sum_kernel, members), out_shape=ja...  15 us
    convert_element_type x1, other arithmetic, local(): field_now = (2.0 * jnp.tanh(0.5 * driven)).astype(jnp.bfloat16)  2.08 us
    unnamed x10, local copies, waits for them, and re-layouts  1.87 us
    reshape x1, local copies, waits for them, and re-layouts, local(): return total.reshape(channels // members, slab_rows, plane_count, length_y)  1.56 us

profile of v14, /device:TPU:1, one launch (start us, length us, event | category | flops | bytes accessed | tf_op | source)
XLA Modules:
  0.0 72.3 jit_solution(3977954241334836965)
XLA Ops:
  0.0 0.7 %convert_element_type.15 = f32[8,2,512]{2,1,0:T(2,128)S(1)} convert(bf16[8,2,512]{2,1,0:T(2,128)(2,1)} %param.16) | non-fusion elementwise | flops 8192 | bytes 49152 | tf_op jit(solution)/shard_map/convert_element_type | solution.py:307
  1.4 0.0 copy-start.2
  1.4 0.6 copy-done.2
  2.0 0.0 copy-start.3
  2.0 0.7 fusion.5
  2.7 0.0 copy-done.3
  2.7 0.6 broadcast_multiply_fusion
  3.3 0.0 copy-start
  3.4 2.1 %multiply_convert_fusion = bf16[32,8,2,512]{3,2,1,0:T(2,128)(2,1)S(1)} fusion(bf16[32,8,2,512]{3,2,1,0:T(2,128)(2,1)} %param.15, f32[8,2,512]{2,1,0:T(2,128)S(1)} %convert_element_type.15, f32[32]{0:T(128)S(1)} %broadcast_multiply_fusion), kind=kLoop, calls=%fused_computation.5 | loop fusion | flops 1572864 | bytes 1081472 | tf_op jit(solution)/shard_map/convert_element_type | solution.py:308
  5.5 0.0 copy-done
  5.5 0.0 copy-start.4
  5.5 0.3 fusion.1
  5.8 0.5 copy-done.4
  6.3 0.3 fusion.2
  6.6 0.1 maximum_bitcast_fusion
  6.7 0.1 copy.22
  6.7 0.8 %copy.23.blocks_ref = bf16[64,8,128]{2,1,0:T(8,128)(2,1)} copy(bf16[64,8,128]{0,2,1:T(8,128)(2,1)S(1)} %bitcast.26) | data formatting | bytes 262144 | tf_op jit(solution)/shard_map/reshape | solution.py:320
  7.5 26.4 %shard_map.145 = bf16[64,8,128]{2,1,0:T(8,128)(2,1)} custom-call(bf16[64,8,128]{2,1,0:T(8,128)(2,1)} %copy.23.blocks_ref), custom_call_target="tpu_custom_call" | custom-call | tf_op jit(solution)/shard_map/pallas_call | solution.py:270
  34.6 18.6 %shard_map.146.back_ref = bf16[64,8,128]{2,1,0:T(8,128)(2,1)} custom-call(bf16[512,128]{1,0:T(8,128)(2,1)} %bitcast.28, bf16[512,64]{1,0:T(8,128)(2,1)} %constant.20.clone.xcos_t_ref, bf16[512,64]{1,0:T(8,128)(2,1)} %constant.21.clone.xsin_t_ref, bf16[128,128]{1,0:T(8,128)(2,1)} %constant.22.clone.swap_t_ref, bf16[2,32,32,64]{3,2,1,0:T(8,128)(2,1)} %bitcast.27, ...), custom_call_target="tpu_custom_call" | custom-call | tf_op jit(solution)/shard_map/pallas_call | solution.py:252
  53.2 1.2 %reshape.21.field_ref = bf16[32,8192]{1,0:T(8,128)(2,1)} reshape(bf16[32,8,2,512]{3,2,1,0:T(2,128)(2,1)S(1)} %multiply_convert_fusion) | data formatting | bytes 1048576 | tf_op jit(solution)/shard_map/reshape | solution.py:347
  54.4 0.7 copy-done.1
  55.1 0.7 copy.24.bias_ref
  55.8 15.0 %shard_map.147 = bf16[4,8192]{1,0:T(4,128)(2,1)} custom-call(bf16[64,8,128]{2,1,0:T(8,128)(2,1)} %shard_map.146.back_ref, bf16[128,512]{1,0:T(8,128)(2,1)} %constant.23.clone.table_ref, bf16[32,32]{1,0:T(8,128)(2,1)} %weight_ref.1, bf16[32,8192]{1,0:T(8,128)(2,1)} %reshape.21.field_ref, f32[32,1]{1,0:T(8,128)} %copy.24.bias_ref), custom_call_target="tpu_custom_call" | custom-call | tf_op jit(solution)/shard_map/pallas_call | solution.py:149
  70.8 1.6 %reshape.23 = bf16[4,8,2,512]{3,2,1,0:T(2,128)(2,1)} reshape(bf16[4,8192]{1,0:T(4,128)(2,1)} %shard_map.147) | data formatting | bytes 131072 | tf_op jit(solution)/shard_map/reshape | solution.py:350
  (1 shorter events, 0.0 us)
Async XLA Ops:
  1.4 0.7 copy-start.2
  2.0 0.7 copy-start.3
  3.3 2.1 %copy-start = (bf16[64,512,1,1]{1,0,3,2:T(8,128)(2,1)S(1)}, bf16[64,512,1,1]{1,0,3,2:T(8,128)(2,1)}, u32[]{:S(2)}) copy-start(bf16[64,512,1,1]{1,0,3,2:T(8,128)(2,1)} %constant.29) | copy-start | bytes 196612
  5.5 0.8 %copy-start.4 = (bf16[64,512,1,1]{1,0,3,2:T(8,128)(2,1)S(1)}, bf16[64,512,1,1]{1,0,3,2:T(8,128)(2,1)}, u32[]{:S(2)}) copy-start(bf16[64,512,1,1]{1,0,3,2:T(8,128)(2,1)} %constant.30) | copy-start | bytes 196612
  54.4 0.7 copy-start.1

commit v15 on v14

--- a/solution.py
+++ b/solution.py
@@ -302,10 +302,12 @@
     slab_index = lax.axis_index("slab")
     level_ids = jnp.arange(amplitudes.shape[0], dtype=jnp.int32)
     amplitude = jnp.sum(jnp.where(level_ids == amp_index[0], amplitudes, 0.0))
-    driven = base_field.astype(jnp.float32) + amplitude * load[:, None, None, None] * forcing[
-        None
-    ].astype(jnp.float32)
-    field_now = (2.0 * jnp.tanh(0.5 * driven)).astype(jnp.bfloat16)
+    cells = slab_rows * plane_count
+    driven = base_field.reshape(channels, cells * length_y).astype(jnp.float32) + amplitude * load[
+        :, None
+    ] * forcing.reshape(1, cells * length_y).astype(jnp.float32)
+    field_rows = (2.0 * jnp.tanh(0.5 * driven)).astype(jnp.bfloat16)
+    field_now = field_rows.reshape(channels, slab_rows, plane_count, length_y)
     y_cos, y_sin = phase_tables(np.arange(modes_y), np.arange(length_y), length_y)
     y_real = jnp.einsum(
         "cxzy,ky->kxcz", field_now, bf16_constant(y_cos), preferred_element_type=jnp.float32
@@ -342,9 +344,7 @@
     table = bf16_constant(
         np.concatenate([weights_y[:, None] * y_cos, -(weights_y[:, None] * y_sin)], axis=0)
     )
-    cells = slab_rows * plane_count
     bias = point_bias.reshape(channels, 1)
-    field_rows = field_now.reshape(channels, cells * length_y)
     members = lax.axis_size("member")
     total = layer_sum(returned, table, point_weight, field_rows, bias, members)
     return total.reshape(channels // members, slab_rows, plane_count, length_y)

time: 72.8 us -> 73.1 us (level)
  other arithmetic: 4.16 us -> 5.16 us
  local copies, waits for them, and re-layouts: 6.16 us -> 5.32 us
    reshape x1 -> x0, local copies, waits for them, and re-layouts: 1.18 us -> none  [local(): field_rows = field_now.reshape(channels, cells * length_y)]
    unnamed x0 -> x1, other arithmetic: none -> 0.74 us
    unnamed x10 -> x13, local copies, waits for them, and re-layouts: 1.87 us -> 1.93 us
where the time goes in v15:
time: 73.1 us; the launch traced here: 72.7 us
  Pallas kernels  60.2 us (82%)
  local copies, waits for them, and re-layouts  5.32 us (7%)
  other arithmetic  5.16 us (7%)
  between operations  1.43 us (2%)
    pallas_call x1, Pallas kernels, slab_exchange(): pl.pallas_call(functools.partial(slab_exchange_kernel, parts), out_shape=...  26.4 us
    pallas_call x1, Pallas kernels, mode_mix_exchange(): pl.pallas_call(functools.partial(mode_mix_kernel, parts), out_shape=jax.S...  18.8 us
    pallas_call x1, Pallas kernels, layer_sum(): pl.pallas_call(functools.partial(layer_sum_kernel, members), out_shape=ja...  15 us
    convert_element_type x2, other arithmetic, local(): field_rows = (2.0 * jnp.tanh(0.5 * driven)).astype(jnp.bfloat16)  3.14 us
    unnamed x13, local copies, waits for them, and re-layouts  1.93 us
    reshape x1, local copies, waits for them, and re-layouts, local(): return total.reshape(channels // members, slab_rows, plane_count, length_y)  1.56 us

profile of v15, /device:TPU:1, one launch (start us, length us, event | category | flops | bytes accessed | tf_op | source)
XLA Modules:
  0.0 72.7 jit_solution(2274908187824796878)
XLA Ops:
  0.0 0.7 %convert_bitcast_fusion = (f32[8,4,2,128]{3,2,1,0:T(2,128)S(1)}, f32[8,2,512]{2,1,0:T(2,128)S(1)}) fusion(bf16[8,2,512]{2,1,0:T(2,128)(2,1)} %param.16), kind=kLoop, calls=%fused_computation.10 | loop fusion | flops 8192 | bytes 81920
  1.4 0.0 copy-start.3
  1.4 0.6 copy-done.3
  2.0 0.6 fusion.5
  2.7 0.0 copy-done.4
  2.7 0.6 broadcast_multiply_fusion
  3.3 0.0 copy-start.1
  3.3 2.1 %multiply_convert_fusion.1 = bf16[32,8,2,512]{3,2,1,0:T(2,128)(2,1)S(1)} fusion(f32[8,2,512]{2,1,0:T(2,128)S(1)} %get-tuple-element.6, f32[32]{0:T(128)S(1)} %broadcast_multiply_fusion, bf16[32,8,2,512]{3,2,1,0:T(2,128)(2,1)} %param.15), kind=kLoop, calls=%fused_computation.6 | loop fusion | flops 1572864 | bytes 1081472 | tf_op jit(solution)/shard_map/convert_element_type | solution.py:309
  5.4 0.0 copy-start.5
  5.5 0.3 fusion.1
  5.7 0.5 copy-done.5
  6.3 0.3 fusion.2
  6.6 0.1 maximum_bitcast_fusion
  6.6 0.1 copy.22
  6.7 0.8 %copy.23.blocks_ref = bf16[64,8,128]{2,1,0:T(8,128)(2,1)} copy(bf16[64,8,128]{0,2,1:T(8,128)(2,1)S(1)} %bitcast.29) | data formatting | bytes 262144 | tf_op jit(solution)/shard_map/reshape | solution.py:322
  7.5 26.4 %shard_map.145 = bf16[64,8,128]{2,1,0:T(8,128)(2,1)} custom-call(bf16[64,8,128]{2,1,0:T(8,128)(2,1)} %copy.23.blocks_ref), custom_call_target="tpu_custom_call" | custom-call | tf_op jit(solution)/shard_map/pallas_call | solution.py:270
  34.6 0.0 copy-start
  34.6 18.8 %shard_map.146.back_ref = bf16[64,8,128]{2,1,0:T(8,128)(2,1)} custom-call(bf16[512,128]{1,0:T(8,128)(2,1)} %bitcast.31, bf16[512,64]{1,0:T(8,128)(2,1)} %constant.20.clone.xcos_t_ref, bf16[512,64]{1,0:T(8,128)(2,1)} %constant.21.clone.xsin_t_ref, bf16[128,128]{1,0:T(8,128)(2,1)} %constant.22.clone.swap_t_ref, bf16[2,32,32,64]{3,2,1,0:T(8,128)(2,1)} %bitcast.30, ...), custom_call_target="tpu_custom_call" | custom-call | tf_op jit(solution)/shard_map/pallas_call | solution.py:252
  53.4 0.3 reshape.42
  53.7 1.1 %multiply_convert_fusion.field_ref = bf16[32,8192]{1,0:T(8,128)(2,1)} fusion(f32[32,8192]{1,0:T(8,128)S(1)} %reshape.42, f32[8192]{0:T(1024)S(1)} %bitcast.32, f32[32]{0:T(128)S(1)} %broadcast_multiply_fusion), kind=kLoop, calls=%fused_computation.5 | loop fusion | flops 1310720 | bytes 1605760 | tf_op jit(solution)/shard_map/convert_element_type | solution.py:309
  54.8 0.7 copy-done.2
  55.4 0.7 copy.24.bias_ref
  56.1 15.0 %shard_map.147 = bf16[4,8192]{1,0:T(4,128)(2,1)} custom-call(bf16[64,8,128]{2,1,0:T(8,128)(2,1)} %shard_map.146.back_ref, bf16[128,512]{1,0:T(8,128)(2,1)} %constant.23.clone.table_ref, bf16[32,32]{1,0:T(8,128)(2,1)} %weight_ref.1, bf16[32,8192]{1,0:T(8,128)(2,1)} %multiply_convert_fusion.field_ref, f32[32,1]{1,0:T(8,128)} %copy.24.bias_ref), custom_call_target="tpu_custom_call" | custom-call | tf_op jit(solution)/shard_map/pallas_call | solution.py:149
  71.1 1.6 %reshape.41 = bf16[4,8,2,512]{3,2,1,0:T(2,128)(2,1)} reshape(bf16[4,8192]{1,0:T(4,128)(2,1)} %shard_map.147) | data formatting | bytes 131072 | tf_op jit(solution)/shard_map/reshape | solution.py:350
  (5 shorter events, 0.0 us)
Async XLA Ops:
  1.4 0.7 copy-start.3
  2.0 0.7 copy-start.4
  3.3 2.1 %copy-start.1 = (bf16[64,512,1,1]{1,0,3,2:T(8,128)(2,1)S(1)}, bf16[64,512,1,1]{1,0,3,2:T(8,128)(2,1)}, u32[]{:S(2)}) copy-start(bf16[64,512,1,1]{1,0,3,2:T(8,128)(2,1)} %constant.29) | copy-start | bytes 196612
  5.4 0.8 %copy-start.5 = (bf16[64,512,1,1]{1,0,3,2:T(8,128)(2,1)S(1)}, bf16[64,512,1,1]{1,0,3,2:T(8,128)(2,1)}, u32[]{:S(2)}) copy-start(bf16[64,512,1,1]{1,0,3,2:T(8,128)(2,1)} %constant.30) | copy-start | bytes 196612
  34.6 18.8 %copy-start = (bf16[32,8,2,512]{3,2,1,0:T(2,128)(2,1)S(1)}, bf16[32,8,2,512]{3,2,1,0:T(2,128)(2,1)}, u32[]{:S(2)}) copy-start(bf16[32,8,2,512]{3,2,1,0:T(2,128)(2,1)} %param.15) | copy-start | bytes 1572868
  54.8 0.7 copy-start.2

commit v16 on v15

--- a/solution.py
+++ b/solution.py
@@ -309,15 +309,9 @@
     field_rows = (2.0 * jnp.tanh(0.5 * driven)).astype(jnp.bfloat16)
     field_now = field_rows.reshape(channels, slab_rows, plane_count, length_y)
     y_cos, y_sin = phase_tables(np.arange(modes_y), np.arange(length_y), length_y)
-    y_real = jnp.einsum(
-        "cxzy,ky->kxcz", field_now, bf16_constant(y_cos), preferred_element_type=jnp.float32
-    )
-    y_imag = -jnp.einsum(
-        "cxzy,ky->kxcz", field_now, bf16_constant(y_sin), preferred_element_type=jnp.float32
-    )
+    forward_table = bf16_constant(np.stack([y_cos, -y_sin]))
     packed = (
-        jnp.stack([y_real, y_imag], axis=2)
-        .transpose(0, 1, 4, 2, 3)
+        jnp.einsum("cxzy,rky->kxzrc", field_now, forward_table, preferred_element_type=jnp.float32)
         .astype(jnp.bfloat16)
         .reshape(modes_y, slab_rows, packed_width)
     )

time: 73.1 us -> 72 us (0.985)
  other arithmetic: 5.16 us -> 4.03 us
    convert_element_type x2, other arithmetic: 3.14 us -> 2.06 us  [local(): field_rows = (2.0 * jnp.tanh(0.5 * driven)).astype(jnp.bfloat16)]
    convert_element_type x1, local copies, waits for them, and re-layouts: 0.27 us -> 1.31 us  [local(): base_field.reshape(channels, cells * length_y).astype(jnp.float32)]
    unnamed x13 -> x11, local copies, waits for them, and re-layouts: 1.93 us -> 1.35 us
where the time goes in v16:
time: 72 us; the launch traced here: 71.6 us
  Pallas kernels  60 us (83%)
  local copies, waits for them, and re-layouts  5.8 us (8%)
  other arithmetic  4.03 us (6%)
  between operations  1.4 us (2%)
    pallas_call x1, Pallas kernels, slab_exchange(): pl.pallas_call(functools.partial(slab_exchange_kernel, parts), out_shape=...  26.4 us
    pallas_call x1, Pallas kernels, mode_mix_exchange(): pl.pallas_call(functools.partial(mode_mix_kernel, parts), out_shape=jax.S...  18.6 us
    pallas_call x1, Pallas kernels, layer_sum(): pl.pallas_call(functools.partial(layer_sum_kernel, members), out_shape=ja...  15 us
    convert_element_type x2, other arithmetic, local(): field_rows = (2.0 * jnp.tanh(0.5 * driven)).astype(jnp.bfloat16)  2.06 us
    reshape x1, local copies, waits for them, and re-layouts, local(): return total.reshape(channels // members, slab_rows, plane_count, length_y)  1.56 us

profile of v16, /device:TPU:1, one launch (start us, length us, event | category | flops | bytes accessed | tf_op | source)
XLA Modules:
  0.0 71.6 jit_solution(5341077233533019880)
XLA Ops:
  0.0 0.7 %convert_bitcast_fusion = (f32[8,4,2,128]{3,2,1,0:T(2,128)S(1)}, f32[8,2,512]{2,1,0:T(2,128)S(1)}) fusion(bf16[8,2,512]{2,1,0:T(2,128)(2,1)} %param.15), kind=kLoop, calls=%fused_computation.6 | loop fusion | flops 8192 | bytes 81920
  1.4 0.0 copy-start.2
  1.4 0.6 copy-done.2
  2.1 0.0 copy-start.3
  2.1 0.6 fusion.3
  2.7 0.0 copy-done.3
  2.7 0.6 broadcast_multiply_fusion
  3.3 1.3 %reshape.42 = f32[32,8192]{1,0:T(8,128)S(1)} reshape(bf16[32,8,2,512]{3,2,1,0:T(2,128)(2,1)} %param.14) | data formatting | bytes 1572864 | tf_op jit(solution)/shard_map/convert_element_type | solution.py:306
  4.6 0.0 copy-start
  4.7 1.1 %multiply_convert_fusion.field_ref = bf16[32,8192]{1,0:T(8,128)(2,1)} fusion(f32[32,8192]{1,0:T(8,128)S(1)} %reshape.42, f32[8192]{0:T(1024)S(1)} %bitcast.22, f32[32]{0:T(128)S(1)} %broadcast_multiply_fusion), kind=kLoop, calls=%fused_computation.2 | loop fusion | flops 1310720 | bytes 1605760 | tf_op jit(solution)/shard_map/convert_element_type | solution.py:309
  5.7 0.0 copy-done
  5.7 0.0 copy-start.4
  5.7 1.0 %fusion.2 = bf16[32,8,2,512,1]{3,2,1,0,4:T(2,128)(2,1)S(1)} fusion(f32[8,2,512]{2,1,0:T(2,128)S(1)} %get-tuple-element.6, f32[32]{0:T(128)S(1)} %broadcast_multiply_fusion, bf16[32,8,2,512]{3,2,1,0:T(2,128)(2,1)S(1)} %copy-done), kind=kLoop, calls=%fused_computation.5 | loop fusion | flops 1572864 | bytes 1081472 | tf_op jit(solution)/shard_map/convert_element_type | solution.py:309
  6.7 0.0 copy-done.4
  6.7 0.3 fusion
  7.1 0.1 copy.19
  7.2 0.8 %copy.20.blocks_ref = bf16[64,8,128]{2,1,0:T(8,128)(2,1)} copy(bf16[64,8,128]{0,2,1:T(8,128)(2,1)S(1)} %bitcast.19) | data formatting | bytes 262144 | tf_op jit(solution)/shard_map/reshape | solution.py:316
  8.0 26.4 %shard_map.136 = bf16[64,8,128]{2,1,0:T(8,128)(2,1)} custom-call(bf16[64,8,128]{2,1,0:T(8,128)(2,1)} %copy.20.blocks_ref), custom_call_target="tpu_custom_call" | custom-call | tf_op jit(solution)/shard_map/pallas_call | solution.py:270
  35.0 18.6 %shard_map.137.back_ref = bf16[64,8,128]{2,1,0:T(8,128)(2,1)} custom-call(bf16[512,128]{1,0:T(8,128)(2,1)} %bitcast.21, bf16[512,64]{1,0:T(8,128)(2,1)} %constant.17.clone.xcos_t_ref, bf16[512,64]{1,0:T(8,128)(2,1)} %constant.18.clone.xsin_t_ref, bf16[128,128]{1,0:T(8,128)(2,1)} %constant.19.clone.swap_t_ref, bf16[2,32,32,64]{3,2,1,0:T(8,128)(2,1)} %bitcast.20, ...), custom_call_target="tpu_custom_call" | custom-call | tf_op jit(solution)/shard_map/pallas_call | solution.py:252
  53.7 0.0 copy-start.1
  53.7 0.6 copy-done.1
  54.3 0.7 copy.21.bias_ref
  55.0 15.0 %shard_map.138 = bf16[4,8192]{1,0:T(4,128)(2,1)} custom-call(bf16[64,8,128]{2,1,0:T(8,128)(2,1)} %shard_map.137.back_ref, bf16[128,512]{1,0:T(8,128)(2,1)} %constant.20.clone.table_ref, bf16[32,32]{1,0:T(8,128)(2,1)} %weight_ref.1, bf16[32,8192]{1,0:T(8,128)(2,1)} %multiply_convert_fusion.field_ref, f32[32,1]{1,0:T(8,128)} %copy.21.bias_ref), custom_call_target="tpu_custom_call" | custom-call | tf_op jit(solution)/shard_map/pallas_call | solution.py:149
  70.0 1.6 %reshape.41 = bf16[4,8,2,512]{3,2,1,0:T(2,128)(2,1)} reshape(bf16[4,8192]{1,0:T(4,128)(2,1)} %shard_map.138) | data formatting | bytes 131072 | tf_op jit(solution)/shard_map/reshape | solution.py:344
  (1 shorter events, 0.0 us)
Async XLA Ops:
  1.4 0.7 copy-start.2
  2.1 0.7 copy-start.3
  4.6 1.1 %copy-start = (bf16[32,8,2,512]{3,2,1,0:T(2,128)(2,1)S(1)}, bf16[32,8,2,512]{3,2,1,0:T(2,128)(2,1)}, u32[]{:S(2)}) copy-start(bf16[32,8,2,512]{3,2,1,0:T(2,128)(2,1)} %param.14) | copy-start | bytes 1572868
  5.7 1.0 %copy-start.4 = (bf16[2,64,512,1,1]{2,1,0,4,3:T(8,128)(2,1)S(1)}, bf16[2,64,512,1,1]{2,1,0,4,3:T(8,128)(2,1)}, u32[]{:S(2)}) copy-start(bf16[2,64,512,1,1]{2,1,0,4,3:T(8,128)(2,1)} %constant.26) | copy-start | bytes 393220
  53.7 0.7 copy-start.1

commit v17 on v16

--- a/solution.py
+++ b/solution.py
@@ -199,7 +199,8 @@
     for step in range(1, parts):
         peer = lax.rem(me + step, parts)
         copy_of(peer, me, peer).wait_send()
-    out_ref[...] = landed[...]
+    if out_ref is not None:
+        out_ref[...] = landed[...]
 
 
 def slab_exchange_kernel(parts, blocks_ref, out_ref, landed, send_sems, recv_sems):
@@ -208,10 +209,14 @@
     swap_blocks(parts, blocks_ref, out_ref, landed, send_sems, recv_sems)
 
 
-def mode_mix_kernel(parts, pencil_ref, xcos_t_ref, xsin_t_ref, swap_t_ref, weight_ref, count_ref, out_ref,
-                    mixed_t, blocks, landed, send_sems, recv_sems):
+def mode_mix_kernel(parts, modes_ref, xcos_t_ref, xsin_t_ref, swap_t_ref, weight_ref, count_ref, out_ref,
+                    mixed_t, first, blocks, landed, first_send, first_recv, send_sems, recv_sems):
     barrier = greet_slab(parts)
-    pencil_t = pencil_ref[...].astype(jnp.float32).T.astype(pencil_ref.dtype)
+    pl.semaphore_wait(barrier, parts - 1)
+    swap_blocks(parts, modes_ref, None, first, first_send, first_recv)
+    pencil = first[...].astype(jnp.float32)
+    pencil = pencil.reshape(pencil.shape[0] * pencil.shape[1], pencil.shape[2])
+    pencil_t = pencil.T.astype(modes_ref.dtype)
     swap_t = swap_t_ref[...]
     swapped_t = jnp.dot(swap_t, pencil_t, preferred_element_type=jnp.float32).astype(pencil_t.dtype)
     spec_t = jnp.dot(pencil_t, xcos_t_ref[...], preferred_element_type=jnp.float32)
@@ -241,14 +246,13 @@
         xsin_t_ref[...], mixed_swapped, contract, preferred_element_type=jnp.float32
     )
     blocks[...] = back.reshape(blocks.shape).astype(blocks.dtype)
-    pl.semaphore_wait(barrier, parts - 1)
     swap_blocks(parts, blocks, out_ref, landed, send_sems, recv_sems)
 
 
 def mode_mix_exchange(pencil, xcos_t, xsin_t, swap_t, weight, count, parts):
-    points, width = pencil.shape
+    shape = pencil.shape
+    width = shape[2]
     modes = xcos_t.shape[1]
-    shape = (parts, points // parts, width)
     return pl.pallas_call(
         functools.partial(mode_mix_kernel, parts),
         out_shape=jax.ShapeDtypeStruct(shape, pencil.dtype),
@@ -259,6 +263,9 @@
             pltpu.VMEM((width, modes), jnp.float32),
             pltpu.VMEM(shape, pencil.dtype),
             pltpu.VMEM(shape, pencil.dtype),
+            pltpu.VMEM(shape, pencil.dtype),
+            pltpu.SemaphoreType.DMA((parts,)),
+            pltpu.SemaphoreType.DMA((parts,)),
             pltpu.SemaphoreType.DMA((parts,)),
             pltpu.SemaphoreType.DMA((parts,)),
         ],
@@ -319,7 +326,6 @@
         [np.arange(modes_x // 2), np.arange(length_x - modes_x // 2, length_x)]
     )
     full_cos, full_sin = phase_tables(frequency_x, np.arange(length_x), length_x)
-    gathered = slab_exchange(packed, slab_count, 1).reshape(length_x, packed_width)
     lane = np.arange(packed_width)
     real_lane = (lane // channels) % 2 == 0
     swap = np.where(
@@ -329,7 +335,7 @@
     )
     weight = spectral_weight[0].transpose(1, 2, 3, 0)
     returned = mode_mix_exchange(
-        gathered, bf16_constant(full_cos.T), bf16_constant(full_sin.T), bf16_constant(swap.T), weight,
+        packed, bf16_constant(full_cos.T), bf16_constant(full_sin.T), bf16_constant(swap.T), weight,
         mode_count, slab_count,
     )
     weights_y = np.where(np.arange(modes_y) == 0, 1.0, 2.0).astype(np.float32) / np.float32(

time: 72 us -> 65.9 us (0.915)
  Pallas kernels: 60 us -> 53.9 us
    pallas_call x1 -> x0, Pallas kernels: 26.4 us -> none  [slab_exchange(): pl.pallas_call(functools.partial(slab_exchange_kernel, parts), out_shape=...]
    pallas_call x1, Pallas kernels: 18.6 us -> 39.9 us  [mode_mix_exchange(): pl.pallas_call(functools.partial(mode_mix_kernel, parts), out_shape=jax.S...]
    pallas_call x1, Pallas kernels: 15 us -> 14 us  [layer_sum(): pl.pallas_call(functools.partial(layer_sum_kernel, members), out_shape=ja...]
where the time goes in v17:
time: 65.9 us; the launch traced here: 65.4 us
  Pallas kernels  53.9 us (82%)
  local copies, waits for them, and re-layouts  5.81 us (9%)
  other arithmetic  4.03 us (6%)
  between operations  1.4 us (2%)
    pallas_call x1, Pallas kernels, mode_mix_exchange(): pl.pallas_call(functools.partial(mode_mix_kernel, parts), out_shape=jax.S...  39.9 us
    pallas_call x1, Pallas kernels, layer_sum(): pl.pallas_call(functools.partial(layer_sum_kernel, members), out_shape=ja...  14 us
    convert_element_type x2, other arithmetic, local(): field_rows = (2.0 * jnp.tanh(0.5 * driven)).astype(jnp.bfloat16)  2.06 us
    reshape x1, local copies, waits for them, and re-layouts, local(): return total.reshape(channels // members, slab_rows, plane_count, length_y)  1.56 us
    unnamed x11, local copies, waits for them, and re-layouts  1.35 us

profile of v17, /device:TPU:1, one launch (start us, length us, event | category | flops | bytes accessed | tf_op | source)
XLA Modules:
  0.0 65.4 jit_solution(15094695771576798381)
XLA Ops:
  0.0 0.7 %convert_bitcast_fusion = (f32[8,4,2,128]{3,2,1,0:T(2,128)S(1)}, f32[8,2,512]{2,1,0:T(2,128)S(1)}) fusion(bf16[8,2,512]{2,1,0:T(2,128)(2,1)} %param.15), kind=kLoop, calls=%fused_computation.6 | loop fusion | flops 8192 | bytes 81920
  1.4 0.0 copy-start.2
  1.4 0.6 copy-done.2
  2.1 0.0 copy-start.3
  2.1 0.6 fusion.3
  2.7 0.0 copy-done.3
  2.7 0.6 broadcast_multiply_fusion
  3.3 1.3 %reshape.38 = f32[32,8192]{1,0:T(8,128)S(1)} reshape(bf16[32,8,2,512]{3,2,1,0:T(2,128)(2,1)} %param.14) | data formatting | bytes 1572864 | tf_op jit(solution)/shard_map/convert_element_type | solution.py:313
  4.6 0.0 copy-start
  4.7 1.1 %multiply_convert_fusion.field_ref = bf16[32,8192]{1,0:T(8,128)(2,1)} fusion(f32[32,8192]{1,0:T(8,128)S(1)} %reshape.38, f32[8192]{0:T(1024)S(1)} %bitcast.20, f32[32]{0:T(128)S(1)} %broadcast_multiply_fusion), kind=kLoop, calls=%fused_computation.2 | loop fusion | flops 1310720 | bytes 1605760 | tf_op jit(solution)/shard_map/convert_element_type | solution.py:316
  5.7 0.0 copy-done
  5.7 0.0 copy-start.4
  5.7 1.0 %fusion.2 = bf16[32,8,2,512,1]{3,2,1,0,4:T(2,128)(2,1)S(1)} fusion(f32[8,2,512]{2,1,0:T(2,128)S(1)} %get-tuple-element.6, f32[32]{0:T(128)S(1)} %broadcast_multiply_fusion, bf16[32,8,2,512]{3,2,1,0:T(2,128)(2,1)S(1)} %copy-done), kind=kLoop, calls=%fused_computation.5 | loop fusion | flops 1572864 | bytes 1081472 | tf_op jit(solution)/shard_map/convert_element_type | solution.py:316
  6.7 0.0 copy-done.4
  6.7 0.3 fusion
  7.1 0.1 copy.19
  7.2 0.8 %copy.20.modes_ref = bf16[64,8,128]{2,1,0:T(8,128)(2,1)} copy(bf16[64,8,128]{0,2,1:T(8,128)(2,1)S(1)} %bitcast.18) | data formatting | bytes 262144 | tf_op jit(solution)/shard_map/reshape | solution.py:323
  8.6 39.9 %shard_map.136.back_ref = bf16[64,8,128]{2,1,0:T(8,128)(2,1)} custom-call(bf16[64,8,128]{2,1,0:T(8,128)(2,1)} %copy.20.modes_ref, bf16[512,64]{1,0:T(8,128)(2,1)} %constant.17.clone.xcos_t_ref, bf16[512,64]{1,0:T(8,128)(2,1)} %constant.18.clone.xsin_t_ref, bf16[128,128]{1,0:T(8,128)(2,1)} %constant.19.clone.swap_t_ref, bf16[2,32,32,64]{3,2,1,0:T(8,128)(2,1)} %bitcast.19, ...), custom_call_target="tpu_custom_call" | custom-call | tf_op jit(solution)/shard_map/pallas_call | solution.py:256
  48.5 0.0 copy-start.1
  48.5 0.6 copy-done.1
  49.1 0.7 %copy.21.bias_ref = f32[32,1]{1,0:T(8,128)} copy(f32[32,1]{0,1:T(1,128)S(1)} %bitcast.21) | data formatting | bytes 256 | tf_op jit(solution)/shard_map/reshape | solution.py:347
  49.8 14.0 %shard_map.137 = bf16[4,8192]{1,0:T(4,128)(2,1)} custom-call(bf16[64,8,128]{2,1,0:T(8,128)(2,1)} %shard_map.136.back_ref, bf16[128,512]{1,0:T(8,128)(2,1)} %constant.20.clone.table_ref, bf16[32,32]{1,0:T(8,128)(2,1)} %weight_ref.1, bf16[32,8192]{1,0:T(8,128)(2,1)} %multiply_convert_fusion.field_ref, f32[32,1]{1,0:T(8,128)} %copy.21.bias_ref), custom_call_target="tpu_custom_call" | custom-call | tf_op jit(solution)/shard_map/pallas_call | solution.py:149
  63.9 1.6 %reshape.37 = bf16[4,8,2,512]{3,2,1,0:T(2,128)(2,1)} reshape(bf16[4,8192]{1,0:T(4,128)(2,1)} %shard_map.137) | data formatting | bytes 131072 | tf_op jit(solution)/shard_map/reshape | solution.py:350
  (1 shorter events, 0.0 us)
Async XLA Ops:
  1.4 0.7 %copy-start.2 = (f32[16]{0:T(128)S(1)}, f32[16]{0:T(128)}, u32[]{:S(2)}) copy-start(f32[16]{0:T(128)} %param.17) | copy-start | bytes 196
  2.1 0.7 %copy-start.3 = (f32[32]{0:T(128)S(1)}, f32[32]{0:T(128)}, u32[]{:S(2)}) copy-start(f32[32]{0:T(128)} %param.16) | copy-start | bytes 388
  4.6 1.1 %copy-start = (bf16[32,8,2,512]{3,2,1,0:T(2,128)(2,1)S(1)}, bf16[32,8,2,512]{3,2,1,0:T(2,128)(2,1)}, u32[]{:S(2)}) copy-start(bf16[32,8,2,512]{3,2,1,0:T(2,128)(2,1)} %param.14) | copy-start | bytes 1572868
  5.7 1.0 %copy-start.4 = (bf16[2,64,512,1,1]{2,1,0,4,3:T(8,128)(2,1)S(1)}, bf16[2,64,512,1,1]{2,1,0,4,3:T(8,128)(2,1)}, u32[]{:S(2)}) copy-start(bf16[2,64,512,1,1]{2,1,0,4,3:T(8,128)(2,1)} %constant.26) | copy-start | bytes 393220
  48.5 0.7 %copy-start.1 = (f32[32]{0:T(128)S(1)}, f32[32]{0:T(128)}, u32[]{:S(2)}) copy-start(f32[32]{0:T(128)} %param.21) | copy-start | bytes 388

commit v18 on v17

--- a/solution.py
+++ b/solution.py
@@ -209,14 +209,32 @@
     swap_blocks(parts, blocks_ref, out_ref, landed, send_sems, recv_sems)
 
 
-def mode_mix_kernel(parts, modes_ref, xcos_t_ref, xsin_t_ref, swap_t_ref, weight_ref, count_ref, out_ref,
-                    mixed_t, first, blocks, landed, first_send, first_recv, send_sems, recv_sems):
+def mode_mix_kernel(parts, field_ref, table_ref, xcos_t_ref, xsin_t_ref, swap_t_ref, weight_ref, count_ref,
+                    out_ref, mixed_t, modes_out, first, blocks, landed, first_send, first_recv, send_sems,
+                    recv_sems):
     barrier = greet_slab(parts)
+    modes, slab_rows, width = modes_out.shape
+    channels = field_ref.shape[0]
+    planes = width // (2 * channels)
+    length = table_ref.shape[2]
+    lane = lax.broadcasted_iota(jnp.int32, (modes, width), 1)
+    real_lanes = (lane // channels) % 2 == 0
+    contract_last = (((1,), (1,)), ((), ()))
+    for row in range(slab_rows):
+        pieces = []
+        for plane in range(planes):
+            cell = row * planes + plane
+            values = field_ref[:, pl.ds(cell * length, length)]
+            pieces += [values, values]
+        stack = jnp.concatenate(pieces, axis=0)
+        real = lax.dot_general(table_ref[0], stack, contract_last, preferred_element_type=jnp.float32)
+        imag = lax.dot_general(table_ref[1], stack, contract_last, preferred_element_type=jnp.float32)
+        modes_out[:, row, :] = jnp.where(real_lanes, real, imag).astype(modes_out.dtype)
     pl.semaphore_wait(barrier, parts - 1)
-    swap_blocks(parts, modes_ref, None, first, first_send, first_recv)
+    swap_blocks(parts, modes_out, None, first, first_send, first_recv)
     pencil = first[...].astype(jnp.float32)
     pencil = pencil.reshape(pencil.shape[0] * pencil.shape[1], pencil.shape[2])
-    pencil_t = pencil.T.astype(modes_ref.dtype)
+    pencil_t = pencil.T.astype(modes_out.dtype)
     swap_t = swap_t_ref[...]
     swapped_t = jnp.dot(swap_t, pencil_t, preferred_element_type=jnp.float32).astype(pencil_t.dtype)
     spec_t = jnp.dot(pencil_t, xcos_t_ref[...], preferred_element_type=jnp.float32)
@@ -249,14 +267,17 @@
     swap_blocks(parts, blocks, out_ref, landed, send_sems, recv_sems)
 
 
-def mode_mix_exchange(pencil, xcos_t, xsin_t, swap_t, weight, count, parts):
-    shape = pencil.shape
-    width = shape[2]
-    modes = xcos_t.shape[1]
+def mode_mix_exchange(field, table, xcos_t, xsin_t, swap_t, weight, count, parts):
+    channels = field.shape[0]
+    modes, length = table.shape[1], table.shape[2]
+    width = swap_t.shape[0]
+    planes = width // (2 * channels)
+    shape = (modes, field.shape[1] // (planes * length), width)
+    pencil = field
     return pl.pallas_call(
         functools.partial(mode_mix_kernel, parts),
         out_shape=jax.ShapeDtypeStruct(shape, pencil.dtype),
-        in_specs=[pl.BlockSpec(memory_space=pltpu.VMEM)] * 5
+        in_specs=[pl.BlockSpec(memory_space=pltpu.VMEM)] * 6
         + [pl.BlockSpec(memory_space=pltpu.SMEM)],
         out_specs=pl.BlockSpec(memory_space=pltpu.VMEM),
         scratch_shapes=[
@@ -264,13 +285,14 @@
             pltpu.VMEM(shape, pencil.dtype),
             pltpu.VMEM(shape, pencil.dtype),
             pltpu.VMEM(shape, pencil.dtype),
+            pltpu.VMEM(shape, pencil.dtype),
             pltpu.SemaphoreType.DMA((parts,)),
             pltpu.SemaphoreType.DMA((parts,)),
             pltpu.SemaphoreType.DMA((parts,)),
             pltpu.SemaphoreType.DMA((parts,)),
         ],
         compiler_params=pltpu.CompilerParams(collective_id=2, has_side_effects=True),
-    )(pencil, xcos_t, xsin_t, swap_t, weight, count)
+    )(field, table, xcos_t, xsin_t, swap_t, weight, count)
 
 
 def slab_exchange(blocks, parts, exchange_id):
@@ -317,11 +339,6 @@
     field_now = field_rows.reshape(channels, slab_rows, plane_count, length_y)
     y_cos, y_sin = phase_tables(np.arange(modes_y), np.arange(length_y), length_y)
     forward_table = bf16_constant(np.stack([y_cos, -y_sin]))
-    packed = (
-        jnp.einsum("cxzy,rky->kxzrc", field_now, forward_table, preferred_element_type=jnp.float32)
-        .astype(jnp.bfloat16)
-        .reshape(modes_y, slab_rows, packed_width)
-    )
     frequency_x = np.concatenate(
         [np.arange(modes_x // 2), np.arange(length_x - modes_x // 2, length_x)]
     )
@@ -335,7 +352,7 @@
     )
     weight = spectral_weight[0].transpose(1, 2, 3, 0)
     returned = mode_mix_exchange(
-        packed, bf16_constant(full_cos.T), bf16_constant(full_sin.T), bf16_constant(swap.T), weight,
+        field_rows, forward_table, bf16_constant(full_cos.T), bf16_constant(full_sin.T), bf16_constant(swap.T), weight,
         mode_count, slab_count,
     )
     weights_y = np.where(np.arange(modes_y) == 0, 1.0, 2.0).astype(np.float32) / np.float32(

time: 65.9 us -> 63 us (0.956)
  other arithmetic: 4.03 us -> 2.31 us
  local copies, waits for them, and re-layouts: 5.81 us -> 4.92 us
    convert_element_type x2 -> x1, other arithmetic: 2.06 us -> 1.04 us  [local(): field_rows = (2.0 * jnp.tanh(0.5 * driven)).astype(jnp.bfloat16)]
    reshape x1 -> x0, local copies, waits for them, and re-layouts: 0.79 us -> none  [local(): packed = jnp.einsum('cxzy,rky->kxzrc', field_now, forward_table, preferre...]
    unnamed x1, other arithmetic: 0.74 us -> 0.01 us
    unnamed x11 -> x9, local copies, waits for them, and re-layouts: 1.35 us -> 1.34 us
where the time goes in v18:
time: 63 us; the launch traced here: 62.6 us
  Pallas kernels  54 us (86%)
  local copies, waits for them, and re-layouts  4.92 us (8%)
  other arithmetic  2.31 us (4%)
  between operations  1.37 us (2%)
    pallas_call x1, Pallas kernels, mode_mix_exchange(): pl.pallas_call(functools.partial(mode_mix_kernel, parts), out_shape=jax.S...  40 us
    pallas_call x1, Pallas kernels, layer_sum(): pl.pallas_call(functools.partial(layer_sum_kernel, members), out_shape=ja...  14 us
    reshape x1, local copies, waits for them, and re-layouts, local(): return total.reshape(channels // members, slab_rows, plane_count, length_y)  1.56 us
    unnamed x9, local copies, waits for them, and re-layouts  1.34 us
    convert_element_type x1, local copies, waits for them, and re-layouts, local(): base_field.reshape(channels, cells * length_y).astype(jnp.float32)  1.32 us

profile of v18, /device:TPU:1, one launch (start us, length us, event | category | flops | bytes accessed | tf_op | source)
XLA Modules:
  0.0 62.6 jit_solution(12720279673134525218)
XLA Ops:
  0.0 0.0 copy-start
  0.0 1.3 %reshape.23 = f32[32,8192]{1,0:T(8,128)S(1)} reshape(bf16[32,8,2,512]{3,2,1,0:T(2,128)(2,1)} %param.14) | data formatting | bytes 1572864 | tf_op jit(solution)/shard_map/convert_element_type | solution.py:335
  1.3 0.0 copy-done
  2.0 0.0 copy-start.2
  2.0 0.6 %copy-done.2 = f32[16]{0:T(128)S(1)} copy-done((f32[16]{0:T(128)S(1)}, f32[16]{0:T(128)}, u32[]{:S(2)}) %copy-start.2) | copy-done | bytes 88
  2.7 0.0 copy-start.3
  2.7 0.6 fusion
  3.3 0.0 copy-done.3
  3.3 0.6 %broadcast_multiply_fusion = f32[32]{0:T(128)S(1)} fusion(f32[32]{0:T(128)S(1)} %copy-done.3, f32[]{:T(128)} %fusion), kind=kLoop, calls=%fused_computation.4 | loop fusion | flops 32 | bytes 260 | tf_op jit(solution)/shard_map/mul | solution.py:335
  4.0 1.0 %multiply_convert_fusion.field_ref = bf16[32,8192]{1,0:T(8,128)(2,1)} fusion(f32[32,8192]{1,0:T(8,128)S(1)} %reshape.23, f32[8192]{0:T(1024)S(1)} %bitcast.10, f32[32]{0:T(128)S(1)} %broadcast_multiply_fusion), kind=kLoop, calls=%fused_computation | loop fusion | flops 1310720 | bytes 1605760 | tf_op jit(solution)/shard_map/convert_element_type | solution.py:338
  5.7 40.0 %shard_map.136.back_ref = bf16[64,8,128]{2,1,0:T(8,128)(2,1)} custom-call(bf16[32,8192]{1,0:T(8,128)(2,1)} %multiply_convert_fusion.field_ref, bf16[2,64,512]{2,1,0:T(8,128)(2,1)} %constant.16.clone.table_ref, bf16[512,64]{1,0:T(8,128)(2,1)} %constant.17.clone.xcos_t_ref, bf16[512,64]{1,0:T(8,128)(2,1)} %constant.18.clone.xsin_t_ref, ...), custom_call_target="tpu_custom_call" | custom-call | tf_op jit(solution)/shard_map/pallas_call | solution.py:277
  45.7 0.0 copy-start.1
  45.7 0.6 %copy-done.1 = f32[32]{0:T(128)S(1)} copy-done((f32[32]{0:T(128)S(1)}, f32[32]{0:T(128)}, u32[]{:S(2)}) %copy-start.1) | copy-done | bytes 152
  46.3 0.7 %copy.15.bias_ref = f32[32,1]{1,0:T(8,128)} copy(f32[32,1]{0,1:T(1,128)S(1)} %bitcast.11) | data formatting | bytes 256 | tf_op jit(solution)/shard_map/reshape | solution.py:364
  47.0 14.0 %shard_map.137 = bf16[4,8192]{1,0:T(4,128)(2,1)} custom-call(bf16[64,8,128]{2,1,0:T(8,128)(2,1)} %shard_map.136.back_ref, bf16[128,512]{1,0:T(8,128)(2,1)} %constant.20.clone.table_ref, bf16[32,32]{1,0:T(8,128)(2,1)} %weight_ref.1, bf16[32,8192]{1,0:T(8,128)(2,1)} %multiply_convert_fusion.field_ref, f32[32,1]{1,0:T(8,128)} %copy.15.bias_ref), custom_call_target="tpu_custom_call" | custom-call | tf_op jit(solution)/shard_map/pallas_call | solution.py:149
  61.1 1.6 %reshape.22 = bf16[4,8,2,512]{3,2,1,0:T(2,128)(2,1)} reshape(bf16[4,8192]{1,0:T(4,128)(2,1)} %shard_map.137) | data formatting | bytes 131072 | tf_op jit(solution)/shard_map/reshape | solution.py:367
  (2 shorter events, 0.0 us)
Async XLA Ops:
  0.0 1.3 %copy-start = (bf16[8,2,512]{2,1,0:T(2,128)(2,1)S(1)}, bf16[8,2,512]{2,1,0:T(2,128)(2,1)}, u32[]{:S(2)}) copy-start(bf16[8,2,512]{2,1,0:T(2,128)(2,1)} %param.15) | copy-start | bytes 49156
  2.0 0.7 %copy-start.2 = (f32[16]{0:T(128)S(1)}, f32[16]{0:T(128)}, u32[]{:S(2)}) copy-start(f32[16]{0:T(128)} %param.17) | copy-start | bytes 196
  2.7 0.7 %copy-start.3 = (f32[32]{0:T(128)S(1)}, f32[32]{0:T(128)}, u32[]{:S(2)}) copy-start(f32[32]{0:T(128)} %param.16) | copy-start | bytes 388
  45.7 0.7 %copy-start.1 = (f32[32]{0:T(128)S(1)}, f32[32]{0:T(128)}, u32[]{:S(2)}) copy-start(f32[32]{0:T(128)} %param.21) | copy-start | bytes 388

commit v19 on v18

--- a/solution.py
+++ b/solution.py
@@ -61,19 +61,21 @@
     return jnp.einsum("kmoi,kmiz->kmoz", weights, values, preferred_element_type=jnp.float32)
 
 
-def layer_sum_kernel(members, back_ref, table_ref, weight_ref, field_ref, bias_ref, out_ref, value, layer,
-                     near, part, far, near_sems, far_send, far_recv):
+def greet_members(members):
     me = lax.axis_index("member")
     slab = lax.axis_index("slab")
     chips = members // 2
     chip, core = me // 2, me % 2
-    sibling = chip * 2 + 1 - core
     mesh_kind = pl.DeviceIdType.MESH
     barrier = pltpu.get_barrier_semaphore()
-    pl.semaphore_signal(barrier, inc=1, device_id=(sibling, slab), device_id_type=mesh_kind)
+    pl.semaphore_signal(barrier, inc=1, device_id=(chip * 2 + 1 - core, slab), device_id_type=mesh_kind)
     for step in range(1, chips):
         peer = lax.rem(chip + step, chips) * 2 + core
         pl.semaphore_signal(barrier, inc=1, device_id=(peer, slab), device_id_type=mesh_kind)
+    return barrier
+
+
+def layer_values(members, back_ref, table_ref, weight_ref, field_ref, bias_ref, value, layer):
     modes, slab_rows, width = back_ref.shape
     channels = weight_ref.shape[0]
     planes = width // (2 * channels)
@@ -101,8 +103,15 @@
     for block in range(members):
         rows = pl.ds(block * block_rows, block_rows)
         layer[block % 2, block // 2] = value[rows, :].astype(layer.dtype)
-    pl.semaphore_wait(barrier, chips)
-
+
+
+def member_total(members, out_ref, layer, near, part, far, near_sems, far_send, far_recv):
+    me = lax.axis_index("member")
+    slab = lax.axis_index("slab")
+    chips = members // 2
+    chip, core = me // 2, me % 2
+    sibling = chip * 2 + 1 - core
+    mesh_kind = pl.DeviceIdType.MESH
     on_chip = pltpu.make_async_remote_copy(
         src_ref=layer.at[1 - core],
         dst_ref=near,
@@ -140,6 +149,14 @@
         peer = lax.rem(chip + step, chips)
         copy_of(peer, chip, peer).wait_send()
     out_ref[...] = (total / members).astype(out_ref.dtype)
+
+
+def layer_sum_kernel(members, back_ref, table_ref, weight_ref, field_ref, bias_ref, out_ref, value, layer,
+                     near, part, far, near_sems, far_send, far_recv):
+    barrier = greet_members(members)
+    layer_values(members, back_ref, table_ref, weight_ref, field_ref, bias_ref, value, layer)
+    pl.semaphore_wait(barrier, members // 2)
+    member_total(members, out_ref, layer, near, part, far, near_sems, far_send, far_recv)
 
 
 def layer_sum(back, table, weight, field, bias, members):
@@ -209,10 +226,12 @@
     swap_blocks(parts, blocks_ref, out_ref, landed, send_sems, recv_sems)
 
 
-def mode_mix_kernel(parts, field_ref, table_ref, xcos_t_ref, xsin_t_ref, swap_t_ref, weight_ref, count_ref,
-                    out_ref, mixed_t, modes_out, first, blocks, landed, first_send, first_recv, send_sems,
-                    recv_sems):
+def mode_mix_kernel(parts, members, field_ref, table_ref, xcos_t_ref, xsin_t_ref, swap_t_ref, weight_ref,
+                    count_ref, back_table_ref, point_weight_ref, bias_ref, out_ref, mixed_t, modes_out, first,
+                    blocks, landed, first_send, first_recv, send_sems, recv_sems, value, layer, near, part,
+                    far, near_sems, far_send, far_recv):
     barrier = greet_slab(parts)
+    greet_members(members)
     modes, slab_rows, width = modes_out.shape
     channels = field_ref.shape[0]
     planes = width // (2 * channels)
@@ -230,7 +249,7 @@
         real = lax.dot_general(table_ref[0], stack, contract_last, preferred_element_type=jnp.float32)
         imag = lax.dot_general(table_ref[1], stack, contract_last, preferred_element_type=jnp.float32)
         modes_out[:, row, :] = jnp.where(real_lanes, real, imag).astype(modes_out.dtype)
-    pl.semaphore_wait(barrier, parts - 1)
+    pl.semaphore_wait(barrier, parts - 1 + members // 2)
     swap_blocks(parts, modes_out, None, first, first_send, first_recv)
     pencil = first[...].astype(jnp.float32)
     pencil = pencil.reshape(pencil.shape[0] * pencil.shape[1], pencil.shape[2])
@@ -264,35 +283,48 @@
         xsin_t_ref[...], mixed_swapped, contract, preferred_element_type=jnp.float32
     )
     blocks[...] = back.reshape(blocks.shape).astype(blocks.dtype)
-    swap_blocks(parts, blocks, out_ref, landed, send_sems, recv_sems)
-
-
-def mode_mix_exchange(field, table, xcos_t, xsin_t, swap_t, weight, count, parts):
-    channels = field.shape[0]
+    swap_blocks(parts, blocks, None, landed, send_sems, recv_sems)
+    layer_values(members, landed, back_table_ref, point_weight_ref, field_ref, bias_ref, value, layer)
+    member_total(members, out_ref, layer, near, part, far, near_sems, far_send, far_recv)
+
+
+def mode_mix_exchange(field, table, xcos_t, xsin_t, swap_t, weight, count, back_table, point_weight, bias,
+                      parts, members):
+    channels, cells_width = field.shape
     modes, length = table.shape[1], table.shape[2]
     width = swap_t.shape[0]
     planes = width // (2 * channels)
-    shape = (modes, field.shape[1] // (planes * length), width)
-    pencil = field
+    shape = (modes, cells_width // (planes * length), width)
+    block_rows = channels // members
+    chips = members // 2
     return pl.pallas_call(
-        functools.partial(mode_mix_kernel, parts),
-        out_shape=jax.ShapeDtypeStruct(shape, pencil.dtype),
+        functools.partial(mode_mix_kernel, parts, members),
+        out_shape=jax.ShapeDtypeStruct((block_rows, cells_width), jnp.bfloat16),
         in_specs=[pl.BlockSpec(memory_space=pltpu.VMEM)] * 6
-        + [pl.BlockSpec(memory_space=pltpu.SMEM)],
+        + [pl.BlockSpec(memory_space=pltpu.SMEM)]
+        + [pl.BlockSpec(memory_space=pltpu.VMEM)] * 3,
         out_specs=pl.BlockSpec(memory_space=pltpu.VMEM),
         scratch_shapes=[
             pltpu.VMEM((width, modes), jnp.float32),
-            pltpu.VMEM(shape, pencil.dtype),
-            pltpu.VMEM(shape, pencil.dtype),
-            pltpu.VMEM(shape, pencil.dtype),
-            pltpu.VMEM(shape, pencil.dtype),
-            pltpu.SemaphoreType.DMA((parts,)),
-            pltpu.SemaphoreType.DMA((parts,)),
-            pltpu.SemaphoreType.DMA((parts,)),
-            pltpu.SemaphoreType.DMA((parts,)),
+            pltpu.VMEM(shape, field.dtype),
+            pltpu.VMEM(shape, field.dtype),
+            pltpu.VMEM(shape, field.dtype),
+            pltpu.VMEM(shape, field.dtype),
+            pltpu.SemaphoreType.DMA((parts,)),
+            pltpu.SemaphoreType.DMA((parts,)),
+            pltpu.SemaphoreType.DMA((parts,)),
+            pltpu.SemaphoreType.DMA((parts,)),
+            pltpu.VMEM((channels, cells_width), jnp.float32),
+            pltpu.VMEM((2, chips, block_rows, cells_width), jnp.bfloat16),
+            pltpu.VMEM((chips, block_rows, cells_width), jnp.bfloat16),
+            pltpu.VMEM((chips, block_rows, cells_width), jnp.bfloat16),
+            pltpu.VMEM((chips, block_rows, cells_width), jnp.bfloat16),
+            pltpu.SemaphoreType.DMA((2,)),
+            pltpu.SemaphoreType.DMA((chips,)),
+            pltpu.SemaphoreType.DMA((chips,)),
         ],
         compiler_params=pltpu.CompilerParams(collective_id=2, has_side_effects=True),
-    )(field, table, xcos_t, xsin_t, swap_t, weight, count)
+    )(field, table, xcos_t, xsin_t, swap_t, weight, count, back_table, point_weight, bias)
 
 
 def slab_exchange(blocks, parts, exchange_id):
@@ -351,10 +383,6 @@
         -(lane[:, None] == lane[None, :] - channels).astype(np.float32),
     )
     weight = spectral_weight[0].transpose(1, 2, 3, 0)
-    returned = mode_mix_exchange(
-        field_rows, forward_table, bf16_constant(full_cos.T), bf16_constant(full_sin.T), bf16_constant(swap.T), weight,
-        mode_count, slab_count,
-    )
     weights_y = np.where(np.arange(modes_y) == 0, 1.0, 2.0).astype(np.float32) / np.float32(
         length_x * length_y
     )
@@ -363,7 +391,10 @@
     )
     bias = point_bias.reshape(channels, 1)
     members = lax.axis_size("member")
-    total = layer_sum(returned, table, point_weight, field_rows, bias, members)
+    total = mode_mix_exchange(
+        field_rows, forward_table, bf16_constant(full_cos.T), bf16_constant(full_sin.T),
+        bf16_constant(swap.T), weight, mode_count, table, point_weight, bias, slab_count, members,
+    )
     return total.reshape(channels // members, slab_rows, plane_count, length_y)
 
 

time: 63 us -> 59.1 us (0.938)
  Pallas kernels: 54 us -> 50.2 us
    pallas_call x2 -> x1, Pallas kernels: 54 us -> 50.2 us  [mode_mix_exchange(): pl.pallas_call(functools.partial(mode_mix_kernel, parts, members), out_sh...]
where the time goes in v19:
time: 59.1 us; the launch traced here: 58.8 us
  Pallas kernels  50.2 us (85%)
  local copies, waits for them, and re-layouts  4.92 us (8%)
  other arithmetic  2.31 us (4%)
  between operations  1.35 us (2%)
    pallas_call x1, Pallas kernels, mode_mix_exchange(): pl.pallas_call(functools.partial(mode_mix_kernel, parts, members), out_sh...  50.2 us
    reshape x1, local copies, waits for them, and re-layouts, local(): return total.reshape(channels // members, slab_rows, plane_count, length_y)  1.56 us
    unnamed x9, local copies, waits for them, and re-layouts  1.35 us
    convert_element_type x1, local copies, waits for them, and re-layouts, local(): base_field.reshape(channels, cells * length_y).astype(jnp.float32)  1.32 us

profile of v19, /device:TPU:1, one launch (start us, length us, event | category | flops | bytes accessed | tf_op | source)
XLA Modules:
  0.0 58.8 jit_solution(3990870932008834873)
XLA Ops:
  0.0 0.0 copy-start
  0.0 1.3 %reshape.23 = f32[32,8192]{1,0:T(8,128)S(1)} reshape(bf16[32,8,2,512]{3,2,1,0:T(2,128)(2,1)} %param.14) | data formatting | bytes 1572864 | tf_op jit(solution)/shard_map/convert_element_type | solution.py:367
  1.3 0.0 copy-done
  2.0 0.0 copy-start.2
  2.0 0.6 %copy-done.2 = f32[16]{0:T(128)S(1)} copy-done((f32[16]{0:T(128)S(1)}, f32[16]{0:T(128)}, u32[]{:S(2)}) %copy-start.2) | copy-done | bytes 88
  2.7 0.0 copy-start.3
  2.7 0.6 %fusion = f32[]{:T(128)} fusion(f32[16]{0:T(128)S(1)} %copy-done.2, s32[]{:T(128)} %bitcast.8), kind=kLoop, calls=%fused_computation.3 | loop fusion | flops 47 | bytes 72 | tf_op jit(solution)/shard_map/reduce_sum | solution.py:365
  3.3 0.0 copy-done.3
  3.3 0.6 %broadcast_multiply_fusion = f32[32]{0:T(128)S(1)} fusion(f32[32]{0:T(128)S(1)} %copy-done.3, f32[]{:T(128)} %fusion), kind=kLoop, calls=%fused_computation.4 | loop fusion | flops 32 | bytes 260 | tf_op jit(solution)/shard_map/mul | solution.py:367
  4.0 1.0 %multiply_convert_fusion.field_ref = bf16[32,8192]{1,0:T(8,128)(2,1)} fusion(f32[32,8192]{1,0:T(8,128)S(1)} %reshape.23, f32[8192]{0:T(1024)S(1)} %bitcast.10, f32[32]{0:T(128)S(1)} %broadcast_multiply_fusion), kind=kLoop, calls=%fused_computation | loop fusion | flops 1310720 | bytes 1605760 | tf_op jit(solution)/shard_map/convert_element_type | solution.py:370
  5.0 0.0 copy-start.1
  5.0 0.7 %copy-done.1 = f32[32]{0:T(128)S(1)} copy-done((f32[32]{0:T(128)S(1)}, f32[32]{0:T(128)}, u32[]{:S(2)}) %copy-start.1) | copy-done | bytes 152
  5.7 0.7 %copy.15.bias_ref = f32[32,1]{1,0:T(8,128)} copy(f32[32,1]{0,1:T(1,128)S(1)} %bitcast.11) | data formatting | bytes 256 | tf_op jit(solution)/shard_map/reshape | solution.py:392
  7.0 50.2 %shard_map.136 = bf16[4,8192]{1,0:T(4,128)(2,1)} custom-call(bf16[32,8192]{1,0:T(8,128)(2,1)} %multiply_convert_fusion.field_ref, bf16[2,64,512]{2,1,0:T(8,128)(2,1)} %constant.16.clone.table_ref, bf16[512,64]{1,0:T(8,128)(2,1)} %constant.18.clone.xcos_t_ref, bf16[512,64]{1,0:T(8,128)(2,1)} %constant.19.clone.xsin_t_ref, ...), custom_call_target="tpu_custom_call" | custom-call | tf_op jit(solution)/shard_map/pallas_call | solution.py:300
  57.2 1.6 %reshape.22 = bf16[4,8,2,512]{3,2,1,0:T(2,128)(2,1)} reshape(bf16[4,8192]{1,0:T(4,128)(2,1)} %shard_map.136) | data formatting | bytes 131072 | tf_op jit(solution)/shard_map/reshape | solution.py:398
  (2 shorter events, 0.0 us)
Async XLA Ops:
  0.0 1.3 %copy-start = (bf16[8,2,512]{2,1,0:T(2,128)(2,1)S(1)}, bf16[8,2,512]{2,1,0:T(2,128)(2,1)}, u32[]{:S(2)}) copy-start(bf16[8,2,512]{2,1,0:T(2,128)(2,1)} %param.15) | copy-start | bytes 49156
  2.0 0.7 %copy-start.2 = (f32[16]{0:T(128)S(1)}, f32[16]{0:T(128)}, u32[]{:S(2)}) copy-start(f32[16]{0:T(128)} %param.17) | copy-start | bytes 196
  2.7 0.7 %copy-start.3 = (f32[32]{0:T(128)S(1)}, f32[32]{0:T(128)}, u32[]{:S(2)}) copy-start(f32[32]{0:T(128)} %param.16) | copy-start | bytes 388
  5.0 0.7 %copy-start.1 = (f32[32]{0:T(128)S(1)}, f32[32]{0:T(128)}, u32[]{:S(2)}) copy-start(f32[32]{0:T(128)} %param.21) | copy-start | bytes 388

commit v20 on v19

--- a/solution.py
+++ b/solution.py
@@ -75,7 +75,7 @@
     return barrier
 
 
-def layer_values(members, back_ref, table_ref, weight_ref, field_ref, bias_ref, value, layer):
+def layer_values(members, back_ref, table_ref, weight_ref, field_ref, bias, value, layer):
     modes, slab_rows, width = back_ref.shape
     channels = weight_ref.shape[0]
     planes = width // (2 * channels)
@@ -99,7 +99,7 @@
                 preferred_element_type=jnp.float32,
             )
             pointwise = jnp.dot(weight_ref[...], field_ref[:, lanes], preferred_element_type=jnp.float32)
-            value[:, lanes] = jax.nn.gelu(pointwise + bias_ref[...] + spectral, approximate=True)
+            value[:, lanes] = jax.nn.gelu(pointwise + bias + spectral, approximate=True)
     for block in range(members):
         rows = pl.ds(block * block_rows, block_rows)
         layer[block % 2, block // 2] = value[rows, :].astype(layer.dtype)
@@ -154,7 +154,7 @@
 def layer_sum_kernel(members, back_ref, table_ref, weight_ref, field_ref, bias_ref, out_ref, value, layer,
                      near, part, far, near_sems, far_send, far_recv):
     barrier = greet_members(members)
-    layer_values(members, back_ref, table_ref, weight_ref, field_ref, bias_ref, value, layer)
+    layer_values(members, back_ref, table_ref, weight_ref, field_ref, bias_ref[...], value, layer)
     pl.semaphore_wait(barrier, members // 2)
     member_total(members, out_ref, layer, near, part, far, near_sems, far_send, far_recv)
 
@@ -226,12 +226,29 @@
     swap_blocks(parts, blocks_ref, out_ref, landed, send_sems, recv_sems)
 
 
-def mode_mix_kernel(parts, members, field_ref, table_ref, xcos_t_ref, xsin_t_ref, swap_t_ref, weight_ref,
-                    count_ref, back_table_ref, point_weight_ref, bias_ref, out_ref, mixed_t, modes_out, first,
-                    blocks, landed, first_send, first_recv, send_sems, recv_sems, value, layer, near, part,
-                    far, near_sems, far_send, far_recv):
+def smem_column(ref, count):
+    rows = lax.broadcasted_iota(jnp.int32, (count, 1), 0)
+    column = jnp.zeros((count, 1), jnp.float32)
+    for index in range(count):
+        column = jnp.where(rows == index, ref[index], column)
+    return column
+
+
+def mode_mix_kernel(parts, members, base_ref, forcing_ref, table_ref, xcos_t_ref, xsin_t_ref, swap_t_ref,
+                    weight_ref, count_ref, back_table_ref, point_weight_ref, load_ref, amplitude_ref,
+                    level_ref, bias_ref, out_ref, field_ref, mixed_t, modes_out, first, blocks, landed,
+                    first_send, first_recv, send_sems, recv_sems, value, layer, near, part, far, near_sems,
+                    far_send, far_recv):
     barrier = greet_slab(parts)
     greet_members(members)
+    channels, cells_width = field_ref.shape
+    scale = smem_column(load_ref, channels) * amplitude_ref[level_ref[0]]
+    bias = smem_column(bias_ref, channels)
+    chunk = table_ref.shape[2]
+    for start in range(0, cells_width, chunk):
+        lanes = pl.ds(start, chunk)
+        driven = base_ref[:, lanes].astype(jnp.float32) + scale * forcing_ref[:, lanes].astype(jnp.float32)
+        field_ref[:, lanes] = (2.0 * jnp.tanh(0.5 * driven)).astype(field_ref.dtype)
     modes, slab_rows, width = modes_out.shape
     channels = field_ref.shape[0]
     planes = width // (2 * channels)
@@ -284,12 +301,13 @@
     )
     blocks[...] = back.reshape(blocks.shape).astype(blocks.dtype)
     swap_blocks(parts, blocks, None, landed, send_sems, recv_sems)
-    layer_values(members, landed, back_table_ref, point_weight_ref, field_ref, bias_ref, value, layer)
+    layer_values(members, landed, back_table_ref, point_weight_ref, field_ref, bias, value, layer)
     member_total(members, out_ref, layer, near, part, far, near_sems, far_send, far_recv)
 
 
-def mode_mix_exchange(field, table, xcos_t, xsin_t, swap_t, weight, count, back_table, point_weight, bias,
-                      parts, members):
+def mode_mix_exchange(base, forcing, table, xcos_t, xsin_t, swap_t, weight, count, back_table, point_weight,
+                      load, amplitudes, level, bias, parts, members):
+    field = base
     channels, cells_width = field.shape
     modes, length = table.shape[1], table.shape[2]
     width = swap_t.shape[0]
@@ -300,11 +318,13 @@
     return pl.pallas_call(
         functools.partial(mode_mix_kernel, parts, members),
         out_shape=jax.ShapeDtypeStruct((block_rows, cells_width), jnp.bfloat16),
-        in_specs=[pl.BlockSpec(memory_space=pltpu.VMEM)] * 6
+        in_specs=[pl.BlockSpec(memory_space=pltpu.VMEM)] * 7
         + [pl.BlockSpec(memory_space=pltpu.SMEM)]
-        + [pl.BlockSpec(memory_space=pltpu.VMEM)] * 3,
+        + [pl.BlockSpec(memory_space=pltpu.VMEM)] * 2
+        + [pl.BlockSpec(memory_space=pltpu.SMEM)] * 4,
         out_specs=pl.BlockSpec(memory_space=pltpu.VMEM),
         scratch_shapes=[
+            pltpu.VMEM((channels, cells_width), jnp.bfloat16),
             pltpu.VMEM((width, modes), jnp.float32),
             pltpu.VMEM(shape, field.dtype),
             pltpu.VMEM(shape, field.dtype),
@@ -324,7 +344,8 @@
             pltpu.SemaphoreType.DMA((chips,)),
         ],
         compiler_params=pltpu.CompilerParams(collective_id=2, has_side_effects=True),
-    )(field, table, xcos_t, xsin_t, swap_t, weight, count, back_table, point_weight, bias)
+    )(base, forcing, table, xcos_t, xsin_t, swap_t, weight, count, back_table, point_weight, load, amplitudes,
+      level, bias)
 
 
 def slab_exchange(blocks, parts, exchange_id):
@@ -361,14 +382,9 @@
     length_x = slab_rows * slab_count
     packed_width = 2 * channels * plane_count
     slab_index = lax.axis_index("slab")
-    level_ids = jnp.arange(amplitudes.shape[0], dtype=jnp.int32)
-    amplitude = jnp.sum(jnp.where(level_ids == amp_index[0], amplitudes, 0.0))
     cells = slab_rows * plane_count
-    driven = base_field.reshape(channels, cells * length_y).astype(jnp.float32) + amplitude * load[
-        :, None
-    ] * forcing.reshape(1, cells * length_y).astype(jnp.float32)
-    field_rows = (2.0 * jnp.tanh(0.5 * driven)).astype(jnp.bfloat16)
-    field_now = field_rows.reshape(channels, slab_rows, plane_count, length_y)
+    base_rows = base_field.reshape(channels, cells * length_y)
+    forcing_rows = forcing.reshape(1, cells * length_y)
     y_cos, y_sin = phase_tables(np.arange(modes_y), np.arange(length_y), length_y)
     forward_table = bf16_constant(np.stack([y_cos, -y_sin]))
     frequency_x = np.concatenate(
@@ -389,11 +405,11 @@
     table = bf16_constant(
         np.concatenate([weights_y[:, None] * y_cos, -(weights_y[:, None] * y_sin)], axis=0)
     )
-    bias = point_bias.reshape(channels, 1)
     members = lax.axis_size("member")
     total = mode_mix_exchange(
-        field_rows, forward_table, bf16_constant(full_cos.T), bf16_constant(full_sin.T),
-        bf16_constant(swap.T), weight, mode_count, table, point_weight, bias, slab_count, members,
+        base_rows, forcing_rows, forward_table, bf16_constant(full_cos.T), bf16_constant(full_sin.T),
+        bf16_constant(swap.T), weight, mode_count, table, point_weight, load, amplitudes, amp_index,
+        point_bias, slab_count, members,
     )
     return total.reshape(channels // members, slab_rows, plane_count, length_y)
 

time: 59.1 us -> 57.1 us (0.966)
  other arithmetic: 2.31 us -> 0 us
    reshape x1 -> x2, local copies, waits for them, and re-layouts: 0.69 us -> 3.56 us  [the longest x1 2.21 us: local(): base_rows = base_field.reshape(channels, cells * length_y)]
    unnamed x9 -> x0, local copies, waits for them, and re-layouts: 1.35 us -> none
    convert_element_type x1 -> x0, local copies, waits for them, and re-layouts: 1.32 us -> none  [local(): base_field.reshape(channels, cells * length_y).astype(jnp.float32)]
    convert_element_type x1 -> x0, other arithmetic: 1.04 us -> none  [local(): field_rows = (2.0 * jnp.tanh(0.5 * driven)).astype(jnp.bfloat16)]
    mul x1 -> x0, other arithmetic: 0.64 us -> none  [local(): amplitude * load[:, None]]
    reduce_sum x1 -> x0, other arithmetic: 0.63 us -> none  [local(): amplitude = jnp.sum(jnp.where(level_ids == amp_index[0], amplitudes, 0.0))]
where the time goes in v20:
time: 57.1 us; the launch traced here: 56.8 us
  Pallas kernels  50.4 us (88%)
  local copies, waits for them, and re-layouts  5.12 us (9%)
  between operations  1.31 us (2%)
    pallas_call x1, Pallas kernels, mode_mix_exchange(): pl.pallas_call(functools.partial(mode_mix_kernel, parts, members), out_sh...  50.4 us
    reshape x1, local copies, waits for them, and re-layouts, local(): base_rows = base_field.reshape(channels, cells * length_y)  2.21 us
    reshape x1, local copies, waits for them, and re-layouts, local(): return total.reshape(channels // members, slab_rows, plane_count, length_y)  1.56 us
    reshape x1, local copies, waits for them, and re-layouts, local(): forcing_rows = forcing.reshape(1, cells * length_y)  1.35 us

profile of v20, /device:TPU:1, one launch (start us, length us, event | category | flops | bytes accessed | tf_op | source)
XLA Modules:
  0.0 56.8 jit_solution(12422750741695259118)
XLA Ops:
  1.3 1.3 %reshape.10.forcing_ref = bf16[1,8192]{1,0:T(2,128)(2,1)} reshape(bf16[8,2,512]{2,1,0:T(2,128)(2,1)} %param.15) | data formatting | bytes 32768 | tf_op jit(solution)/shard_map/reshape | solution.py:387
  2.6 2.2 %reshape.9.base_ref = bf16[32,8192]{1,0:T(8,128)(2,1)} reshape(bf16[32,8,2,512]{3,2,1,0:T(2,128)(2,1)} %param.14) | data formatting | bytes 1048576 | tf_op jit(solution)/shard_map/reshape | solution.py:386
  4.9 50.4 %shard_map.136 = bf16[4,8192]{1,0:T(4,128)(2,1)} custom-call(bf16[32,8192]{1,0:T(8,128)(2,1)} %reshape.9.base_ref, bf16[1,8192]{1,0:T(2,128)(2,1)} %reshape.10.forcing_ref, bf16[2,64,512]{2,1,0:T(8,128)(2,1)} %constant.10.clone.table_ref, bf16[512,64]{1,0:T(8,128)(2,1)} %constant.12.clone.xcos_t_ref, bf16[512,64]{1,0:T(8,128)(2,1)} %constant.13.clone.xsin_t_ref, ...), custom_call_target="tpu_custom_call" | custom-call | tf_op jit(solution)/shard_map/pallas_call | solution.py:318
  55.2 1.6 %reshape.11 = bf16[4,8,2,512]{3,2,1,0:T(2,128)(2,1)} reshape(bf16[4,8192]{1,0:T(4,128)(2,1)} %shard_map.136) | data formatting | bytes 131072 | tf_op jit(solution)/shard_map/reshape | solution.py:414

commit v21 on v20

--- a/solution.py
+++ b/solution.py
@@ -245,10 +245,14 @@
     scale = smem_column(load_ref, channels) * amplitude_ref[level_ref[0]]
     bias = smem_column(bias_ref, channels)
     chunk = table_ref.shape[2]
-    for start in range(0, cells_width, chunk):
-        lanes = pl.ds(start, chunk)
-        driven = base_ref[:, lanes].astype(jnp.float32) + scale * forcing_ref[:, lanes].astype(jnp.float32)
-        field_ref[:, lanes] = (2.0 * jnp.tanh(0.5 * driven)).astype(field_ref.dtype)
+    rows_here, planes_here = base_ref.shape[1], base_ref.shape[2]
+    for row in range(rows_here):
+        for plane in range(planes_here):
+            lanes = pl.ds((row * planes_here + plane) * chunk, chunk)
+            driven = base_ref[:, row, plane, :].astype(jnp.float32) + scale * forcing_ref[
+                pl.ds(row, 1), plane, :
+            ].astype(jnp.float32)
+            field_ref[:, lanes] = (2.0 * jnp.tanh(0.5 * driven)).astype(field_ref.dtype)
     modes, slab_rows, width = modes_out.shape
     channels = field_ref.shape[0]
     planes = width // (2 * channels)
@@ -308,7 +312,8 @@
 def mode_mix_exchange(base, forcing, table, xcos_t, xsin_t, swap_t, weight, count, back_table, point_weight,
                       load, amplitudes, level, bias, parts, members):
     field = base
-    channels, cells_width = field.shape
+    channels = field.shape[0]
+    cells_width = field.shape[1] * field.shape[2] * field.shape[3]
     modes, length = table.shape[1], table.shape[2]
     width = swap_t.shape[0]
     planes = width // (2 * channels)
@@ -383,8 +388,6 @@
     packed_width = 2 * channels * plane_count
     slab_index = lax.axis_index("slab")
     cells = slab_rows * plane_count
-    base_rows = base_field.reshape(channels, cells * length_y)
-    forcing_rows = forcing.reshape(1, cells * length_y)
     y_cos, y_sin = phase_tables(np.arange(modes_y), np.arange(length_y), length_y)
     forward_table = bf16_constant(np.stack([y_cos, -y_sin]))
     frequency_x = np.concatenate(
@@ -407,7 +410,7 @@
     )
     members = lax.axis_size("member")
     total = mode_mix_exchange(
-        base_rows, forcing_rows, forward_table, bf16_constant(full_cos.T), bf16_constant(full_sin.T),
+        base_field, forcing, forward_table, bf16_constant(full_cos.T), bf16_constant(full_sin.T),
         bf16_constant(swap.T), weight, mode_count, table, point_weight, load, amplitudes, amp_index,
         point_bias, slab_count, members,
     )

time: 57.1 us -> 53.5 us (0.937)
  local copies, waits for them, and re-layouts: 5.12 us -> 1.56 us
    reshape x2 -> x0, local copies, waits for them, and re-layouts: 3.56 us -> none  [the longest x1 2.21 us: local(): base_rows = base_field.reshape(channels, cells * length_y)]
where the time goes in v21:
time: 53.5 us; the launch traced here: 53.3 us
  Pallas kernels  50.4 us (94%)
  local copies, waits for them, and re-layouts  1.56 us (3%)
  between operations  1.3 us (2%)
    pallas_call x1, Pallas kernels, mode_mix_exchange(): pl.pallas_call(functools.partial(mode_mix_kernel, parts, members), out_sh...  50.4 us
    reshape x1, local copies, waits for them, and re-layouts, local(): return total.reshape(channels // members, slab_rows, plane_count, length_y)  1.56 us

profile of v21, /device:TPU:1, one launch (start us, length us, event | category | flops | bytes accessed | tf_op | source)
XLA Modules:
  0.0 53.3 jit_solution(8779115037130175875)
XLA Ops:
  1.3 50.4 %shard_map.136 = bf16[4,8192]{1,0:T(4,128)(2,1)} custom-call(bf16[32,8,2,512]{3,2,1,0:T(2,128)(2,1)} %base_ref.1, bf16[8,2,512]{2,1,0:T(2,128)(2,1)} %forcing_ref.1, bf16[2,64,512]{2,1,0:T(8,128)(2,1)} %constant.10.clone.table_ref, bf16[512,64]{1,0:T(8,128)(2,1)} %constant.12.clone.xcos_t_ref, bf16[512,64]{1,0:T(8,128)(2,1)} %constant.13.clone.xsin_t_ref, ...), custom_call_target="tpu_custom_call" | custom-call | tf_op jit(solution)/shard_map/pallas_call | solution.py:323
  51.7 1.6 %reshape.3 = bf16[4,8,2,512]{3,2,1,0:T(2,128)(2,1)} reshape(bf16[4,8192]{1,0:T(4,128)(2,1)} %shard_map.136) | data formatting | bytes 131072 | tf_op jit(solution)/shard_map/reshape | solution.py:417

commit v22 on v21

--- a/solution.py
+++ b/solution.py
@@ -148,7 +148,15 @@
     for step in range(1, chips):
         peer = lax.rem(chip + step, chips)
         copy_of(peer, chip, peer).wait_send()
-    out_ref[...] = (total / members).astype(out_ref.dtype)
+    mean = (total / members).astype(out_ref.dtype)
+    if len(out_ref.shape) == 2:
+        out_ref[...] = mean
+    else:
+        rows_out, planes_out, length_out = out_ref.shape[1], out_ref.shape[2], out_ref.shape[3]
+        for row in range(rows_out):
+            for plane in range(planes_out):
+                cell = row * planes_out + plane
+                out_ref[:, row, plane, :] = mean[:, cell * length_out:(cell + 1) * length_out]
 
 
 def layer_sum_kernel(members, back_ref, table_ref, weight_ref, field_ref, bias_ref, out_ref, value, layer,
@@ -322,7 +330,7 @@
     chips = members // 2
     return pl.pallas_call(
         functools.partial(mode_mix_kernel, parts, members),
-        out_shape=jax.ShapeDtypeStruct((block_rows, cells_width), jnp.bfloat16),
+        out_shape=jax.ShapeDtypeStruct((block_rows,) + base.shape[1:], jnp.bfloat16),
         in_specs=[pl.BlockSpec(memory_space=pltpu.VMEM)] * 7
         + [pl.BlockSpec(memory_space=pltpu.SMEM)]
         + [pl.BlockSpec(memory_space=pltpu.VMEM)] * 2
@@ -414,7 +422,7 @@
         bf16_constant(swap.T), weight, mode_count, table, point_weight, load, amplitudes, amp_index,
         point_bias, slab_count, members,
     )
-    return total.reshape(channels // members, slab_rows, plane_count, length_y)
+    return total
 
 
 def solution(mesh):

time: 53.5 us -> 53.5 us (level)
    reshape x1 -> x0, local copies, waits for them, and re-layouts: 1.56 us -> none  [local(): return total.reshape(channels // members, slab_rows, plane_count, length_y)]
    unnamed x0 -> x1, local copies, waits for them, and re-layouts: none -> 1.52 us
where the time goes in v22:
time: 53.5 us; the launch traced here: 53.3 us
  Pallas kernels  50.4 us (94%)
  local copies, waits for them, and re-layouts  1.52 us (3%)
  between operations  1.3 us (2%)
    pallas_call x1, Pallas kernels, mode_mix_exchange(): pl.pallas_call(functools.partial(mode_mix_kernel, parts, members), out_sh...  50.4 us
    unnamed x1, local copies, waits for them, and re-layouts  1.52 us

profile of v22, /device:TPU:1, one launch (start us, length us, event | category | flops | bytes accessed | tf_op | source)
XLA Modules:
  0.0 53.3 jit_solution(13421198199248255974)
XLA Ops:
  1.3 50.4 %shard_map.136 = bf16[4,8,2,512]{3,2,1,0:T(2,128)(2,1)} custom-call(bf16[32,8,2,512]{3,2,1,0:T(2,128)(2,1)} %base_ref.1, bf16[8,2,512]{2,1,0:T(2,128)(2,1)} %forcing_ref.1, bf16[2,64,512]{2,1,0:T(8,128)(2,1)} %constant.10.clone.table_ref, bf16[512,64]{1,0:T(8,128)(2,1)} %constant.12.clone.xcos_t_ref, bf16[512,64]{1,0:T(8,128)(2,1)} %constant.13.clone.xsin_t_ref, ...), custom_call_target="tpu_custom_call" | custom-call | tf_op jit(solution)/shard_map/pallas_call | solution.py:331
  51.8 1.5 %copy.18 = bf16[4,8,2,512]{3,2,1,0:T(2,128)(2,1)} copy(bf16[4,8,2,512]{3,2,1,0:T(2,128)(2,1)} %shard_map.136) | data formatting | bytes 131072

commit v23 on v22

--- a/solution.py
+++ b/solution.py
@@ -307,12 +307,48 @@
     mixed = (mixed_t[...] * kept).astype(pencil_t.dtype)
     mixed_swapped = jnp.dot(swap_t, mixed, preferred_element_type=jnp.float32).astype(pencil_t.dtype)
     contract = (((1,), (1,)), ((), ()))
-    back = lax.dot_general(xcos_t_ref[...], mixed, contract, preferred_element_type=jnp.float32)
-    back = back - lax.dot_general(
-        xsin_t_ref[...], mixed_swapped, contract, preferred_element_type=jnp.float32
-    )
-    blocks[...] = back.reshape(blocks.shape).astype(blocks.dtype)
-    swap_blocks(parts, blocks, None, landed, send_sems, recv_sems)
+    me = lax.axis_index("slab")
+    member = lax.axis_index("member")
+    group = 8 if parts % 8 == 0 else 1
+    groups = parts // group
+    rows_per = blocks.shape[1]
+    span = group * rows_per
+
+    def copy_of(source, target, peer):
+        return pltpu.make_async_remote_copy(
+            src_ref=blocks.at[source],
+            dst_ref=landed.at[target],
+            send_sem=send_sems.at[source],
+            recv_sem=recv_sems.at[target],
+            device_id=(member, peer),
+            device_id_type=pl.DeviceIdType.MESH,
+        )
+
+    for step in range(groups):
+        chosen = lax.rem(me // group + step, groups)
+        start = pl.multiple_of(chosen * span, span)
+        back = lax.dot_general(
+            xcos_t_ref[pl.ds(start, span), :], mixed, contract, preferred_element_type=jnp.float32
+        )
+        back = back - lax.dot_general(
+            xsin_t_ref[pl.ds(start, span), :], mixed_swapped, contract,
+            preferred_element_type=jnp.float32,
+        )
+        blocks[pl.ds(chosen * group, group)] = back.reshape(group, rows_per, -1).astype(blocks.dtype)
+        for offset in range(group):
+            peer = chosen * group + lax.rem(me + offset, group)
+
+            @pl.when(peer != me)
+            def _():
+                copy_of(peer, me, peer).start()
+
+    landed[me] = blocks[me]
+    for step in range(1, parts):
+        source = lax.rem(me + parts - step, parts)
+        copy_of(source, source, source).wait_recv()
+    for step in range(1, parts):
+        peer = lax.rem(me + step, parts)
+        copy_of(peer, me, peer).wait_send()
     layer_values(members, landed, back_table_ref, point_weight_ref, field_ref, bias, value, layer)
     member_total(members, out_ref, layer, near, part, far, near_sems, far_send, far_recv)
 

time: 53.5 us -> 53.9 us (level)
  no operation moved by 1% of the time
where the time goes in v23:
time: 53.9 us; the launch traced here: 53.7 us
  Pallas kernels  50.8 us (94%)
  local copies, waits for them, and re-layouts  1.52 us (3%)
  between operations  1.3 us (2%)
    pallas_call x1, Pallas kernels, mode_mix_exchange(): pl.pallas_call(functools.partial(mode_mix_kernel, parts, members), out_sh...  50.8 us
    unnamed x1, local copies, waits for them, and re-layouts  1.52 us

profile of v23, /device:TPU:1, one launch (start us, length us, event | category | flops | bytes accessed | tf_op | source)
XLA Modules:
  0.0 53.7 jit_solution(4863081383840721556)
XLA Ops:
  1.3 50.8 %shard_map.136 = bf16[4,8,2,512]{3,2,1,0:T(2,128)(2,1)} custom-call(bf16[32,8,2,512]{3,2,1,0:T(2,128)(2,1)} %base_ref.1, bf16[8,2,512]{2,1,0:T(2,128)(2,1)} %forcing_ref.1, bf16[2,64,512]{2,1,0:T(8,128)(2,1)} %constant.10.clone.table_ref, bf16[512,64]{1,0:T(8,128)(2,1)} %constant.12.clone.xcos_t_ref, bf16[512,64]{1,0:T(8,128)(2,1)} %constant.13.clone.xsin_t_ref, ...), custom_call_target="tpu_custom_call" | custom-call | tf_op jit(solution)/shard_map/pallas_call | solution.py:367
  52.1 1.5 %copy.18 = bf16[4,8,2,512]{3,2,1,0:T(2,128)(2,1)} copy(bf16[4,8,2,512]{3,2,1,0:T(2,128)(2,1)} %shard_map.136) | data formatting | bytes 131072

commit v24 on v22

--- a/solution.py
+++ b/solution.py
@@ -290,13 +290,16 @@
     spec_t = spec_t.astype(pencil_t.dtype).astype(jnp.float32)
     outputs = weight_ref.shape[1]
     planes = spec_t.shape[0] // (2 * outputs)
-    for plane in range(planes):
-        base = plane * 2 * outputs
-        real = spec_t[base:base + outputs, :]
-        imag = spec_t[base + outputs:base + 2 * outputs, :]
-        for out in range(outputs):
-            weight_real = weight_ref[0, out].astype(jnp.float32)
-            weight_imag = weight_ref[1, out].astype(jnp.float32)
+    halves = [
+        (spec_t[plane * 2 * outputs:plane * 2 * outputs + outputs, :],
+         spec_t[plane * 2 * outputs + outputs:(plane + 1) * 2 * outputs, :])
+        for plane in range(planes)
+    ]
+    for out in range(outputs):
+        weight_real = weight_ref[0, out].astype(jnp.float32)
+        weight_imag = weight_ref[1, out].astype(jnp.float32)
+        for plane, (real, imag) in enumerate(halves):
+            base = plane * 2 * outputs
             mixed_t[pl.ds(base + out, 1), :] = jnp.sum(
                 weight_real * real - weight_imag * imag, axis=0, keepdims=True
             )

time: 53.5 us -> 53.2 us (level)
  no operation moved by 1% of the time
where the time goes in v24:
time: 53.2 us; the launch traced here: 53 us
  Pallas kernels  50.2 us (94%)
  local copies, waits for them, and re-layouts  1.52 us (3%)
  between operations  1.3 us (2%)
    pallas_call x1, Pallas kernels, mode_mix_exchange(): pl.pallas_call(functools.partial(mode_mix_kernel, parts, members), out_sh...  50.2 us
    unnamed x1, local copies, waits for them, and re-layouts  1.52 us

profile of v24, /device:TPU:1, one launch (start us, length us, event | category | flops | bytes accessed | tf_op | source)
XLA Modules:
  0.0 53.0 jit_solution(9574903303531453788)
XLA Ops:
  1.3 50.2 %shard_map.136 = bf16[4,8,2,512]{3,2,1,0:T(2,128)(2,1)} custom-call(bf16[32,8,2,512]{3,2,1,0:T(2,128)(2,1)} %base_ref.1, bf16[8,2,512]{2,1,0:T(2,128)(2,1)} %forcing_ref.1, bf16[2,64,512]{2,1,0:T(8,128)(2,1)} %constant.10.clone.table_ref, bf16[512,64]{1,0:T(8,128)(2,1)} %constant.12.clone.xcos_t_ref, bf16[512,64]{1,0:T(8,128)(2,1)} %constant.13.clone.xsin_t_ref, ...), custom_call_target="tpu_custom_call" | custom-call | tf_op jit(solution)/shard_map/pallas_call | solution.py:334
  51.5 1.5 %copy.18 = bf16[4,8,2,512]{3,2,1,0:T(2,128)(2,1)} copy(bf16[4,8,2,512]{3,2,1,0:T(2,128)(2,1)} %shard_map.136) | data formatting | bytes 131072

commit v25 on v24

--- a/solution.py
+++ b/solution.py
@@ -232,6 +232,13 @@
     barrier = greet_slab(parts)
     pl.semaphore_wait(barrier, parts - 1)
     swap_blocks(parts, blocks_ref, out_ref, landed, send_sems, recv_sems)
+
+
+def swap_parts(rows, channels):
+    pieces = []
+    for start in range(0, rows.shape[0], 2 * channels):
+        pieces += [rows[start + channels:start + 2 * channels], -rows[start:start + channels]]
+    return jnp.concatenate(pieces, axis=0)
 
 
 def smem_column(ref, count):
@@ -284,7 +291,7 @@
     pencil = pencil.reshape(pencil.shape[0] * pencil.shape[1], pencil.shape[2])
     pencil_t = pencil.T.astype(modes_out.dtype)
     swap_t = swap_t_ref[...]
-    swapped_t = jnp.dot(swap_t, pencil_t, preferred_element_type=jnp.float32).astype(pencil_t.dtype)
+    swapped_t = swap_parts(pencil_t.astype(jnp.float32), channels).astype(pencil_t.dtype)
     spec_t = jnp.dot(pencil_t, xcos_t_ref[...], preferred_element_type=jnp.float32)
     spec_t = spec_t + jnp.dot(swapped_t, xsin_t_ref[...], preferred_element_type=jnp.float32)
     spec_t = spec_t.astype(pencil_t.dtype).astype(jnp.float32)
@@ -308,7 +315,7 @@
             )
     kept = (lax.axis_index("slab") < count_ref[0]).astype(jnp.float32)
     mixed = (mixed_t[...] * kept).astype(pencil_t.dtype)
-    mixed_swapped = jnp.dot(swap_t, mixed, preferred_element_type=jnp.float32).astype(pencil_t.dtype)
+    mixed_swapped = swap_parts(mixed.astype(jnp.float32), channels).astype(pencil_t.dtype)
     contract = (((1,), (1,)), ((), ()))
     back = lax.dot_general(xcos_t_ref[...], mixed, contract, preferred_element_type=jnp.float32)
     back = back - lax.dot_general(

time: 53.2 us -> 53 us (level)
  no operation moved by 1% of the time
where the time goes in v25:
time: 53 us; the launch traced here: 52.8 us
  Pallas kernels  50 us (94%)
  local copies, waits for them, and re-layouts  1.52 us (3%)
  between operations  1.3 us (2%)
    pallas_call x1, Pallas kernels, mode_mix_exchange(): pl.pallas_call(functools.partial(mode_mix_kernel, parts, members), out_sh...  50 us
    unnamed x1, local copies, waits for them, and re-layouts  1.52 us

profile of v25, /device:TPU:1, one launch (start us, length us, event | category | flops | bytes accessed | tf_op | source)
XLA Modules:
  0.0 52.8 jit_solution(11662847688534866980)
XLA Ops:
  1.3 50.0 %shard_map.136 = bf16[4,8,2,512]{3,2,1,0:T(2,128)(2,1)} custom-call(bf16[32,8,2,512]{3,2,1,0:T(2,128)(2,1)} %base_ref.1, bf16[8,2,512]{2,1,0:T(2,128)(2,1)} %forcing_ref.1, bf16[2,64,512]{2,1,0:T(8,128)(2,1)} %constant.10.clone.table_ref, bf16[512,64]{1,0:T(8,128)(2,1)} %constant.12.clone.xcos_t_ref, bf16[512,64]{1,0:T(8,128)(2,1)} %constant.13.clone.xsin_t_ref, ...), custom_call_target="tpu_custom_call" | custom-call | tf_op jit(solution)/shard_map/pallas_call | solution.py:341
  51.3 1.5 %copy.18 = bf16[4,8,2,512]{3,2,1,0:T(2,128)(2,1)} copy(bf16[4,8,2,512]{3,2,1,0:T(2,128)(2,1)} %shard_map.136) | data formatting | bytes 131072
